TPU v7x, 512 devices: a whole 4x4x16 slice. The times are simulated.
512 devices in a mesh: ctx: 256 (over x, y_hi, z, core), head: 2 (over y_lo).
Axes of the slice: x: 4, y: 4 (y_hi: 2, y_lo: 2; y = y_hi * 2 + y_lo), z: 16, core: 2. Of those that a mesh axis runs over, the one named last changes fastest.
Arguments:
- queries: float32 [32768, 16, 128], P('ctx', 'head'), may hold values from -52 to 52
- key_states: float32 [32768, 8, 128], P('ctx', 'head'), may hold values from -6 to 6
- value_states: float32 [32768, 8, 128], P('ctx', 'head'), may hold values from -6 to 6
- out_grad: float32 [32768, 16, 128], P('ctx', 'head'), may hold values from -18 to 18
- step_begins: int32 [32768], P('ctx'), may hold values from 0 to 1, as said below
Outputs:
- query_grad: float32 [32768, 16, 128], P('ctx', 'head')
- key_grad: float32 [32768, 8, 128], P('ctx', 'head')
- value_grad: float32 [32768, 8, 128], P('ctx', 'head')
- grad_square: float32 [], replicated
Inputs may be any that keep to these rules, and one draw needn't show every extreme that they name: `step_begins`: steps begin at positions 32 and 64, and at offsets 128 // 4 and 64 of the blocks of 128 positions numbered 32768 // 256 - 1 and 128; none begins at positions 128 to 255, nor at other positions of blocks 32768 // 256 and 129.
All inputs are finite; a program needn't handle non-finite values.
Results may differ from a plain program's by a relative error of at most 0.00045.
Values sent between devices are 32-bit elements; how exact they have to be, the bound alone decides.
No kernel may reach another device: no remote copies, remote signals or barrier semaphores. Data moves between devices by JAX's collectives and lax.ppermute only.
A program may use at most 64 MiB of HBM per device.

v0:
```python
import jax
import jax.numpy as jnp
from jax import lax
from jax.sharding import PartitionSpec as P

WINDOW = 1024


floor_mark = -(2**30)
masked_score = -1e30


def entering(value, axis, join, neutral):
    count, mine = (lax.axis_size(axis), lax.axis_index(axis))
    pieces = jax.tree.map(lambda part: lax.all_gather(part, axis), value)
    total = jax.tree.map(
        lambda part, zero: jnp.full_like(part, 0) + jnp.asarray(zero, part.dtype), value, neutral
    )

    def lap(position, total):
        longer = join(total, jax.tree.map(lambda part: part[position], pieces))
        return jax.tree.map(lambda new, old: jnp.where(position < mine, new, old), longer, total)

    return lax.fori_loop(0, count - 1, lap, total)


def passed_along(value, axis, steps):
    count = lax.axis_size(axis)
    first, last = (max(0, -steps), min(count, count - steps))
    return lax.ppermute(value, axis, [(source, source + steps) for source in range(first, last)])


def combine_starts(first_part, second_part):
    top_start = jnp.maximum(second_part[0], first_part[0])
    second = jnp.maximum(
        second_part[1], jnp.where(second_part[0] > floor_mark, first_part[0], first_part[1])
    )
    return (top_start, second)


def shards(queries, key_states, value_states, out_grad, step_begins):
    row_count, head_count, head_width = queries.shape
    group_count = key_states.shape[1]
    reach_blocks = WINDOW // row_count
    offset = lax.axis_index("ctx") * row_count
    places = offset + jnp.arange(row_count, dtype=jnp.int32)
    begins_here = (step_begins > 0) | (places == 0)
    starts = jnp.where(begins_here, places, floor_mark)
    top_start = jnp.max(starts)
    second = jnp.max(jnp.where(starts < top_start, starts, floor_mark))
    identity = (jnp.int32(floor_mark), jnp.int32(floor_mark))
    carried = entering((top_start, second), "ctx", combine_starts, identity)
    running = jnp.maximum(carried[0], lax.cummax(starts, axis=0))
    before = jnp.concatenate([carried[0][None], running[:-1]])
    step_marks = jnp.where(begins_here, before, floor_mark)
    earliest = jnp.maximum(carried[1], lax.cummax(step_marks, axis=0))
    own_pair = jnp.stack([key_states, value_states])
    fetched = [own_pair]
    latest = own_pair
    for distance in range(1, reach_blocks + 1):
        latest = passed_along(own_pair, "ctx", distance)
        fetched.append(latest)
    ordered = jnp.concatenate(fetched[::-1], axis=1)
    key_all = ordered[0]
    value_all = ordered[1]
    key_places = (
        offset
        - reach_blocks * row_count
        + jnp.arange((reach_blocks + 1) * row_count, dtype=jnp.int32)
    )
    score_scale = head_width ** (-0.5)
    grouped = queries.reshape(row_count, group_count, head_count // group_count, head_width)
    scores = (
        jnp.einsum("qkgd,skd->kgqs", grouped, key_all, precision=lax.Precision.HIGHEST)
        * score_scale
    )
    visible = (key_places[None, :] <= places[:, None]) & (
        key_places[None, :] > places[:, None] - WINDOW
    )
    visible = visible & (key_places[None, :] >= earliest[:, None]) & (key_places[None, :] >= 0)
    scores = jnp.where(visible, scores, masked_score)
    row_peak = jnp.max(scores, axis=-1, keepdims=True)
    weights = jnp.exp(scores - row_peak)
    weights = weights / jnp.sum(weights, axis=-1, keepdims=True)
    mixed_out = jnp.einsum("kgqs,skd->qkgd", weights, value_all, precision=lax.Precision.HIGHEST)
    grad_grouped = out_grad.reshape(grouped.shape)
    weight_grad = jnp.einsum(
        "qkgd,skd->kgqs", grad_grouped, value_all, precision=lax.Precision.HIGHEST
    )
    row_delta = jnp.transpose(jnp.sum(grad_grouped * mixed_out, axis=-1), (1, 2, 0))[..., None]
    score_grad = weights * (weight_grad - row_delta)
    query_grad = (
        jnp.einsum("kgqs,skd->qkgd", score_grad, key_all, precision=lax.Precision.HIGHEST)
        * score_scale
    )
    query_grad = query_grad.reshape(row_count, head_count, head_width)
    key_part = (
        jnp.einsum("kgqs,qkgd->skd", score_grad, grouped, precision=lax.Precision.HIGHEST)
        * score_scale
    )
    value_part = jnp.einsum(
        "kgqs,qkgd->skd", weights, grad_grouped, precision=lax.Precision.HIGHEST
    )
    grad_parts = jnp.stack([key_part, value_part])

    def grad_piece(distance):
        first_row = (reach_blocks - distance) * row_count
        return grad_parts[:, first_row : first_row + row_count]

    returned = grad_piece(0)
    for distance in range(1, reach_blocks + 1):
        returned = returned + passed_along(grad_piece(distance), "ctx", -distance)
    key_grad = returned[0]
    value_grad = returned[1]
    local_sum = (
        jnp.sum(query_grad * query_grad)
        + jnp.sum(key_grad * key_grad)
        + jnp.sum(value_grad * value_grad)
    )
    entry_count = (
        row_count
        * lax.axis_size("ctx")
        * (head_count + 2 * group_count)
        * lax.axis_size("head")
        * head_width
    )
    grad_square = lax.psum(local_sum, ("ctx", "head")) / entry_count
    return (query_grad, key_grad, value_grad, grad_square)


def solution(mesh):
    placed = (
        P("ctx", "head", None),
        P("ctx", "head", None),
        P("ctx", "head", None),
        P("ctx", "head", None),
        P("ctx"),
    )
    return jax.shard_map(
        shards,
        mesh=mesh,
        in_specs=placed,
        out_specs=(P("ctx", "head", None), P("ctx", "head", None), P("ctx", "head", None), P()),
        check_vma=False,
    )
```

profile of v0, /device:TPU:1, one launch (start us, length us, event | category | flops | bytes accessed | tf_op | source)
XLA Modules:
  0.0 1980.5 jit_solution(13816603555013800970)
XLA Ops:
  1.8 10.4 collective-permute-start
  12.3 9.7 collective-permute-start.1
  21.9 2.8 collective-permute-start.2
  24.7 2.8 collective-permute-start.3
  27.6 3.1 collective-permute-start.4
  38.1 766.1 %all-reduce.2 = (s32[256]{0:T(256)S(1)}, s32[256]{0:T(256)S(1)}) all-reduce(s32[256]{0:T(256)S(1)} %dynamic-update-slice, s32[256]{0:T(256)S(1)} %dynamic-update-slice.1), channel_id=1, replica_groups=mesh['ctx'=256,'head'=2] {'ctx'}, use_global_device_ids=true, to_apply=%add | all-reduce | flops 512 | bytes 4096
  804.3 807.3 %while.15 = (s32[]{:T(128)}, s32[]{:T(128)}, s32[]{:T(128)}, s32[]{:T(128)}, s32[256]{0:T(256)S(1)}, /*index=5*/s32[256]{0:T(256)S(1)}, s32[]{:T(128)}, s32[]{:T(128)}) while((s32[]{:T(128)}, s32[]{:T(128)}, s32[]{:T(128)}, s32[]{:T(128)}, s32[256]{0:T(256)S(1)}, /*index=5*/s32[256]{0:T(256)S(1)}, s32[]{:T(128)}, s32[]{:T(128)}) %tuple.48), condition=%wide.region_3.4_spmd, body=%wide.region_2.3_spmd.sunk | while | flops 9 | bytes 206 | solution.py:24
  1620.8 2.1 collective-permute-start.7
  1623.1 5.7 collective-permute-done.5
  1628.8 11.2 collective-permute-done.6
  1640.0 5.8 collective-permute-done.7
  1645.9 4.3 fusion.1
  1651.1 5.0 fusion.11
  1656.1 5.1 convolution_bitcast_fusion
  1661.2 4.8 fusion
  1666.0 4.4 fusion.5
  1678.6 50.3 %collective-permute-done.15 = f32[2,128,4,128]{3,1,2,0:T(8,128)S(1)} collective-permute-done((f32[2,128,4,128]{3,1,2,0:T(8,128)S(1)}, f32[2,128,4,128]{3,1,2,0:T(8,128)S(1)}, u32[]{:S(2)}, u32[]{:S(2)}) %collective-permute-start.15) | collective-permute-done | bytes 524320 | tf_op jit(solution)/shard_map/ppermute | solution.py:30
  1730.1 16.2 collective-permute-done.14
  1747.6 5.3 collective-permute-done.13
  1754.9 4.8 fusion.28
  1760.6 11.6 collective-permute-done.10
  1773.0 23.0 %collective-permute-done.8 = f32[2,128,4,128]{3,1,2,0:T(8,128)} collective-permute-done((f32[2,128,4,128]{3,1,2,0:T(8,128)}, f32[2,128,4,128]{3,1,2,0:T(8,128)}, u32[]{:S(2)}, u32[]{:S(2)}) %collective-permute-start.8) | collective-permute-done | bytes 524320 | tf_op jit(solution)/shard_map/ppermute | solution.py:30
  1796.0 2.5 fusion.21
  1803.1 175.6 %psum.7 = f32[]{:T(128)} all-reduce(f32[]{:T(128)S(6)} %add.100), channel_id=1, replica_groups=mesh['ctx'=256,'head'=2] {'ctx','head'}, use_global_device_ids=true, to_apply=%region_12.13 | all-reduce | flops 1 | bytes 8 | tf_op jit(solution)/shard_map/psum | solution.py:127
  (577 shorter events, 335.3 us)
Async XLA Ops:
  0.6 1645.3 %copy-start = (f32[128,8,128]{2,1,0:T(8,128)S(1)}, f32[128,8,128]{2,1,0:T(8,128)}, u32[]{:S(2)}) copy-start(f32[128,8,128]{2,1,0:T(8,128)} %param.7) | copy-start | bytes 1572868
  1.8 1614.1 %collective-permute-start = (f32[2,128,4,128]{3,1,2,0:T(8,128)S(1)}, f32[2,128,4,128]{3,1,2,0:T(8,128)}, u32[]{:S(2)}, u32[]{:S(2)}) collective-permute-start(f32[2,128,4,128]{3,1,2,0:T(8,128)S(1)} %pad_maximum_fusion.1), channel_id=1, source_target_pairs={{0,16},{2,18},{4,20},{6,22},{8,24},{10,26},{12,28},{14,30},{16,32}... | collective-permute-start | bytes 1572872 | tf_op jit(solution)/shard_map/ppermute | solution.py:30
  12.3 1606.1 %collective-permute-start.1 = (f32[2,128,4,128]{3,1,2,0:T(8,128)S(1)}, f32[2,128,4,128]{3,1,2,0:T(8,128)}, u32[]{:S(2)}, u32[]{:S(2)}) collective-permute-start(f32[2,128,4,128]{3,1,2,0:T(8,128)S(1)} %pad_maximum_fusion.1), channel_id=1, source_target_pairs={{0,14},{2,16},{4,18},{6,20},{8,22},{10,24},{12,26},{14,28},{16,30}... | collective-permute-start | bytes 1572872 | tf_op jit(solution)/shard_map/ppermute | solution.py:30
  21.9 1598.8 %collective-permute-start.2 = (f32[2,128,4,128]{3,1,2,0:T(8,128)S(1)}, f32[2,128,4,128]{3,1,2,0:T(8,128)S(1)}, u32[]{:S(2)}, u32[]{:S(2)}) collective-permute-start(f32[2,128,4,128]{3,1,2,0:T(8,128)S(1)} %pad_maximum_fusion.1), channel_id=1, source_target_pairs={{0,12},{2,14},{4,16},{6,18},{8,20},{10,22},{12,24},{14,26},{16,28}... | collective-permute-start | bytes 1572872 | tf_op jit(solution)/shard_map/ppermute | solution.py:30
  24.7 1598.2 %collective-permute-start.3 = (f32[2,128,4,128]{3,1,2,0:T(8,128)S(1)}, f32[2,128,4,128]{3,1,2,0:T(8,128)S(1)}, u32[]{:S(2)}, u32[]{:S(2)}) collective-permute-start(f32[2,128,4,128]{3,1,2,0:T(8,128)S(1)} %pad_maximum_fusion.1), channel_id=1, source_target_pairs={{0,10},{2,12},{4,14},{6,16},{8,18},{10,20},{12,22},{14,24},{16,26}... | collective-permute-start | bytes 1572872 | tf_op jit(solution)/shard_map/ppermute | solution.py:30
  27.6 1595.4 %collective-permute-start.4 = (f32[2,128,4,128]{3,1,2,0:T(8,128)S(1)}, f32[2,128,4,128]{3,1,2,0:T(8,128)S(1)}, u32[]{:S(2)}, u32[]{:S(2)}) collective-permute-start(f32[2,128,4,128]{3,1,2,0:T(8,128)S(1)} %pad_maximum_fusion.1), channel_id=1, source_target_pairs={{0,8},{2,10},{4,12},{6,14},{8,16},{10,18},{12,20},{14,22},{16,24},... | collective-permute-start | bytes 1572872 | tf_op jit(solution)/shard_map/ppermute | solution.py:30
  1616.0 12.8 collective-permute-start.5
  1618.4 21.6 %collective-permute-start.6 = (f32[2,128,4,128]{3,1,2,0:T(8,128)S(1)}, f32[2,128,4,128]{3,1,2,0:T(8,128)S(1)}, u32[]{:S(2)}, u32[]{:S(2)}) collective-permute-start(f32[2,128,4,128]{3,1,2,0:T(8,128)S(1)} %pad_maximum_fusion.1), channel_id=1, source_target_pairs={{0,4},{2,6},{4,8},{6,10},{8,12},{10,14},{12,16},{14,18},{16,20},{1... | collective-permute-start | bytes 1572872 | tf_op jit(solution)/shard_map/ppermute | solution.py:30
  1620.8 25.0 %collective-permute-start.7 = (f32[2,128,4,128]{3,1,2,0:T(8,128)S(1)}, f32[2,128,4,128]{3,1,2,0:T(8,128)S(1)}, u32[]{:S(2)}, u32[]{:S(2)}) collective-permute-start(f32[2,128,4,128]{3,1,2,0:T(8,128)S(1)} %pad_maximum_fusion.1), channel_id=1, source_target_pairs={{0,2},{2,4},{4,6},{6,8},{8,10},{10,12},{12,14},{14,16},{16,18},{18... | collective-permute-start | bytes 1572872 | tf_op jit(solution)/shard_map/ppermute | solution.py:30
  1645.9 5.2 copy-start.5
  1661.2 9.3 copy-start.1
  1672.1 56.7 %collective-permute-start.15 = (f32[2,128,4,128]{3,1,2,0:T(8,128)S(1)}, f32[2,128,4,128]{3,1,2,0:T(8,128)S(1)}, u32[]{:S(2)}, u32[]{:S(2)}) collective-permute-start(f32[2,128,4,128]{3,1,2,0:T(8,128)S(1)} %get-tuple-element.146), channel_id=1, source_target_pairs={{16,0},{18,2},{20,4},{22,6},{24,8},{26,10},{28,12},{30,14},{32,16}... | collective-permute-start | bytes 1572872 | tf_op jit(solution)/shard_map/ppermute | solution.py:30
  1673.4 72.9 %collective-permute-start.14 = (f32[2,128,4,128]{3,1,2,0:T(8,128)S(1)}, f32[2,128,4,128]{3,1,2,0:T(8,128)S(1)}, u32[]{:S(2)}, u32[]{:S(2)}) collective-permute-start(f32[2,128,4,128]{3,1,2,0:T(8,128)S(1)} %get-tuple-element.147), channel_id=1, source_target_pairs={{14,0},{16,2},{18,4},{20,6},{22,8},{24,10},{26,12},{28,14},{30,16}... | collective-permute-start | bytes 1572872 | tf_op jit(solution)/shard_map/ppermute | solution.py:30
  1674.7 78.3 %collective-permute-start.13 = (f32[2,128,4,128]{3,1,2,0:T(8,128)S(1)}, f32[2,128,4,128]{3,1,2,0:T(8,128)S(1)}, u32[]{:S(2)}, u32[]{:S(2)}) collective-permute-start(f32[2,128,4,128]{3,1,2,0:T(8,128)S(1)} %get-tuple-element.145), channel_id=1, source_target_pairs={{12,0},{14,2},{16,4},{18,6},{20,8},{22,10},{24,12},{26,14},{28,16}... | collective-permute-start | bytes 1572872 | tf_op jit(solution)/shard_map/ppermute | solution.py:30
  1676.0 84.7 %collective-permute-start.12 = (f32[2,128,4,128]{3,1,2,0:T(8,128)}, f32[2,128,4,128]{3,1,2,0:T(8,128)}, u32[]{:S(2)}, u32[]{:S(2)}) collective-permute-start(f32[2,128,4,128]{3,1,2,0:T(8,128)} %get-tuple-element.144), channel_id=1, source_target_pairs={{10,0},{12,2},{14,4},{16,6},{18,8},{20,10},{22,12},{24,14},{26,16}... | collective-permute-start | bytes 1572872 | tf_op jit(solution)/shard_map/ppermute | solution.py:30
  1677.3 83.4 %collective-permute-start.11 = (f32[2,128,4,128]{3,1,2,0:T(8,128)}, f32[2,128,4,128]{3,1,2,0:T(8,128)}, u32[]{:S(2)}, u32[]{:S(2)}) collective-permute-start(f32[2,128,4,128]{3,1,2,0:T(8,128)} %get-tuple-element.143), channel_id=1, source_target_pairs={{8,0},{10,2},{12,4},{14,6},{16,8},{18,10},{20,12},{22,14},{24,16},... | collective-permute-start | bytes 1572872 | tf_op jit(solution)/shard_map/ppermute | solution.py:30
  1728.8 30.8 %copy-start.2 = (f32[2,128,4,128]{3,1,2,0:T(8,128)}, f32[2,128,4,128]{3,1,2,0:T(8,128)S(1)}, u32[]{:S(2)}) copy-start(f32[2,128,4,128]{3,1,2,0:T(8,128)S(1)} %collective-permute-done.15) | copy-start | bytes 1572868
  1728.8 43.4 %collective-permute-start.10 = (f32[2,128,4,128]{3,1,2,0:T(8,128)}, f32[2,128,4,128]{3,1,2,0:T(8,128)}, u32[]{:S(2)}, u32[]{:S(2)}) collective-permute-start(f32[2,128,4,128]{3,1,2,0:T(8,128)} %get-tuple-element.142), channel_id=1, source_target_pairs={{6,0},{8,2},{10,4},{12,6},{14,8},{16,10},{18,12},{20,14},{22,16},{... | collective-permute-start | bytes 1572872 | tf_op jit(solution)/shard_map/ppermute | solution.py:30
  1746.3 13.3 copy-start.3
  1746.3 26.7 %collective-permute-start.9 = (f32[2,128,4,128]{3,1,2,0:T(8,128)}, f32[2,128,4,128]{3,1,2,0:T(8,128)}, u32[]{:S(2)}, u32[]{:S(2)}) collective-permute-start(f32[2,128,4,128]{3,1,2,0:T(8,128)} %get-tuple-element.141), channel_id=1, source_target_pairs={{4,0},{6,2},{8,4},{10,6},{12,8},{14,10},{16,12},{18,14},{20,16},{2... | collective-permute-start | bytes 1572872 | tf_op jit(solution)/shard_map/ppermute | solution.py:30
  1752.9 6.7 copy-start.4
  1752.9 43.1 %collective-permute-start.8 = (f32[2,128,4,128]{3,1,2,0:T(8,128)}, f32[2,128,4,128]{3,1,2,0:T(8,128)}, u32[]{:S(2)}, u32[]{:S(2)}) collective-permute-start(f32[2,128,4,128]{3,1,2,0:T(8,128)} %get-tuple-element.140), channel_id=1, source_target_pairs={{2,0},{4,2},{6,4},{8,6},{10,8},{12,10},{14,12},{16,14},{18,16},{20... | collective-permute-start | bytes 1572872 | tf_op jit(solution)/shard_map/ppermute | solution.py:30
where the time goes:
time: 1990 us; the launch traced here: 1980 us
  blocking collectives  942 us (47%)
  loops' own time  508 us (26%)
  local copies, waits for them, and re-layouts  312 us (16%)
  waiting for transfers between devices  130 us (7%)
  starting transfers between devices  44.5 us (2%)
  matrix products  28.4 us (1%)
    unnamed x1, blocking collectives  766 us
    another operation x1, loops' own time, entering(): return lax.fori_loop(0, count - 1, lap, total)  508 us
    dynamic_slice x510, local copies, waits for them, and re-layouts, lap(): longer = join(total, jax.tree.map(lambda part: part[position], pieces))  300 us
    psum x1, blocking collectives, shards(): grad_square = lax.psum(local_sum, ('ctx', 'head')) / entry_count  176 us
    ppermute x16, waiting for transfers between devices, passed_along(): lax.ppermute(value, axis, [(source, source + steps) for source in range(f...  130 us
    ppermute x16, starting transfers between devices, passed_along(): lax.ppermute(value, axis, [(source, source + steps) for source in range(f...  44.5 us
  transfers between devices with their start and end apart: 16, of which 9 were waited for; matrix products, arithmetic and copies ran while one was open for 16% of the time, Pallas kernels for 0%

commit v1 on v0

v1 whole, which is shorter than its diff:
```python
import functools

import jax
import jax.numpy as jnp
from jax import lax
from jax.experimental import pallas as pl
from jax.experimental.pallas import tpu as pltpu
from jax.sharding import Mesh
from jax.sharding import PartitionSpec as P

HIDDEN = -1e30
TOK = 128
CHIP = 2 * TOK
REACH = 4
ROWS = 2 * CHIP
BODY = 4 * CHIP
F32, BF16 = jnp.float32, jnp.bfloat16
CTX = ("x", "yh", "z", "core")
VMEM_LIMIT = 56 << 20


def call(kernel, out_shape, in_specs, out_specs, grid=(), flops=0, moved=0, scratch=()):
    return pl.pallas_call(
        kernel,
        out_shape=out_shape,
        grid=grid,
        in_specs=in_specs,
        out_specs=out_specs,
        scratch_shapes=scratch,
        compiler_params=pltpu.CompilerParams(vmem_limit_bytes=VMEM_LIMIT),
        cost_estimate=pl.CostEstimate(flops=flops, bytes_accessed=moved, transcendentals=0),
    )


def whole(*shape):
    return pl.BlockSpec(shape, lambda *_: (0,) * len(shape))


def per_head(*shape):
    return pl.BlockSpec((1,) + shape, lambda h: (h,) + (0,) * len(shape))


SCALAR = pl.BlockSpec(memory_space=pltpu.SMEM)


def sds(*shape):
    return jax.ShapeDtypeStruct(shape, F32)


def split(x):
    high = x.astype(BF16)
    return high, (x - high.astype(F32)).astype(BF16)


def left(x, axis):
    high, low = split(x)
    return jnp.concatenate([high, low, high], axis=axis)


def right(x):
    high, low = split(x)
    return jnp.concatenate([high, high, low], axis=0)


def mm(a, b):
    return jnp.dot(a, b, preferred_element_type=F32)


def spot(core, shape, axis):
    slot = lax.broadcasted_iota(jnp.int32, shape, axis)
    half = jnp.where(slot >= TOK, 1, 0)
    half = jnp.where(core == 0, half, 1 - half)
    return half * TOK + (slot & (TOK - 1))


def begins_row(block_ref):
    return jnp.concatenate([block_ref[BODY : BODY + 1, :], block_ref[BODY + 1 : BODY + 2, :]], axis=1)


def begun_after(row, core):
    later = spot(core, (CHIP, CHIP), 1) > spot(core, (CHIP, CHIP), 0)
    return jnp.sum(jnp.where(later, row, 0.0), axis=1, keepdims=True)


def prep_kernel(core_ref, q_ref, d_ref, k_ref, v_ref, b_ref, qd_own, qd_sib, kv_own, kv_sib):
    core = core_ref[0]
    for side in range(2):

        @pl.when(core == side)
        def _():
            for source, kind in ((q_ref, 0), (d_ref, 1)):
                for head in range(4):
                    qd_own[kind, head] = source[pl.ds(4 * side + head, TOK, stride=8), :]
                    qd_sib[kind, head] = source[pl.ds(4 * (1 - side) + head, TOK, stride=8), :]
            for source, kind in ((k_ref, 0), (v_ref, 1)):
                for head in range(2):
                    rows = pl.ds((2 * kind + head) * TOK, TOK)
                    kv_own[rows, :] = source[pl.ds(2 * side + head, TOK, stride=4), :]
                    kv_sib[rows, :] = source[pl.ds(2 * (1 - side) + head, TOK, stride=4), :]

    row = lax.broadcasted_iota(jnp.int32, (8, TOK), 0)
    begins = jnp.where(row == 0, jnp.where(b_ref[...] > 0, 1.0, 0.0), 0.0)
    kv_own[4 * TOK :, :] = begins
    kv_sib[4 * TOK :, :] = begins


def pack_kernel(own_ref, far_ref, out_ref):
    for part in range(4):
        for half, source in ((0, own_ref), (1, far_ref)):
            out_ref[pl.ds(part * CHIP + half * TOK, TOK), :] = source[pl.ds(part * TOK, TOK), :]
    row = lax.broadcasted_iota(jnp.int32, (8, TOK), 0)
    first, second = (source[4 * TOK : 4 * TOK + 1, :] for source in (own_ref, far_ref))
    out_ref[BODY:, :] = jnp.where(row == 0, first, jnp.where(row == 1, second, 0.0))


def query_rows(own_ref, far_ref, kind, head):
    parts = []
    for mate in range(2):
        parts += [own_ref[kind, 2 * head + mate], far_ref[kind, 2 * head + mate]]
    return parts


def across(parts):
    return jnp.concatenate([part.T for part in parts], axis=1)


def near_kernel(width, chip_ref, core_ref, own_ref, far_ref, b0, b1, b2, b3, p_ref, dp_ref, stat_ref):
    head = pl.program_id(0)
    chip, core = chip_ref[0], core_ref[0]
    scale = width ** (-0.5)
    queries = right(across(query_rows(own_ref, far_ref, 0, head)) * scale)
    cotangent = right(across(query_rows(own_ref, far_ref, 1, head)))
    place_row = spot(core, (CHIP, CHIP), 1)
    place_col = spot(core, (CHIP, CHIP), 0)
    row0 = begins_row(b0)
    so_far = mm(
        jnp.broadcast_to(row0, (8, CHIP)).astype(BF16),
        jnp.where(place_col <= place_row, 1.0, 0.0).astype(BF16),
    )[0:1, :]
    so_far = jnp.concatenate([so_far, so_far], axis=1)
    causal = place_col <= place_row
    causal = jnp.concatenate([causal, causal], axis=1)
    between = so_far - jnp.sum(row0, axis=1, keepdims=True)
    peak = None
    for distance, block in enumerate((b0, b1, b2, b3)):
        row = begins_row(block)
        after = begun_after(row, core)
        if distance:
            after = jnp.where(chip >= distance, after, 1e6)
        if distance == 1:
            between = so_far
        elif distance > 1:
            between = between + total
        total = jnp.sum(row, axis=1, keepdims=True)
        scores = mm(left(block[pl.ds(head * CHIP, CHIP), :], 1), queries)
        seen = after + between <= 1.5
        if distance == 0:
            seen = seen & causal
        scores = jnp.where(seen, scores, HIDDEN)
        rows = pl.ds(distance * CHIP, CHIP)
        p_ref[0, rows, :] = scores
        top = jnp.max(scores, axis=0, keepdims=True)
        peak = top if peak is None else jnp.maximum(peak, top)
        dp_ref[0, rows, :] = mm(left(block[pl.ds(2 * CHIP + head * CHIP, CHIP), :], 1), cotangent)
    mass = jnp.zeros_like(peak)
    moment = jnp.zeros_like(peak)
    for distance in range(REACH):
        rows = pl.ds(distance * CHIP, CHIP)
        p = jnp.exp(p_ref[0, rows, :] - peak)
        p_ref[0, rows, :] = p
        mass = mass + jnp.sum(p, axis=0, keepdims=True)
        moment = moment + jnp.sum(p * dp_ref[0, rows, :], axis=0, keepdims=True)
    stat_ref[0, 0:1, :] = peak
    stat_ref[0, 1:2, :] = mass
    stat_ref[0, 2:3, :] = moment
    stat_ref[0, 3:4, :] = between + total


def gradients(p, ds, q_right, d_right, keys):
    k_high, k_low = split(keys.T)
    keys_left = jnp.concatenate([k_high, k_low, k_high], axis=1)
    ds_high, ds_low = split(ds)
    value_grad = mm(left(p, 1), d_right)
    key_grad = mm(jnp.concatenate([ds_high, ds_low, ds_high], axis=1), q_right)
    query_grad = mm(keys_left, jnp.concatenate([ds_high, ds_high, ds_low], axis=0))
    return key_grad, value_grad, query_grad


def last_kernel(width, chip_ref, core_ref, own_ref, far_ref, b4, stat_ref, out_ref, dq_ref, stat2_ref):
    head = pl.program_id(0)
    chip, core = chip_ref[0], core_ref[0]
    scale = width ** (-0.5)
    q_parts = query_rows(own_ref, far_ref, 0, head)
    d_parts = query_rows(own_ref, far_ref, 1, head)
    keys = block_keys = b4[pl.ds(head * CHIP, CHIP), :]
    scores = mm(left(keys, 1), right(across(q_parts) * scale))
    dp = mm(left(b4[pl.ds(2 * CHIP + head * CHIP, CHIP), :], 1), right(across(d_parts)))
    after = jnp.where(chip >= REACH, begun_after(begins_row(b4), core), 1e6)
    inside = spot(core, (CHIP, CHIP), 0) > spot(core, (CHIP, CHIP), 1)
    inside = jnp.concatenate([inside, inside], axis=1)
    seen = (after + stat_ref[0, 3:4, :] <= 1.5) & inside
    scores = jnp.where(seen, scores, HIDDEN)
    near_peak = stat_ref[0, 0:1, :]
    peak = jnp.maximum(near_peak, jnp.max(scores, axis=0, keepdims=True))
    shrink = jnp.exp(near_peak - peak)
    p = jnp.exp(scores - peak)
    mass = stat_ref[0, 1:2, :] * shrink + jnp.sum(p, axis=0, keepdims=True)
    moment = stat_ref[0, 2:3, :] * shrink + jnp.sum(p * dp, axis=0, keepdims=True)
    share = 1.0 / mass
    delta = moment * share
    p = p * share
    ds = p * (dp - delta)
    q_right = right(jnp.concatenate(q_parts, axis=0) * scale)
    d_right = right(jnp.concatenate(d_parts, axis=0))
    key_grad, value_grad, query_grad = gradients(p, ds, q_right, d_right, block_keys)
    out_ref[pl.ds(head * CHIP, CHIP), :] = key_grad
    out_ref[pl.ds(2 * CHIP + head * CHIP, CHIP), :] = value_grad
    dq_ref[0] = query_grad
    stat2_ref[0, 0:1, :] = shrink * share
    stat2_ref[0, 1:2, :] = delta


def back_kernel(width, own_ref, far_ref, b0, b1, b2, b3, p_ref, dp_ref, dq4_ref, stat2_ref,
                g0, g1, g2, g3, dq_own, dq_sib, sum_ref):
    head = pl.program_id(0)
    scale = width ** (-0.5)
    q_right = right(jnp.concatenate(query_rows(own_ref, far_ref, 0, head), axis=0) * scale)
    d_right = right(jnp.concatenate(query_rows(own_ref, far_ref, 1, head), axis=0))
    share, delta = stat2_ref[0, 0:1, :], stat2_ref[0, 1:2, :]
    total = dq4_ref[0]
    for distance, block, out in ((3, b3, g3), (2, b2, g2), (1, b1, g1), (0, b0, g0)):
        rows = pl.ds(distance * CHIP, CHIP)
        p = p_ref[0, rows, :] * share
        ds = p * (dp_ref[0, rows, :] - delta)
        key_grad, value_grad, query_grad = gradients(
            p, ds, q_right, d_right, block[pl.ds(head * CHIP, CHIP), :]
        )
        total = total + query_grad
        out[pl.ds(head * CHIP, CHIP), :] = key_grad
        out[pl.ds(2 * CHIP + head * CHIP, CHIP), :] = value_grad
    total = total * scale
    sum_ref[0] = jnp.broadcast_to(jnp.sum(total * total), (8, TOK))
    for mate in range(2):
        dq_own[mate] = total[:, (2 * mate) * TOK : (2 * mate + 1) * TOK].T
        dq_sib[mate] = total[:, (2 * mate + 1) * TOK : (2 * mate + 2) * TOK].T


def final_kernel(got_ref, own_ref, sum_ref, keep_ref, give_ref, row_ref):
    total = jnp.zeros((8, TOK), F32)
    for part in range(4):
        for half, out in ((0, keep_ref), (1, give_ref)):
            rows = pl.ds(part * CHIP + half * TOK, TOK)
            grad = got_ref[rows, :] + own_ref[rows, :]
            out[pl.ds(part * TOK, TOK), :] = grad
            total = total + jnp.sum((grad * grad).reshape(TOK // 8, 8, TOK), axis=0)
    row = jnp.sum(total, axis=0, keepdims=True) + (sum_ref[0, 0:1, :] + sum_ref[1, 0:1, :]) * (1.0 / TOK)
    row_ref[...] = jnp.broadcast_to(row, row_ref.shape)


def place_kernel(core_ref, dq_own, dq_far, kv_own, kv_far, q_out, k_out, v_out):
    core = core_ref[0]
    for side in range(2):

        @pl.when(core == side)
        def _():
            for source, where in ((dq_own, side), (dq_far, 1 - side)):
                for head in range(4):
                    q_out[pl.ds(4 * where + head, TOK, stride=8), :] = source[head]
            for source, where in ((kv_own, side), (kv_far, 1 - side)):
                for head in range(2):
                    k_out[pl.ds(2 * where + head, TOK, stride=4), :] = source[pl.ds(head * TOK, TOK), :]
                    v_out[pl.ds(2 * where + head, TOK, stride=4), :] = source[pl.ds((2 + head) * TOK, TOK), :]


def shards(sizes, queries, key_states, value_states, out_grad, step_begins):
    tokens, heads, width = queries.shape
    groups = key_states.shape[1]
    count = sizes["x"] * sizes["yh"] * sizes["z"] * sizes["core"]
    plane = sizes["x"] * sizes["yh"] * sizes["core"] * sizes["yl"]
    chip = lax.axis_index(("x", "yh", "z")).astype(jnp.int32).reshape(1)
    core = lax.axis_index("core").astype(jnp.int32).reshape(1)

    def swap(value):
        return lax.ppermute(value, "core", [(0, 1), (1, 0)])

    def onward(value, step):
        pairs = [(i, i + step) for i in range(max(0, -step), min(count, count - step))]
        return lax.ppermute(value, CTX, pairs)

    qd_own, qd_sib, kv_own, kv_sib = call(
        prep_kernel,
        (sds(2, 4, TOK, width), sds(2, 4, TOK, width), sds(4 * TOK + 8, width), sds(4 * TOK + 8, width)),
        [SCALAR] + [whole(tokens * heads, width)] * 2 + [whole(tokens * groups, width)] * 2 + [whole(1, tokens)],
        (whole(2, 4, TOK, width), whole(2, 4, TOK, width), whole(4 * TOK + 8, width), whole(4 * TOK + 8, width)),
        grid=(1,),
        moved=3 << 20,
    )(
        core,
        queries.reshape(tokens * heads, width),
        out_grad.reshape(tokens * heads, width),
        key_states.reshape(tokens * groups, width),
        value_states.reshape(tokens * groups, width),
        step_begins.reshape(1, tokens),
    )
    kv_far = swap(kv_sib)
    block = whole(BODY + 8, width)
    body = whole(BODY, width)
    first = call(
        pack_kernel,
        sds(BODY + 8, width),
        [whole(4 * TOK + 8, width)] * 2,
        block,
        grid=(1,),
        moved=1 << 20,
    )(kv_own, kv_far)
    blocks = [first]
    for _ in range(REACH):
        blocks.append(onward(blocks[-1], 2))
    qd_far = swap(qd_sib)
    qd = whole(2, 4, TOK, width)
    one = 2 * ROWS * CHIP * width
    p, dp, stat = call(
        functools.partial(near_kernel, width),
        (sds(2, REACH * CHIP, ROWS), sds(2, REACH * CHIP, ROWS), sds(2, 8, ROWS)),
        [SCALAR, SCALAR, qd, qd] + [block] * REACH,
        (per_head(REACH * CHIP, ROWS), per_head(REACH * CHIP, ROWS), per_head(8, ROWS)),
        grid=(2,),
        flops=2 * 2 * REACH * 3 * one,
        moved=12 << 20,
    )(chip, core, qd_own, qd_far, *blocks[:REACH])
    grad4, dq4, stat2 = call(
        functools.partial(last_kernel, width),
        (sds(BODY, width), sds(2, width, ROWS), sds(2, 8, ROWS)),
        [SCALAR, SCALAR, qd, qd, block, per_head(8, ROWS)],
        (body, per_head(width, ROWS), per_head(8, ROWS)),
        grid=(2,),
        flops=2 * 5 * 3 * one,
        moved=3 << 20,
    )(chip, core, qd_own, qd_far, blocks[REACH], stat)
    got = onward(grad4, -2)
    half = pl.BlockSpec((2, TOK, width), lambda h: (h, 0, 0))
    *grads, dq_own, dq_sib, dq_sum = call(
        functools.partial(back_kernel, width),
        (sds(BODY, width),) * REACH + (sds(4, TOK, width), sds(4, TOK, width), sds(2, 8, TOK)),
        [qd, qd] + [block] * REACH
        + [per_head(REACH * CHIP, ROWS)] * 2 + [per_head(width, ROWS), per_head(8, ROWS)],
        (body,) * REACH + (half, half, per_head(8, TOK)),
        grid=(2,),
        flops=2 * 3 * REACH * 3 * one,
        moved=14 << 20,
    )(qd_own, qd_far, *blocks[:REACH], p, dp, dq4, stat2)
    for distance in range(REACH - 1, 0, -1):
        got = onward(got + grads[distance], -2)
    dq_far = swap(dq_sib)
    keep, give, row = call(
        final_kernel,
        (sds(4 * TOK, width), sds(4 * TOK, width), sds(plane, width)),
        [body, body, whole(2, 8, TOK)],
        (whole(4 * TOK, width), whole(4 * TOK, width), whole(plane, width)),
        grid=(1,),
        moved=2 << 20,
    )(got, grads[0], dq_sum)
    kv_back = swap(give)
    parts = lax.all_to_all(row.reshape(plane, 1, width), ("x", "yh", "core", "yl"), 0, 0)
    parts = jnp.broadcast_to(jnp.sum(parts, axis=0, keepdims=True), (sizes["z"], 1, width))
    parts = lax.all_to_all(parts, "z", 0, 0)
    entries = count * sizes["yl"] * tokens * (heads + 2 * groups) * width
    grad_square = jnp.sum(parts) / entries
    dq, dk, dv = call(
        place_kernel,
        (sds(tokens * heads, width), sds(tokens * groups, width), sds(tokens * groups, width)),
        [SCALAR] + [whole(4, TOK, width)] * 2 + [whole(4 * TOK, width)] * 2,
        (whole(tokens * heads, width), whole(tokens * groups, width), whole(tokens * groups, width)),
        grid=(1,),
        moved=2 << 20,
    )(core, dq_own, dq_far, keep, kv_back)
    return (
        dq.reshape(queries.shape),
        dk.reshape(key_states.shape),
        dv.reshape(value_states.shape),
        grad_square,
    )


def solution(mesh):
    sizes = {"z": 16, "core": 2, "yh": 2, "yl": mesh.shape["head"]}
    sizes["x"] = mesh.shape["ctx"] // (sizes["z"] * sizes["core"] * sizes["yh"])
    names = ("x", "yh", "z", "core", "yl")
    fine = Mesh(mesh.devices.reshape([sizes[name] for name in names]), names)
    rows = P(CTX, "yl", None)
    return jax.shard_map(
        functools.partial(shards, sizes),
        mesh=fine,
        in_specs=(rows, rows, rows, rows, P(CTX)),
        out_specs=(rows, rows, rows, P()),
        check_vma=False,
    )
```

time: 1990 us -> 204 us (0.10)
  blocking collectives: 942 us -> 61.1 us
  loops' own time: 508 us -> 0 us
  local copies, waits for them, and re-layouts: 312 us -> 3.85 us
  waiting for transfers between devices: 130 us -> 52.1 us
  Pallas kernels: 0 us -> 31.7 us
  matrix products: 28.4 us -> 0 us
    unnamed x1 -> x0, blocking collectives: 766 us -> none
    another operation x1 -> x0, loops' own time: 508 us -> none  [entering(): return lax.fori_loop(0, count - 1, lap, total)]
    dynamic_slice x510 -> x0, local copies, waits for them, and re-layouts: 300 us -> none  [lap(): longer = join(total, jax.tree.map(lambda part: part[position], pieces))]
    psum x1 -> x0, blocking collectives: 176 us -> none  [shards(): grad_square = lax.psum(local_sum, ('ctx', 'head')) / entry_count]
    ppermute x16 -> x12, waiting for transfers between devices: 130 us -> 52.1 us  [the longest x8 50.8 us: onward(): return lax.ppermute(value, CTX, pairs)]
    all_to_all x0 -> x2, blocking collectives: none -> 61.1 us  [the longest x1 42 us: shards(): lax.all_to_all(row.reshape(plane, 1, width), ('x', 'yh', 'core', 'yl'), 0...]
    pallas_call x0 -> x7, Pallas kernels: none -> 31.7 us  [the longest x1 9.99 us: shards(): call(functools.partial(back_kernel, width), (sds(BODY, width),) * REACH +...]
    dot_general x6 -> x0, matrix products: 28.4 us -> none  [the longest x1 5.13 us: shards(): jnp.einsum('kgqs,qkgd->skd', weights, grad_grouped, precision=lax.Precisi...]
  transfers between devices with their start and end apart: 16 -> 12, of which waited for: 9 -> 8; matrix products, arithmetic and copies ran while one was open for 16% -> 0% of each run, Pallas kernels for 0% -> 10%
where the time goes in v1:
time: 204 us; the launch traced here: 203 us
  blocking collectives  61.1 us (30%)
  waiting for transfers between devices  52.1 us (26%)
  starting transfers between devices  47.5 us (23%)
  Pallas kernels  31.7 us (16%)
  other arithmetic  3.94 us (2%)
  local copies, waits for them, and re-layouts  3.85 us (2%)
  between operations  2.64 us (1%)
    ppermute x8, waiting for transfers between devices, onward(): return lax.ppermute(value, CTX, pairs)  50.8 us
    all_to_all x1, blocking collectives, shards(): lax.all_to_all(row.reshape(plane, 1, width), ('x', 'yh', 'core', 'yl'), 0...  42 us
    ppermute x4, starting transfers between devices, swap(): return lax.ppermute(value, 'core', [(0, 1), (1, 0)])  28.7 us
    all_to_all x1, blocking collectives, shards(): parts = lax.all_to_all(parts, 'z', 0, 0)  19.1 us
    ppermute x8, starting transfers between devices, onward(): return lax.ppermute(value, CTX, pairs)  18.7 us
    pallas_call x1, Pallas kernels, shards(): call(functools.partial(back_kernel, width), (sds(BODY, width),) * REACH +...  9.99 us
    pallas_call x1, Pallas kernels, shards(): call(functools.partial(near_kernel, width), (sds(2, REACH * CHIP, ROWS),...  7.92 us
    pallas_call x1, Pallas kernels, shards(): call(functools.partial(last_kernel, width), (sds(BODY, width), sds(2, wid...  4.89 us
  transfers between devices with their start and end apart: 12, of which 8 were waited for; matrix products, arithmetic and copies ran while one was open for 0% of the time, Pallas kernels for 10%

profile of v1, /device:TPU:1, one launch (start us, length us, event | category | flops | bytes accessed | tf_op | source)
XLA Modules:
  0.0 202.9 jit_solution(10815621442337460059)
XLA Ops:
  0.6 2.7 %shard_map.84 = (f32[2,4,128,128]{3,2,1,0:T(8,128)}, f32[2,4,128,128]{3,2,1,0:T(8,128)}, f32[520,128]{1,0:T(8,128)}, f32[520,128]{1,0:T(8,128)}) custom-call(s32[1]{0:T(128)} %bitcast.core_ref, f32[1024,128]{1,0:T(8,128)} %bitcast.14, f32[1024,128]{1,0:T(8,128)} %bitcast.15, f32[512,128]{1,0:T(8,128)} %bitcast.16, f32[512,128]{1,0:T(8,128)} %bitcast.17, ...), custom_call_target="tpu_custom_call" | custom-call | bytes 3145728 | tf_op jit(solution)/shard_map/pallas_call | solution.py:290
  3.3 8.8 %collective-permute-start.1 = (f32[520,128]{1,0:T(8,128)}, f32[520,128]{1,0:T(8,128)S(1)}, u32[]{:S(2)}, u32[]{:S(2)}) collective-permute-start(f32[520,128]{1,0:T(8,128)} %get-tuple-element.30), channel_id=1, source_target_pairs={{0,2},{2,0},{1,3},{3,1},{4,6},{6,4},{5,7},{7,5},{8,10},{10,8},{9,1... | collective-permute-start | bytes 798728 | tf_op jit(solution)/shard_map/ppermute | solution.py:284
  12.1 1.4 collective-permute-done.1.far_ref
  14.2 1.9 shard_map.85.b0
  16.1 1.3 collective-permute-start.2
  17.4 11.6 %collective-permute-done.2.b1 = f32[1032,128]{1,0:T(8,128)S(1)} collective-permute-done((f32[1032,128]{1,0:T(8,128)}, f32[1032,128]{1,0:T(8,128)S(1)}, u32[]{:S(2)}, u32[]{:S(2)}) %collective-permute-start.2) | collective-permute-done | bytes 528416 | tf_op jit(solution)/shard_map/ppermute | solution.py:288
  29.0 4.0 %collective-permute-start.3 = (f32[1032,128]{1,0:T(8,128)S(1)}, f32[1032,128]{1,0:T(8,128)S(1)}, u32[]{:S(2)}, u32[]{:S(2)}) collective-permute-start(f32[1032,128]{1,0:T(8,128)S(1)} %collective-permute-done.2.b1), channel_id=1, source_target_pairs={{0,4},{2,6},{4,8},{6,10},{8,12},{10,14},{12,16},{14,18},{16,20},{1... | collective-permute-start | bytes 1585160 | tf_op jit(solution)/shard_map/ppermute | solution.py:288
  33.0 10.4 %collective-permute-done.3.b2 = f32[1032,128]{1,0:T(8,128)S(1)} collective-permute-done((f32[1032,128]{1,0:T(8,128)S(1)}, f32[1032,128]{1,0:T(8,128)S(1)}, u32[]{:S(2)}, u32[]{:S(2)}) %collective-permute-start.3) | collective-permute-done | bytes 528416 | tf_op jit(solution)/shard_map/ppermute | solution.py:288
  43.4 4.1 %collective-permute-start.4 = (f32[1032,128]{1,0:T(8,128)S(1)}, f32[1032,128]{1,0:T(8,128)S(1)}, u32[]{:S(2)}, u32[]{:S(2)}) collective-permute-start(f32[1032,128]{1,0:T(8,128)S(1)} %collective-permute-done.3.b2), channel_id=1, source_target_pairs={{0,4},{2,6},{4,8},{6,10},{8,12},{10,14},{12,16},{14,18},{16,20},{1... | collective-permute-start | bytes 1585160 | tf_op jit(solution)/shard_map/ppermute | solution.py:288
  47.6 4.0 %collective-permute-start = (f32[2,4,128,128]{3,2,1,0:T(8,128)}, f32[2,4,128,128]{3,2,1,0:T(8,128)S(1)}, u32[]{:S(2)}, u32[]{:S(2)}) collective-permute-start(f32[2,4,128,128]{3,2,1,0:T(8,128)} %get-tuple-element.28), channel_id=1, source_target_pairs={{0,2},{2,0},{1,3},{3,1},{4,6},{6,4},{5,7},{7,5},{8,10},{10,8},{9,1... | collective-permute-start | bytes 1572872 | tf_op jit(solution)/shard_map/ppermute | solution.py:284
  51.5 5.5 %collective-permute-done.4.b3 = f32[1032,128]{1,0:T(8,128)S(1)} collective-permute-done((f32[1032,128]{1,0:T(8,128)S(1)}, f32[1032,128]{1,0:T(8,128)S(1)}, u32[]{:S(2)}, u32[]{:S(2)}) %collective-permute-start.4) | collective-permute-done | bytes 528416 | tf_op jit(solution)/shard_map/ppermute | solution.py:288
  57.0 4.1 %collective-permute-start.5 = (f32[1032,128]{1,0:T(8,128)S(1)}, f32[1032,128]{1,0:T(8,128)S(1)}, u32[]{:S(2)}, u32[]{:S(2)}) collective-permute-start(f32[1032,128]{1,0:T(8,128)S(1)} %collective-permute-done.4.b3), channel_id=1, source_target_pairs={{0,4},{2,6},{4,8},{6,10},{8,12},{10,14},{12,16},{14,18},{16,20},{1... | collective-permute-start | bytes 1585160 | tf_op jit(solution)/shard_map/ppermute | solution.py:288
  62.0 7.9 %shard_map.86 = (f32[2,1024,512]{2,1,0:T(8,128)}, f32[2,1024,512]{2,1,0:T(8,128)}, f32[2,8,512]{2,1,0:T(8,128)}) custom-call(s32[1]{0:T(128)} %bitcast.6.chip_ref, s32[1]{0:T(128)} %bitcast.core_ref, f32[2,4,128,128]{3,2,1,0:T(8,128)} %get-tuple-element.27.own_ref, f32[2,4,128,128]{3,2,1,0:T(8,128)} %copy-done.3, f32[1032,128]{1,0:T(8,128)} %shard_map.85.b0, ...), custom_call_target="tpu_custom_call" | custom-call | flops 1610612736 | bytes 12582912 | tf_op jit(solution)/shard_map/pallas_call | solution.py:322
  70.7 4.9 %shard_map.87 = (f32[1024,128]{1,0:T(8,128)}, f32[2,128,512]{2,1,0:T(8,128)}, f32[2,8,512]{2,1,0:T(8,128)}) custom-call(s32[1]{0:T(128)} %bitcast.6.chip_ref, s32[1]{0:T(128)} %bitcast.core_ref, f32[2,4,128,128]{3,2,1,0:T(8,128)} %get-tuple-element.27.own_ref, f32[2,4,128,128]{3,2,1,0:T(8,128)} %copy-done.3, f32[1032,128]{1,0:T(8,128)} %copy-done.8, ...), custom_call_target="tpu_custom_call" | custom-call | flops 1006632960 | bytes 3145728 | tf_op jit(solution)/shard_map/pallas_call | solution.py:331
  76.9 10.0 %shard_map.88 = (f32[1024,128]{1,0:T(8,128)}, f32[1024,128]{1,0:T(8,128)}, f32[1024,128]{1,0:T(8,128)}, f32[1024,128]{1,0:T(8,128)}, f32[4,128,128]{2,1,0:T(8,12...) custom-call(f32[2,4,128,128]{3,2,1,0:T(8,128)} %get-tuple-element.27.own_ref, f32[2,4,128,128]{3,2,1,0:T(8,128)} %copy-done.3, ...), custom_call_target="tpu_custom_call" | custom-call | flops 2415919104 | bytes 14680064 | tf_op jit(solution)/shard_map/pallas_call | solution.py:342
  86.9 1.4 collective-permute-done.7
  90.7 9.7 %collective-permute-done.8 = f32[1024,128]{1,0:T(8,128)S(1)} collective-permute-done((f32[1024,128]{1,0:T(8,128)S(1)}, f32[1024,128]{1,0:T(8,128)S(1)}, u32[]{:S(2)}, u32[]{:S(2)}) %collective-permute-start.8) | collective-permute-done | bytes 524320 | tf_op jit(solution)/shard_map/ppermute | solution.py:288
  102.8 10.8 %collective-permute-done.9 = f32[1024,128]{1,0:T(8,128)S(1)} collective-permute-done((f32[1024,128]{1,0:T(8,128)S(1)}, f32[1024,128]{1,0:T(8,128)S(1)}, u32[]{:S(2)}, u32[]{:S(2)}) %collective-permute-start.9) | collective-permute-done | bytes 524320 | tf_op jit(solution)/shard_map/ppermute | solution.py:288
  116.0 7.3 %collective-permute-start.6 = (f32[4,128,128]{2,1,0:T(8,128)S(1)}, f32[4,128,128]{2,1,0:T(8,128)S(1)}, u32[]{:S(2)}, u32[]{:S(2)}) collective-permute-start(f32[4,128,128]{2,1,0:T(8,128)S(1)} %copy-done.9), channel_id=1, source_target_pairs={{0,2},{2,0},{1,3},{3,1},{4,6},{6,4},{5,7},{7,5},{8,10},{10,8},{9,1... | collective-permute-start | bytes 786440 | tf_op jit(solution)/shard_map/ppermute | solution.py:284
  125.5 2.0 shard_map.89
  127.5 8.7 %collective-permute-start.11 = (f32[512,128]{1,0:T(8,128)}, f32[512,128]{1,0:T(8,128)S(1)}, u32[]{:S(2)}, u32[]{:S(2)}) collective-permute-start(f32[512,128]{1,0:T(8,128)} %get-tuple-element.45), channel_id=1, source_target_pairs={{0,2},{2,0},{1,3},{3,1},{4,6},{6,4},{5,7},{7,5},{8,10},{10,8},{9,1... | collective-permute-start | bytes 786440 | tf_op jit(solution)/shard_map/ppermute | solution.py:284
  136.1 42.0 %all_to_all.10 = f32[32,1,128]{2,1,0:T(1,128)S(1)} all-to-all(f32[32,1,128]{2,1,0:T(1,128)} %bitcast.19), channel_id=1, replica_groups=mesh['x'=4,'yh'=2,'z'=16,'core'=2,'yl'=2] {'x','yh','core','yl'}, dimensions={0} | all-to-all | bytes 32768 | tf_op jit(solution)/shard_map/all_to_all | solution.py:364
  178.2 19.1 %all_to_all.11 = f32[16,1,128]{2,1,0:T(1,128)S(1)} all-to-all(f32[16,1,128]{2,1,0:T(1,128)S(1)} %broadcast_in_dim.2), channel_id=1, replica_groups=mesh['x'=4,'yh'=2,'z'=16,'core'=2,'yl'=2] {'z'}, dimensions={0} | all-to-all | bytes 16384 | tf_op jit(solution)/shard_map/all_to_all | solution.py:366
  199.4 2.4 %shard_map.90 = (f32[1024,128]{1,0:T(8,128)}, f32[512,128]{1,0:T(8,128)}, f32[512,128]{1,0:T(8,128)}) custom-call(s32[1]{0:T(128)} %bitcast.core_ref, f32[4,128,128]{2,1,0:T(8,128)} %get-tuple-element.36.dq_own, f32[4,128,128]{2,1,0:T(8,128)} %copy-done.6, f32[512,128]{1,0:T(8,128)} %get-tuple-element.44.kv_own, f32[512,128]{1,0:T(8,128)} %copy-done.7), custom_call_target="tpu_custom_call" | custom-call | bytes 2097152 | tf_op jit(solution)/shard_map/pallas_call | solution.py:369
  (35 shorter events, 14.3 us)
Async XLA Ops:
  3.3 10.1 %collective-permute-start.1 = (f32[520,128]{1,0:T(8,128)}, f32[520,128]{1,0:T(8,128)S(1)}, u32[]{:S(2)}, u32[]{:S(2)}) collective-permute-start(f32[520,128]{1,0:T(8,128)} %get-tuple-element.30), channel_id=1, source_target_pairs={{0,2},{2,0},{1,3},{3,1},{4,6},{6,4},{5,7},{7,5},{8,10},{10,8},{9,1... | collective-permute-start | bytes 798728 | tf_op jit(solution)/shard_map/ppermute | solution.py:284
  13.5 0.7 copy-start.5
  16.1 12.9 %collective-permute-start.2 = (f32[1032,128]{1,0:T(8,128)}, f32[1032,128]{1,0:T(8,128)S(1)}, u32[]{:S(2)}, u32[]{:S(2)}) collective-permute-start(f32[1032,128]{1,0:T(8,128)} %shard_map.85.b0), channel_id=1, source_target_pairs={{0,4},{2,6},{4,8},{6,10},{8,12},{10,14},{12,16},{14,18},{16,20},{1... | collective-permute-start | bytes 1585160 | tf_op jit(solution)/shard_map/ppermute | solution.py:288
  29.0 32.2 %copy-start = (f32[1032,128]{1,0:T(8,128)}, f32[1032,128]{1,0:T(8,128)S(1)}, u32[]{:S(2)}) copy-start(f32[1032,128]{1,0:T(8,128)S(1)} %collective-permute-done.2.b1) | copy-start | bytes 1585156
  29.0 14.4 %collective-permute-start.3 = (f32[1032,128]{1,0:T(8,128)S(1)}, f32[1032,128]{1,0:T(8,128)S(1)}, u32[]{:S(2)}, u32[]{:S(2)}) collective-permute-start(f32[1032,128]{1,0:T(8,128)S(1)} %collective-permute-done.2.b1), channel_id=1, source_target_pairs={{0,4},{2,6},{4,8},{6,10},{8,12},{10,14},{12,16},{14,18},{16,20},{1... | collective-permute-start | bytes 1585160 | tf_op jit(solution)/shard_map/ppermute | solution.py:288
  43.4 17.8 %copy-start.1 = (f32[1032,128]{1,0:T(8,128)}, f32[1032,128]{1,0:T(8,128)S(1)}, u32[]{:S(2)}) copy-start(f32[1032,128]{1,0:T(8,128)S(1)} %collective-permute-done.3.b2) | copy-start | bytes 1585156
  43.4 13.6 %collective-permute-start.4 = (f32[1032,128]{1,0:T(8,128)S(1)}, f32[1032,128]{1,0:T(8,128)S(1)}, u32[]{:S(2)}, u32[]{:S(2)}) collective-permute-start(f32[1032,128]{1,0:T(8,128)S(1)} %collective-permute-done.3.b2), channel_id=1, source_target_pairs={{0,4},{2,6},{4,8},{6,10},{8,12},{10,14},{12,16},{14,18},{16,20},{1... | collective-permute-start | bytes 1585160 | tf_op jit(solution)/shard_map/ppermute | solution.py:288
  47.6 13.6 %collective-permute-start = (f32[2,4,128,128]{3,2,1,0:T(8,128)}, f32[2,4,128,128]{3,2,1,0:T(8,128)S(1)}, u32[]{:S(2)}, u32[]{:S(2)}) collective-permute-start(f32[2,4,128,128]{3,2,1,0:T(8,128)} %get-tuple-element.28), channel_id=1, source_target_pairs={{0,2},{2,0},{1,3},{3,1},{4,6},{6,4},{5,7},{7,5},{8,10},{10,8},{9,1... | collective-permute-start | bytes 1572872 | tf_op jit(solution)/shard_map/ppermute | solution.py:284
  57.0 4.2 %copy-start.2 = (f32[1032,128]{1,0:T(8,128)}, f32[1032,128]{1,0:T(8,128)S(1)}, u32[]{:S(2)}) copy-start(f32[1032,128]{1,0:T(8,128)S(1)} %collective-permute-done.4.b3) | copy-start | bytes 1585156
  57.0 12.9 %collective-permute-start.5 = (f32[1032,128]{1,0:T(8,128)S(1)}, f32[1032,128]{1,0:T(8,128)S(1)}, u32[]{:S(2)}, u32[]{:S(2)}) collective-permute-start(f32[1032,128]{1,0:T(8,128)S(1)} %collective-permute-done.4.b3), channel_id=1, source_target_pairs={{0,4},{2,6},{4,8},{6,10},{8,12},{10,14},{12,16},{14,18},{16,20},{1... | collective-permute-start | bytes 1585160 | tf_op jit(solution)/shard_map/ppermute | solution.py:288
  61.2 0.8 copy-start.3
  69.9 0.8 copy-start.8
  75.6 12.7 %collective-permute-start.7 = (f32[1024,128]{1,0:T(8,128)}, f32[1024,128]{1,0:T(8,128)S(1)}, u32[]{:S(2)}, u32[]{:S(2)}) collective-permute-start(f32[1024,128]{1,0:T(8,128)} %get-tuple-element.38), channel_id=1, source_target_pairs={{4,0},{6,2},{8,4},{10,6},{12,8},{14,10},{16,12},{18,14},{20,16},{2... | collective-permute-start | bytes 1572872 | tf_op jit(solution)/shard_map/ppermute | solution.py:288
  86.9 29.2 %copy-start.9 = (f32[4,128,128]{2,1,0:T(8,128)S(1)}, f32[4,128,128]{2,1,0:T(8,128)}, u32[]{:S(2)}) copy-start(f32[4,128,128]{2,1,0:T(8,128)} %get-tuple-element.37) | copy-start | bytes 786436
  89.4 11.0 %collective-permute-start.8 = (f32[1024,128]{1,0:T(8,128)S(1)}, f32[1024,128]{1,0:T(8,128)S(1)}, u32[]{:S(2)}, u32[]{:S(2)}) collective-permute-start(f32[1024,128]{1,0:T(8,128)S(1)} %add.17), channel_id=1, source_target_pairs={{4,0},{6,2},{8,4},{10,6},{12,8},{14,10},{16,12},{18,14},{20,16},{2... | collective-permute-start | bytes 1572872 | tf_op jit(solution)/shard_map/ppermute | solution.py:288
  101.5 12.1 %collective-permute-start.9 = (f32[1024,128]{1,0:T(8,128)S(1)}, f32[1024,128]{1,0:T(8,128)S(1)}, u32[]{:S(2)}, u32[]{:S(2)}) collective-permute-start(f32[1024,128]{1,0:T(8,128)S(1)} %add.18), channel_id=1, source_target_pairs={{4,0},{6,2},{8,4},{10,6},{12,8},{14,10},{16,12},{18,14},{20,16},{2... | collective-permute-start | bytes 1572872 | tf_op jit(solution)/shard_map/ppermute | solution.py:288
  114.7 9.9 %collective-permute-start.10 = (f32[1024,128]{1,0:T(8,128)S(1)}, f32[1024,128]{1,0:T(8,128)S(1)}, u32[]{:S(2)}, u32[]{:S(2)}) collective-permute-start(f32[1024,128]{1,0:T(8,128)S(1)} %add.19), channel_id=1, source_target_pairs={{4,0},{6,2},{8,4},{10,6},{12,8},{14,10},{16,12},{18,14},{20,16},{2... | collective-permute-start | bytes 1572872 | tf_op jit(solution)/shard_map/ppermute | solution.py:288
  116.0 82.5 %collective-permute-start.6 = (f32[4,128,128]{2,1,0:T(8,128)S(1)}, f32[4,128,128]{2,1,0:T(8,128)S(1)}, u32[]{:S(2)}, u32[]{:S(2)}) collective-permute-start(f32[4,128,128]{2,1,0:T(8,128)S(1)} %copy-done.9), channel_id=1, source_target_pairs={{0,2},{2,0},{1,3},{3,1},{4,6},{6,4},{5,7},{7,5},{8,10},{10,8},{9,1... | collective-permute-start | bytes 786440 | tf_op jit(solution)/shard_map/ppermute | solution.py:284
  124.7 0.8 copy-start.4
  127.5 71.1 %collective-permute-start.11 = (f32[512,128]{1,0:T(8,128)}, f32[512,128]{1,0:T(8,128)S(1)}, u32[]{:S(2)}, u32[]{:S(2)}) collective-permute-start(f32[512,128]{1,0:T(8,128)} %get-tuple-element.45), channel_id=1, source_target_pairs={{0,2},{2,0},{1,3},{3,1},{4,6},{6,4},{5,7},{7,5},{8,10},{10,8},{9,1... | collective-permute-start | bytes 786440 | tf_op jit(solution)/shard_map/ppermute | solution.py:284
  198.6 0.7 copy-start.6
  198.6 0.8 copy-start.7

commit v2 on v1

v2 whole, which is shorter than its diff:
```python
import functools

import jax
import jax.numpy as jnp
from jax import lax
from jax.experimental import pallas as pl
from jax.experimental.pallas import tpu as pltpu
from jax.sharding import Mesh
from jax.sharding import PartitionSpec as P

HIDDEN = -1e30
TOK = 128
CHIP = 2 * TOK
REACH = 4
ROWS = 2 * CHIP
BODY = 2 * CHIP
F32, BF16 = jnp.float32, jnp.bfloat16
CTX = ("x", "yh", "z", "core")


def call(kernel, out_shape, in_specs, out_specs, grid=(1,), flops=0, moved=0, vmem=12):
    return pl.pallas_call(
        kernel,
        out_shape=out_shape,
        grid=grid,
        in_specs=in_specs,
        out_specs=out_specs,
        compiler_params=pltpu.CompilerParams(vmem_limit_bytes=vmem << 20),
        cost_estimate=pl.CostEstimate(flops=flops, bytes_accessed=moved, transcendentals=0),
    )


def whole(*shape):
    return pl.BlockSpec(shape, lambda *_: (0,) * len(shape))


def per_head(*shape):
    return pl.BlockSpec((1,) + shape, lambda h: (h,) + (0,) * len(shape))


SCALAR = pl.BlockSpec(memory_space=pltpu.SMEM)


def sds(*shape):
    return jax.ShapeDtypeStruct(shape, F32)


def split(x):
    high = x.astype(BF16)
    return high, (x - high.astype(F32)).astype(BF16)


def left(x, axis):
    high, low = split(x)
    return jnp.concatenate([high, low, high], axis=axis)


def right(x):
    high, low = split(x)
    return jnp.concatenate([high, high, low], axis=0)


def mm(a, b):
    return jnp.dot(a, b, preferred_element_type=F32)


def spot(core, shape, axis):
    slot = lax.broadcasted_iota(jnp.int32, shape, axis)
    half = jnp.where(slot >= TOK, 1, 0)
    half = jnp.where(core == 0, half, 1 - half)
    return half * TOK + (slot & (TOK - 1))


def begins_row(block_ref):
    return jnp.concatenate([block_ref[BODY : BODY + 1, :], block_ref[BODY + 1 : BODY + 2, :]], axis=1)


def begun_after(row, core):
    later = spot(core, (CHIP, CHIP), 1) > spot(core, (CHIP, CHIP), 0)
    return jnp.sum(jnp.where(later, row, 0.0), axis=1, keepdims=True)


def prep_kernel(core_ref, q_ref, d_ref, k_ref, v_ref, b_ref, qd_own, qd_sib, kv_own, kv_sib):
    core = core_ref[0]
    for side in range(2):

        @pl.when(core == side)
        def _():
            for source, kind in ((q_ref, 0), (d_ref, 1)):
                for head in range(4):
                    qd_own[kind, head] = source[pl.ds(4 * side + head, TOK, stride=8), :]
                    qd_sib[kind, head] = source[pl.ds(4 * (1 - side) + head, TOK, stride=8), :]
            for source, kind in ((k_ref, 0), (v_ref, 1)):
                for head in range(2):
                    rows = pl.ds((2 * kind + head) * TOK, TOK)
                    kv_own[rows, :] = source[pl.ds(2 * side + head, TOK, stride=4), :]
                    kv_sib[rows, :] = source[pl.ds(2 * (1 - side) + head, TOK, stride=4), :]

    row = lax.broadcasted_iota(jnp.int32, (8, TOK), 0)
    begins = jnp.where(row == 0, jnp.where(b_ref[...] > 0, 1.0, 0.0), 0.0)
    kv_own[4 * TOK :, :] = begins
    kv_sib[4 * TOK :, :] = begins


def pack_kernel(own_ref, far_ref, k_ref, v_ref):
    for kind, out in ((0, k_ref), (1, v_ref)):
        for head in range(2):
            for half, source in ((0, own_ref), (1, far_ref)):
                out[pl.ds(head * CHIP + half * TOK, TOK), :] = source[pl.ds((2 * kind + head) * TOK, TOK), :]
    row = lax.broadcasted_iota(jnp.int32, (8, TOK), 0)
    first, second = (source[4 * TOK : 4 * TOK + 1, :] for source in (own_ref, far_ref))
    k_ref[BODY:, :] = jnp.where(row == 0, first, jnp.where(row == 1, second, 0.0))


def query_rows(own_ref, far_ref, kind, head):
    parts = []
    for mate in range(2):
        parts += [own_ref[kind, 2 * head + mate], far_ref[kind, 2 * head + mate]]
    return parts


def across(parts):
    return jnp.concatenate([part.T for part in parts], axis=1)


def near_kernel(width, chip_ref, core_ref, own_ref, far_ref, *refs):
    k_refs, v_refs, (p_ref, dp_ref, stat_ref) = refs[:REACH], refs[REACH : 2 * REACH], refs[2 * REACH :]
    head = pl.program_id(0)
    chip, core = chip_ref[0], core_ref[0]
    scale = width ** (-0.5)
    queries = right(across(query_rows(own_ref, far_ref, 0, head)) * scale)
    cotangent = right(across(query_rows(own_ref, far_ref, 1, head)))
    place_row = spot(core, (CHIP, CHIP), 1)
    place_col = spot(core, (CHIP, CHIP), 0)
    row0 = begins_row(k_refs[0])
    so_far = mm(
        jnp.broadcast_to(row0, (8, CHIP)).astype(BF16),
        jnp.where(place_col <= place_row, 1.0, 0.0).astype(BF16),
    )[0:1, :]
    so_far = jnp.concatenate([so_far, so_far], axis=1)
    causal = place_col <= place_row
    causal = jnp.concatenate([causal, causal], axis=1)
    between = so_far - jnp.sum(row0, axis=1, keepdims=True)
    peak = None
    for distance, (k_ref, v_ref) in enumerate(zip(k_refs, v_refs)):
        row = begins_row(k_ref)
        after = begun_after(row, core)
        if distance:
            after = jnp.where(chip >= distance, after, 1e6)
        if distance == 1:
            between = so_far
        elif distance > 1:
            between = between + total
        total = jnp.sum(row, axis=1, keepdims=True)
        scores = mm(left(k_ref[pl.ds(head * CHIP, CHIP), :], 1), queries)
        seen = after + between <= 1.5
        if distance == 0:
            seen = seen & causal
        scores = jnp.where(seen, scores, HIDDEN)
        rows = pl.ds(distance * CHIP, CHIP)
        p_ref[0, rows, :] = scores
        top = jnp.max(scores, axis=0, keepdims=True)
        peak = top if peak is None else jnp.maximum(peak, top)
        dp_ref[0, rows, :] = mm(left(v_ref[pl.ds(head * CHIP, CHIP), :], 1), cotangent)
    mass = jnp.zeros_like(peak)
    moment = jnp.zeros_like(peak)
    for distance in range(REACH):
        rows = pl.ds(distance * CHIP, CHIP)
        p = jnp.exp(p_ref[0, rows, :] - peak)
        p_ref[0, rows, :] = p
        mass = mass + jnp.sum(p, axis=0, keepdims=True)
        moment = moment + jnp.sum(p * dp_ref[0, rows, :], axis=0, keepdims=True)
    stat_ref[0, 0:1, :] = peak
    stat_ref[0, 1:2, :] = mass
    stat_ref[0, 2:3, :] = moment
    stat_ref[0, 3:4, :] = between + total


def gradients(p, ds, q_right, d_right, keys):
    k_high, k_low = split(keys.T)
    keys_left = jnp.concatenate([k_high, k_low, k_high], axis=1)
    ds_high, ds_low = split(ds)
    value_grad = mm(left(p, 1), d_right)
    key_grad = mm(jnp.concatenate([ds_high, ds_low, ds_high], axis=1), q_right)
    query_grad = mm(keys_left, jnp.concatenate([ds_high, ds_high, ds_low], axis=0))
    return key_grad, value_grad, query_grad


def last_kernel(width, chip_ref, core_ref, own_ref, far_ref, k_ref, v_ref, stat_ref, gk_ref, gv_ref, dq_ref, stat2_ref):
    head = pl.program_id(0)
    chip, core = chip_ref[0], core_ref[0]
    scale = width ** (-0.5)
    q_parts = query_rows(own_ref, far_ref, 0, head)
    d_parts = query_rows(own_ref, far_ref, 1, head)
    keys = k_ref[pl.ds(head * CHIP, CHIP), :]
    scores = mm(left(keys, 1), right(across(q_parts) * scale))
    dp = mm(left(v_ref[pl.ds(head * CHIP, CHIP), :], 1), right(across(d_parts)))
    after = jnp.where(chip >= REACH, begun_after(begins_row(k_ref), core), 1e6)
    inside = spot(core, (CHIP, CHIP), 0) > spot(core, (CHIP, CHIP), 1)
    inside = jnp.concatenate([inside, inside], axis=1)
    seen = (after + stat_ref[0, 3:4, :] <= 1.5) & inside
    scores = jnp.where(seen, scores, HIDDEN)
    near_peak = stat_ref[0, 0:1, :]
    peak = jnp.maximum(near_peak, jnp.max(scores, axis=0, keepdims=True))
    shrink = jnp.exp(near_peak - peak)
    p = jnp.exp(scores - peak)
    mass = stat_ref[0, 1:2, :] * shrink + jnp.sum(p, axis=0, keepdims=True)
    moment = stat_ref[0, 2:3, :] * shrink + jnp.sum(p * dp, axis=0, keepdims=True)
    share = 1.0 / mass
    delta = moment * share
    p = p * share
    ds = p * (dp - delta)
    q_right = right(jnp.concatenate(q_parts, axis=0) * scale)
    d_right = right(jnp.concatenate(d_parts, axis=0))
    key_grad, value_grad, query_grad = gradients(p, ds, q_right, d_right, keys)
    gk_ref[...] = key_grad
    gv_ref[...] = value_grad
    dq_ref[0] = query_grad
    stat2_ref[0, 0:1, :] = shrink * share
    stat2_ref[0, 1:2, :] = delta


def back_kernel(width, own_ref, far_ref, *refs):
    k_refs, (p_ref, dp_ref, dq4_ref, stat2_ref) = refs[:REACH], refs[REACH : REACH + 4]
    gk_refs, gv_refs = refs[REACH + 4 : 2 * REACH + 4], refs[2 * REACH + 4 : 3 * REACH + 4]
    dq_own, dq_sib, sum_ref = refs[3 * REACH + 4 :]
    head = pl.program_id(0)
    scale = width ** (-0.5)
    q_right = right(jnp.concatenate(query_rows(own_ref, far_ref, 0, head), axis=0) * scale)
    d_right = right(jnp.concatenate(query_rows(own_ref, far_ref, 1, head), axis=0))
    share, delta = stat2_ref[0, 0:1, :], stat2_ref[0, 1:2, :]
    total = dq4_ref[0]
    for distance in reversed(range(REACH)):
        rows = pl.ds(distance * CHIP, CHIP)
        p = p_ref[0, rows, :] * share
        ds = p * (dp_ref[0, rows, :] - delta)
        key_grad, value_grad, query_grad = gradients(
            p, ds, q_right, d_right, k_refs[distance][pl.ds(head * CHIP, CHIP), :]
        )
        total = total + query_grad
        gk_refs[distance][...] = key_grad
        gv_refs[distance][...] = value_grad
    total = total * scale
    sum_ref[0] = jnp.broadcast_to(jnp.sum(total * total), (8, TOK))
    for mate in range(2):
        dq_own[mate] = total[:, (2 * mate) * TOK : (2 * mate + 1) * TOK].T
        dq_sib[mate] = total[:, (2 * mate + 1) * TOK : (2 * mate + 2) * TOK].T


def final_kernel(got_k, got_v, own_k, own_v, sum_ref, keep_ref, give_ref, row_ref):
    total = jnp.zeros((8, TOK), F32)
    for kind, (got, own) in enumerate(((got_k, own_k), (got_v, own_v))):
        for head in range(2):
            for half, out in ((0, keep_ref), (1, give_ref)):
                rows = pl.ds(head * CHIP + half * TOK, TOK)
                grad = got[rows, :] + own[rows, :]
                out[pl.ds((2 * kind + head) * TOK, TOK), :] = grad
                total = total + jnp.sum((grad * grad).reshape(TOK // 8, 8, TOK), axis=0)
    row = jnp.sum(total, axis=0, keepdims=True) + (sum_ref[0, 0:1, :] + sum_ref[1, 0:1, :]) * (1.0 / TOK)
    row_ref[...] = jnp.broadcast_to(row, row_ref.shape)


def place_q_kernel(core_ref, own_ref, far_ref, q_out):
    core = core_ref[0]
    for side in range(2):

        @pl.when(core == side)
        def _():
            for source, where in ((own_ref, side), (far_ref, 1 - side)):
                for head in range(4):
                    q_out[pl.ds(4 * where + head, TOK, stride=8), :] = source[head]


def place_kv_kernel(core_ref, own_ref, far_ref, k_out, v_out):
    core = core_ref[0]
    for side in range(2):

        @pl.when(core == side)
        def _():
            for source, where in ((own_ref, side), (far_ref, 1 - side)):
                for head in range(2):
                    k_out[pl.ds(2 * where + head, TOK, stride=4), :] = source[pl.ds(head * TOK, TOK), :]
                    v_out[pl.ds(2 * where + head, TOK, stride=4), :] = source[pl.ds((2 + head) * TOK, TOK), :]


def shards(sizes, queries, key_states, value_states, out_grad, step_begins):
    tokens, heads, width = queries.shape
    groups = key_states.shape[1]
    chips = sizes["x"] * sizes["yh"] * sizes["z"]
    plane = sizes["x"] * sizes["yh"] * sizes["core"] * sizes["yl"]
    chip = lax.axis_index(("x", "yh", "z")).astype(jnp.int32).reshape(1)
    core = lax.axis_index("core").astype(jnp.int32).reshape(1)

    def send(value, step, cross=0):
        pairs = [
            (c * 2 + k, (c + step) * 2 + (k ^ cross))
            for c in range(max(0, -step), min(chips, chips - step))
            for k in range(2)
        ]
        return lax.ppermute(value, CTX, pairs)

    half_rows = whole(4 * TOK + 8, width)
    qd = whole(2, 4, TOK, width)
    qd_own, qd_sib, kv_own, kv_sib = call(
        prep_kernel,
        (sds(2, 4, TOK, width), sds(2, 4, TOK, width), sds(4 * TOK + 8, width), sds(4 * TOK + 8, width)),
        [SCALAR] + [whole(tokens * heads, width)] * 2 + [whole(tokens * groups, width)] * 2 + [whole(1, tokens)],
        (qd, qd, half_rows, half_rows),
        moved=3 << 20,
    )(
        core,
        queries.reshape(tokens * heads, width),
        out_grad.reshape(tokens * heads, width),
        key_states.reshape(tokens * groups, width),
        value_states.reshape(tokens * groups, width),
        step_begins.reshape(1, tokens),
    )
    keys, body = whole(BODY + 8, width), whole(BODY, width)
    pack = call(
        pack_kernel,
        (sds(BODY + 8, width), sds(BODY, width)),
        [half_rows] * 2,
        (keys, body),
        moved=1 << 20,
    )
    first = pack(send(kv_own, 1), send(kv_sib, 1, 1))
    first, qd_sib, kv_sib = lax.optimization_barrier((first, qd_sib, kv_sib))
    blocks = [None, first]
    for _ in range(REACH - 1):
        blocks.append((send(blocks[-1][0], 1), send(blocks[-1][1], 1)))
    blocks[0] = pack(kv_own, send(kv_sib, 0, 1))
    qd_far = send(qd_sib, 0, 1)
    near_k = [block[0] for block in blocks[:REACH]]
    near_v = [block[1] for block in blocks[:REACH]]
    one = 2 * ROWS * CHIP * width
    p, dp, stat = call(
        functools.partial(near_kernel, width),
        (sds(2, REACH * CHIP, ROWS), sds(2, REACH * CHIP, ROWS), sds(2, 8, ROWS)),
        [SCALAR, SCALAR, qd, qd] + [keys] * REACH + [body] * REACH,
        (per_head(REACH * CHIP, ROWS), per_head(REACH * CHIP, ROWS), per_head(8, ROWS)),
        grid=(2,),
        flops=2 * 2 * REACH * 3 * one,
        moved=12 << 20,
        vmem=28,
    )(chip, core, qd_own, qd_far, *near_k, *near_v)
    part = pl.BlockSpec((CHIP, width), lambda h: (h, 0))
    grad_k, grad_v, dq4, stat2 = call(
        functools.partial(last_kernel, width),
        (sds(BODY, width), sds(BODY, width), sds(2, width, ROWS), sds(2, 8, ROWS)),
        [SCALAR, SCALAR, qd, qd, keys, body, per_head(8, ROWS)],
        (part, part, per_head(width, ROWS), per_head(8, ROWS)),
        grid=(2,),
        flops=2 * 5 * 3 * one,
        moved=3 << 20,
        vmem=20,
    )(chip, core, qd_own, qd_far, *blocks[REACH], stat)
    got_k, got_v = send(grad_k, -1), send(grad_v, -1)
    half = pl.BlockSpec((2, TOK, width), lambda h: (h, 0, 0))
    grads = call(
        functools.partial(back_kernel, width),
        (sds(BODY, width),) * (2 * REACH) + (sds(4, TOK, width), sds(4, TOK, width), sds(2, 8, TOK)),
        [qd, qd] + [keys] * REACH
        + [per_head(REACH * CHIP, ROWS)] * 2 + [per_head(width, ROWS), per_head(8, ROWS)],
        (part,) * (2 * REACH) + (half, half, per_head(8, TOK)),
        grid=(2,),
        flops=2 * 3 * REACH * 3 * one,
        moved=14 << 20,
        vmem=32,
    )(qd_own, qd_far, *near_k, p, dp, dq4, stat2)
    gk, gv = grads[:REACH], grads[REACH : 2 * REACH]
    dq_own, dq_sib, dq_sum = grads[2 * REACH :]
    dq_far = send(dq_sib, 0, 1)
    for distance in range(REACH - 1, 0, -1):
        got_k = send(got_k + gk[distance], -1)
        got_v = send(got_v + gv[distance], -1)
    dq = call(
        place_q_kernel,
        sds(tokens * heads, width),
        [SCALAR] + [whole(4, TOK, width)] * 2,
        whole(tokens * heads, width),
        moved=1 << 20,
    )(core, dq_own, dq_far)
    quarter = whole(4 * TOK, width)
    keep, give, row = call(
        final_kernel,
        (sds(4 * TOK, width), sds(4 * TOK, width), sds(plane, width)),
        [body] * 4 + [whole(2, 8, TOK)],
        (quarter, quarter, whole(plane, width)),
        moved=2 << 20,
    )(got_k, got_v, gk[0], gv[0], dq_sum)
    far = send(give, 0, 1)
    parts = lax.all_to_all(row.reshape(plane, 1, width), ("x", "yh", "core", "yl"), 0, 0)
    parts = jnp.broadcast_to(jnp.sum(parts, axis=0, keepdims=True), (sizes["z"], 1, width))
    parts = lax.all_to_all(parts, "z", 0, 0)
    entries = chips * sizes["core"] * sizes["yl"] * tokens * (heads + 2 * groups) * width
    grad_square = jnp.sum(parts) / entries
    dk, dv = call(
        place_kv_kernel,
        (sds(tokens * groups, width), sds(tokens * groups, width)),
        [SCALAR] + [quarter] * 2,
        (whole(tokens * groups, width), whole(tokens * groups, width)),
        moved=1 << 20,
    )(core, keep, far)
    return (
        dq.reshape(queries.shape),
        dk.reshape(key_states.shape),
        dv.reshape(value_states.shape),
        grad_square,
    )


def solution(mesh):
    sizes = {"z": 16, "core": 2, "yh": 2, "yl": mesh.shape["head"]}
    sizes["x"] = mesh.shape["ctx"] // (sizes["z"] * sizes["core"] * sizes["yh"])
    names = ("x", "yh", "z", "core", "yl")
    fine = Mesh(mesh.devices.reshape([sizes[name] for name in names]), names)
    rows = P(CTX, "yl", None)
    return jax.shard_map(
        functools.partial(shards, sizes),
        mesh=fine,
        in_specs=(rows, rows, rows, rows, P(CTX)),
        out_specs=(rows, rows, rows, P()),
        check_vma=False,
    )
```

time: 204 us -> 182 us (0.89)
  starting transfers between devices: 47.5 us -> 69.8 us
  blocking collectives: 61.1 us -> 39.5 us
  Pallas kernels: 31.7 us -> 16.1 us
  waiting for transfers between devices: 52.1 us -> 44 us
  local copies, waits for them, and re-layouts: 3.85 us -> 8.53 us
  other arithmetic: 3.94 us -> 0.82 us
    all_to_all x1 -> x0, blocking collectives: 19.1 us -> none  [shards(): parts = lax.all_to_all(parts, 'z', 0, 0)]
    ppermute x12 -> x20, waiting for transfers between devices: 52.1 us -> 33.7 us  [send(): return lax.ppermute(value, CTX, pairs)]
    ppermute x12 -> x20, starting transfers between devices: 47.5 us -> 61.8 us  [send(): return lax.ppermute(value, CTX, pairs)]
    all_to_all x0 -> x1, waiting for transfers between devices: none -> 10.3 us  [shards(): parts = lax.all_to_all(parts, 'z', 0, 0)]
    pallas_call x4 -> x6, Pallas kernels: 19.1 us -> 10.5 us  [the longest x1 4.92 us: shards(): call(functools.partial(back_kernel, width), (sds(BODY, width),) * (2 * RE...]
    all_to_all x0 -> x1, starting transfers between devices: none -> 7.96 us  [shards(): parts = lax.all_to_all(parts, 'z', 0, 0)]
    unnamed x20 -> x18, local copies, waits for them, and re-layouts: 3.84 us -> 7.92 us
    add x3 -> x6, other arithmetic: 3.29 us -> 0.17 us  [the longest x3 0.09 us: shards(): got_k = send(got_k + gk[distance], -1)]
  transfers between devices with their start and end apart: 12 -> 21, of which waited for: 8 -> 12; matrix products, arithmetic and copies ran while one was open for 0% -> 1% of each run, Pallas kernels for 10% -> 6%
where the time goes in v2:
time: 182 us; the launch traced here: 181 us
  starting transfers between devices  69.8 us (38%)
  waiting for transfers between devices  44 us (24%)
  blocking collectives  39.5 us (22%)
  Pallas kernels  16.1 us (9%)
  local copies, waits for them, and re-layouts  8.53 us (5%)
  between operations  2.73 us (2%)
    ppermute x20, starting transfers between devices, send(): return lax.ppermute(value, CTX, pairs)  61.8 us
    all_to_all x1, blocking collectives, shards(): lax.all_to_all(row.reshape(plane, 1, width), ('x', 'yh', 'core', 'yl'), 0...  39.5 us
    ppermute x20, waiting for transfers between devices, send(): return lax.ppermute(value, CTX, pairs)  33.7 us
    all_to_all x1, waiting for transfers between devices, shards(): parts = lax.all_to_all(parts, 'z', 0, 0)  10.3 us
    all_to_all x1, starting transfers between devices, shards(): parts = lax.all_to_all(parts, 'z', 0, 0)  7.96 us
    unnamed x18, local copies, waits for them, and re-layouts  7.92 us
    pallas_call x1, Pallas kernels, shards(): call(functools.partial(near_kernel, width), (sds(2, REACH * CHIP, ROWS),...  5.26 us
    pallas_call x1, Pallas kernels, shards(): call(functools.partial(back_kernel, width), (sds(BODY, width),) * (2 * RE...  4.92 us
  transfers between devices with their start and end apart: 21, of which 12 were waited for; matrix products, arithmetic and copies ran while one was open for 1% of the time, Pallas kernels for 6%

profile of v2, /device:TPU:1, one launch (start us, length us, event | category | flops | bytes accessed | tf_op | source)
XLA Modules:
  0.0 181.5 jit_solution(8135683029697473430)
XLA Ops:
  5.5 4.4 %collective-permute-start = (f32[520,128]{1,0:T(8,128)S(1)}, f32[520,128]{1,0:T(8,128)S(1)}, u32[]{:S(2)}, u32[]{:S(2)}) collective-permute-start(f32[520,128]{1,0:T(8,128)S(1)} %get-tuple-element.40.own_ref), channel_id=1, source_target_pairs={{0,4},{2,6},{4,8},{6,10},{8,12},{10,14},{12,16},{14,18},{16,20},{1... | collective-permute-start | bytes 798728 | tf_op jit(solution)/shard_map/ppermute | solution.py:300
  9.9 4.4 %collective-permute-start.1 = (f32[520,128]{1,0:T(8,128)S(1)}, f32[520,128]{1,0:T(8,128)S(1)}, u32[]{:S(2)}, u32[]{:S(2)}) collective-permute-start(f32[520,128]{1,0:T(8,128)S(1)} %get-tuple-element.46), channel_id=1, source_target_pairs={{0,6},{2,4},{4,10},{6,8},{8,14},{10,12},{12,18},{14,16},{16,22},{1... | collective-permute-start | bytes 798728 | tf_op jit(solution)/shard_map/ppermute | solution.py:300
  14.3 6.1 %collective-permute-done.1.far_ref = f32[520,128]{1,0:T(8,128)S(1)} collective-permute-done((f32[520,128]{1,0:T(8,128)S(1)}, f32[520,128]{1,0:T(8,128)S(1)}, u32[]{:S(2)}, u32[]{:S(2)}) %collective-permute-start.1) | collective-permute-done | bytes 266272 | tf_op jit(solution)/shard_map/ppermute | solution.py:300
  20.4 6.3 %collective-permute-start.4 = (f32[520,128]{1,0:T(8,128)S(1)}, f32[520,128]{1,0:T(8,128)S(1)}, u32[]{:S(2)}, u32[]{:S(2)}) collective-permute-start(f32[520,128]{1,0:T(8,128)S(1)} %get-tuple-element.48.refs_1_), channel_id=1, source_target_pairs={{0,4},{2,6},{4,8},{6,10},{8,12},{10,14},{12,16},{14,18},{16,20},{1... | collective-permute-start | bytes 798728 | tf_op jit(solution)/shard_map/ppermute | solution.py:300
  29.9 2.6 %collective-permute-start.2 = (f32[2,4,128,128]{3,2,1,0:T(8,128)S(1)}, f32[2,4,128,128]{3,2,1,0:T(8,128)S(1)}, u32[]{:S(2)}, u32[]{:S(2)}) collective-permute-start(f32[2,4,128,128]{3,2,1,0:T(8,128)S(1)} %get-tuple-element.45), channel_id=1, source_target_pairs={{0,2},{2,0},{4,6},{6,4},{8,10},{10,8},{12,14},{14,12},{16,18},{18,... | collective-permute-start | bytes 1572872 | tf_op jit(solution)/shard_map/ppermute | solution.py:300
  32.9 4.4 %collective-permute-start.5 = (f32[520,128]{1,0:T(8,128)S(1)}, f32[520,128]{1,0:T(8,128)S(1)}, u32[]{:S(2)}, u32[]{:S(2)}) collective-permute-start(f32[520,128]{1,0:T(8,128)S(1)} %collective-permute-done.4.refs_2_), channel_id=1, source_target_pairs={{0,4},{2,6},{4,8},{6,10},{8,12},{10,14},{12,16},{14,18},{16,20},{1... | collective-permute-start | bytes 798728 | tf_op jit(solution)/shard_map/ppermute | solution.py:300
  38.0 4.5 %collective-permute-start.7 = (f32[512,128]{1,0:T(8,128)S(1)}, f32[512,128]{1,0:T(8,128)}, u32[]{:S(2)}, u32[]{:S(2)}) collective-permute-start(f32[512,128]{1,0:T(8,128)S(1)} %collective-permute-done.6.refs_6_), channel_id=1, source_target_pairs={{0,4},{2,6},{4,8},{6,10},{8,12},{10,14},{12,16},{14,18},{16,20},{1... | collective-permute-start | bytes 786440 | tf_op jit(solution)/shard_map/ppermute | solution.py:300
  45.7 2.7 %collective-permute-start.8 = (f32[520,128]{1,0:T(8,128)S(1)}, f32[520,128]{1,0:T(8,128)S(1)}, u32[]{:S(2)}, u32[]{:S(2)}) collective-permute-start(f32[520,128]{1,0:T(8,128)S(1)} %collective-permute-done.5.refs_3_), channel_id=1, source_target_pairs={{0,4},{2,6},{4,8},{6,10},{8,12},{10,14},{12,16},{14,18},{16,20},{1... | collective-permute-start | bytes 798728 | tf_op jit(solution)/shard_map/ppermute | solution.py:300
  49.1 5.4 %collective-permute-start.9 = (f32[512,128]{1,0:T(8,128)}, f32[512,128]{1,0:T(8,128)}, u32[]{:S(2)}, u32[]{:S(2)}) collective-permute-start(f32[512,128]{1,0:T(8,128)} %collective-permute-done.7.refs_7_), channel_id=1, source_target_pairs={{0,4},{2,6},{4,8},{6,10},{8,12},{10,14},{12,16},{14,18},{16,20},{1... | collective-permute-start | bytes 786440 | tf_op jit(solution)/shard_map/ppermute | solution.py:300
  56.5 5.3 %shard_map.87 = (f32[2,1024,512]{2,1,0:T(8,128)S(1)}, f32[2,1024,512]{2,1,0:T(8,128)S(1)}, f32[2,8,512]{2,1,0:T(8,128)S(1)}) custom-call(s32[1]{0:T(128)} %bitcast.6.chip_ref, s32[1]{0:T(128)} %bitcast.core_ref, f32[2,4,128,128]{3,2,1,0:T(8,128)S(1)} %get-tuple-element.39.own_ref, f32[2,4,128,128]{3,2,1,0:T(8,128)S(1)} %collective-permute-done.2.far_ref, ...), custom_call_target="tpu_custom_call" | custom-call | flops 1610612736 | bytes 12582912 | tf_op jit(solution)/shard_map/pallas_call | solution.py:336
  61.8 3.7 %shard_map.88 = (f32[512,128]{1,0:T(8,128)S(1)}, f32[512,128]{1,0:T(8,128)S(1)}, f32[2,128,512]{2,1,0:T(8,128)S(1)}, f32[2,8,512]{2,1,0:T(8,128)S(1)}) custom-call(s32[1]{0:T(128)} %bitcast.6.chip_ref, s32[1]{0:T(128)} %bitcast.core_ref, f32[2,4,128,128]{3,2,1,0:T(8,128)S(1)} %get-tuple-element.39.own_ref, ...), custom_call_target="tpu_custom_call" | custom-call | flops 1006632960 | bytes 3145728 | tf_op jit(solution)/shard_map/pallas_call | solution.py:347
  68.1 4.9 %shard_map.89 = (f32[512,128]{1,0:T(8,128)S(1)}, f32[512,128]{1,0:T(8,128)S(1)}, f32[512,128]{1,0:T(8,128)S(1)}, f32[512,128]{1,0:T(8,128)S(1)}, f32[512,128]{1,...) custom-call(f32[2,4,128,128]{3,2,1,0:T(8,128)S(1)} %get-tuple-elemen, ...), custom_call_target="tpu_custom_call" | custom-call | flops 2415919104 | bytes 14680064 | tf_op jit(solution)/shard_map/pallas_call | solution.py:359
  73.0 3.3 %collective-permute-done.11 = f32[512,128]{1,0:T(8,128)S(1)} collective-permute-done((f32[512,128]{1,0:T(8,128)S(1)}, f32[512,128]{1,0:T(8,128)S(1)}, u32[]{:S(2)}, u32[]{:S(2)}) %collective-permute-start.11) | collective-permute-done | bytes 262176 | tf_op jit(solution)/shard_map/ppermute | solution.py:300
  77.6 4.3 %collective-permute-done.15 = f32[512,128]{1,0:T(8,128)S(1)} collective-permute-done((f32[512,128]{1,0:T(8,128)S(1)}, f32[512,128]{1,0:T(8,128)S(1)}, u32[]{:S(2)}, u32[]{:S(2)}) %collective-permute-start.15) | collective-permute-done | bytes 262176 | tf_op jit(solution)/shard_map/ppermute | solution.py:300
  83.3 3.5 %collective-permute-done.12 = f32[512,128]{1,0:T(8,128)S(1)} collective-permute-done((f32[512,128]{1,0:T(8,128)S(1)}, f32[512,128]{1,0:T(8,128)S(1)}, u32[]{:S(2)}, u32[]{:S(2)}) %collective-permute-start.12) | collective-permute-done | bytes 262176 | tf_op jit(solution)/shard_map/ppermute | solution.py:300
  88.1 4.3 %collective-permute-done.16 = f32[512,128]{1,0:T(8,128)S(1)} collective-permute-done((f32[512,128]{1,0:T(8,128)S(1)}, f32[512,128]{1,0:T(8,128)S(1)}, u32[]{:S(2)}, u32[]{:S(2)}) %collective-permute-start.16) | collective-permute-done | bytes 262176 | tf_op jit(solution)/shard_map/ppermute | solution.py:300
  93.7 3.8 %collective-permute-done.13 = f32[512,128]{1,0:T(8,128)S(1)} collective-permute-done((f32[512,128]{1,0:T(8,128)S(1)}, f32[512,128]{1,0:T(8,128)S(1)}, u32[]{:S(2)}, u32[]{:S(2)}) %collective-permute-start.13) | collective-permute-done | bytes 262176 | tf_op jit(solution)/shard_map/ppermute | solution.py:300
  98.8 4.1 %collective-permute-done.17 = f32[512,128]{1,0:T(8,128)S(1)} collective-permute-done((f32[512,128]{1,0:T(8,128)S(1)}, f32[512,128]{1,0:T(8,128)S(1)}, u32[]{:S(2)}, u32[]{:S(2)}) %collective-permute-start.17) | collective-permute-done | bytes 262176 | tf_op jit(solution)/shard_map/ppermute | solution.py:300
  104.2 6.3 %collective-permute-start.10 = (f32[4,128,128]{2,1,0:T(8,128)S(1)}, f32[4,128,128]{2,1,0:T(8,128)S(1)}, u32[]{:S(2)}, u32[]{:S(2)}) collective-permute-start(f32[4,128,128]{2,1,0:T(8,128)S(1)} %get-tuple-element.57), channel_id=1, source_target_pairs={{0,2},{2,0},{4,6},{6,4},{8,10},{10,8},{12,14},{14,12},{16,18},{18,... | collective-permute-start | bytes 786440 | tf_op jit(solution)/shard_map/ppermute | solution.py:300
  110.5 2.7 %collective-permute-done.18.got_v = f32[512,128]{1,0:T(8,128)S(1)} collective-permute-done((f32[512,128]{1,0:T(8,128)S(1)}, f32[512,128]{1,0:T(8,128)S(1)}, u32[]{:S(2)}, u32[]{:S(2)}) %collective-permute-start.18) | collective-permute-done | bytes 262176 | tf_op jit(solution)/shard_map/ppermute | solution.py:300
  113.3 5.5 %collective-permute-start.19 = (f32[512,128]{1,0:T(8,128)S(1)}, f32[512,128]{1,0:T(8,128)S(1)}, u32[]{:S(2)}, u32[]{:S(2)}) collective-permute-start(f32[512,128]{1,0:T(8,128)S(1)} %get-tuple-element.70), channel_id=1, source_target_pairs={{0,2},{2,0},{4,6},{6,4},{8,10},{10,8},{12,14},{14,12},{16,18},{18,... | collective-permute-start | bytes 786440 | tf_op jit(solution)/shard_map/ppermute | solution.py:300
  118.9 39.5 %all_to_all.10 = f32[32,1,128]{2,1,0:T(1,128)S(1)} all-to-all(f32[32,1,128]{2,1,0:T(1,128)S(1)} %bitcast.18), channel_id=1, replica_groups=mesh['x'=4,'yh'=2,'z'=16,'core'=2,'yl'=2] {'x','yh','core','yl'}, dimensions={0} | all-to-all | bytes 32768 | tf_op jit(solution)/shard_map/all_to_all | solution.py:392
  159.0 8.0 %all-to-all-start.1 = ((f32[16,1,128]{2,1,0:T(1,128)}), f32[16,1,128]{2,1,0:T(1,128)S(1)}, u32[]{:S(2)}, u32[]{:S(2)}) async-start(f32[16,1,128]{2,1,0:T(1,128)} %broadcast_in_dim.2), calls=%async_computation.1 | async-start | bytes 16384 | tf_op jit(solution)/shard_map/all_to_all | solution.py:394
  167.9 10.3 %all-to-all-done.1 = f32[16,1,128]{2,1,0:T(1,128)S(1)} async-done(((f32[16,1,128]{2,1,0:T(1,128)}), f32[16,1,128]{2,1,0:T(1,128)S(1)}, u32[]{:S(2)}, u32[]{:S(2)}) %all-to-all-start.1) | async-done | bytes 8224 | tf_op jit(solution)/shard_map/all_to_all | solution.py:394
  (55 shorter events, 28.5 us)
Async XLA Ops:
  0.6 1.0 copy-start
  1.7 1.0 copy-start.1
  5.5 8.8 %collective-permute-start = (f32[520,128]{1,0:T(8,128)S(1)}, f32[520,128]{1,0:T(8,128)S(1)}, u32[]{:S(2)}, u32[]{:S(2)}) collective-permute-start(f32[520,128]{1,0:T(8,128)S(1)} %get-tuple-element.40.own_ref), channel_id=1, source_target_pairs={{0,4},{2,6},{4,8},{6,10},{8,12},{10,14},{12,16},{14,18},{16,20},{1... | collective-permute-start | bytes 798728 | tf_op jit(solution)/shard_map/ppermute | solution.py:300
  9.9 10.5 %collective-permute-start.1 = (f32[520,128]{1,0:T(8,128)S(1)}, f32[520,128]{1,0:T(8,128)S(1)}, u32[]{:S(2)}, u32[]{:S(2)}) collective-permute-start(f32[520,128]{1,0:T(8,128)S(1)} %get-tuple-element.46), channel_id=1, source_target_pairs={{0,6},{2,4},{4,10},{6,8},{8,14},{10,12},{12,18},{14,16},{16,22},{1... | collective-permute-start | bytes 798728 | tf_op jit(solution)/shard_map/ppermute | solution.py:300
  20.4 12.5 %collective-permute-start.4 = (f32[520,128]{1,0:T(8,128)S(1)}, f32[520,128]{1,0:T(8,128)S(1)}, u32[]{:S(2)}, u32[]{:S(2)}) collective-permute-start(f32[520,128]{1,0:T(8,128)S(1)} %get-tuple-element.48.refs_1_), channel_id=1, source_target_pairs={{0,4},{2,6},{4,8},{6,10},{8,12},{10,14},{12,16},{14,18},{16,20},{1... | collective-permute-start | bytes 798728 | tf_op jit(solution)/shard_map/ppermute | solution.py:300
  26.8 11.3 %collective-permute-start.6 = (f32[512,128]{1,0:T(8,128)S(1)}, f32[512,128]{1,0:T(8,128)S(1)}, u32[]{:S(2)}, u32[]{:S(2)}) collective-permute-start(f32[512,128]{1,0:T(8,128)S(1)} %get-tuple-element.50.refs_5_), channel_id=1, source_target_pairs={{0,4},{2,6},{4,8},{6,10},{8,12},{10,14},{12,16},{14,18},{16,20},{1... | collective-permute-start | bytes 786440 | tf_op jit(solution)/shard_map/ppermute | solution.py:300
  29.9 24.6 %collective-permute-start.2 = (f32[2,4,128,128]{3,2,1,0:T(8,128)S(1)}, f32[2,4,128,128]{3,2,1,0:T(8,128)S(1)}, u32[]{:S(2)}, u32[]{:S(2)}) collective-permute-start(f32[2,4,128,128]{3,2,1,0:T(8,128)S(1)} %get-tuple-element.45), channel_id=1, source_target_pairs={{0,2},{2,0},{4,6},{6,4},{8,10},{10,8},{12,14},{14,12},{16,18},{18,... | collective-permute-start | bytes 1572872 | tf_op jit(solution)/shard_map/ppermute | solution.py:300
  32.9 12.8 %collective-permute-start.5 = (f32[520,128]{1,0:T(8,128)S(1)}, f32[520,128]{1,0:T(8,128)S(1)}, u32[]{:S(2)}, u32[]{:S(2)}) collective-permute-start(f32[520,128]{1,0:T(8,128)S(1)} %collective-permute-done.4.refs_2_), channel_id=1, source_target_pairs={{0,4},{2,6},{4,8},{6,10},{8,12},{10,14},{12,16},{14,18},{16,20},{1... | collective-permute-start | bytes 798728 | tf_op jit(solution)/shard_map/ppermute | solution.py:300
  38.0 11.1 %collective-permute-start.7 = (f32[512,128]{1,0:T(8,128)S(1)}, f32[512,128]{1,0:T(8,128)}, u32[]{:S(2)}, u32[]{:S(2)}) collective-permute-start(f32[512,128]{1,0:T(8,128)S(1)} %collective-permute-done.6.refs_6_), channel_id=1, source_target_pairs={{0,4},{2,6},{4,8},{6,10},{8,12},{10,14},{12,16},{14,18},{16,20},{1... | collective-permute-start | bytes 786440 | tf_op jit(solution)/shard_map/ppermute | solution.py:300
  43.2 11.3 %collective-permute-start.3 = (f32[520,128]{1,0:T(8,128)S(1)}, f32[520,128]{1,0:T(8,128)S(1)}, u32[]{:S(2)}, u32[]{:S(2)}) collective-permute-start(f32[520,128]{1,0:T(8,128)S(1)} %get-tuple-element.46), channel_id=1, source_target_pairs={{0,2},{2,0},{4,6},{6,4},{8,10},{10,8},{12,14},{14,12},{16,18},{18,... | collective-permute-start | bytes 798728 | tf_op jit(solution)/shard_map/ppermute | solution.py:300
  45.7 16.0 %collective-permute-start.8 = (f32[520,128]{1,0:T(8,128)S(1)}, f32[520,128]{1,0:T(8,128)S(1)}, u32[]{:S(2)}, u32[]{:S(2)}) collective-permute-start(f32[520,128]{1,0:T(8,128)S(1)} %collective-permute-done.5.refs_3_), channel_id=1, source_target_pairs={{0,4},{2,6},{4,8},{6,10},{8,12},{10,14},{12,16},{14,18},{16,20},{1... | collective-permute-start | bytes 798728 | tf_op jit(solution)/shard_map/ppermute | solution.py:300
  49.1 12.6 %collective-permute-start.9 = (f32[512,128]{1,0:T(8,128)}, f32[512,128]{1,0:T(8,128)}, u32[]{:S(2)}, u32[]{:S(2)}) collective-permute-start(f32[512,128]{1,0:T(8,128)} %collective-permute-done.7.refs_7_), channel_id=1, source_target_pairs={{0,4},{2,6},{4,8},{6,10},{8,12},{10,14},{12,16},{14,18},{16,20},{1... | collective-permute-start | bytes 786440 | tf_op jit(solution)/shard_map/ppermute | solution.py:300
  54.6 1.0 copy-start.6
  65.5 10.8 %collective-permute-start.11 = (f32[512,128]{1,0:T(8,128)S(1)}, f32[512,128]{1,0:T(8,128)S(1)}, u32[]{:S(2)}, u32[]{:S(2)}) collective-permute-start(f32[512,128]{1,0:T(8,128)S(1)} %get-tuple-element.58), channel_id=1, source_target_pairs={{4,0},{6,2},{8,4},{10,6},{12,8},{14,10},{16,12},{18,14},{20,16},{2... | collective-permute-start | bytes 786440 | tf_op jit(solution)/shard_map/ppermute | solution.py:300
  66.8 15.1 %collective-permute-start.15 = (f32[512,128]{1,0:T(8,128)S(1)}, f32[512,128]{1,0:T(8,128)S(1)}, u32[]{:S(2)}, u32[]{:S(2)}) collective-permute-start(f32[512,128]{1,0:T(8,128)S(1)} %get-tuple-element.62), channel_id=1, source_target_pairs={{4,0},{6,2},{8,4},{10,6},{12,8},{14,10},{16,12},{18,14},{20,16},{2... | collective-permute-start | bytes 786440 | tf_op jit(solution)/shard_map/ppermute | solution.py:300
  76.3 10.5 %collective-permute-start.12 = (f32[512,128]{1,0:T(8,128)S(1)}, f32[512,128]{1,0:T(8,128)S(1)}, u32[]{:S(2)}, u32[]{:S(2)}) collective-permute-start(f32[512,128]{1,0:T(8,128)S(1)} %add.26), channel_id=1, source_target_pairs={{4,0},{6,2},{8,4},{10,6},{12,8},{14,10},{16,12},{18,14},{20,16},{2... | collective-permute-start | bytes 786440 | tf_op jit(solution)/shard_map/ppermute | solution.py:300
  82.0 10.5 %collective-permute-start.16 = (f32[512,128]{1,0:T(8,128)S(1)}, f32[512,128]{1,0:T(8,128)S(1)}, u32[]{:S(2)}, u32[]{:S(2)}) collective-permute-start(f32[512,128]{1,0:T(8,128)S(1)} %add.29), channel_id=1, source_target_pairs={{4,0},{6,2},{8,4},{10,6},{12,8},{14,10},{16,12},{18,14},{20,16},{2... | collective-permute-start | bytes 786440 | tf_op jit(solution)/shard_map/ppermute | solution.py:300
  86.8 10.7 %collective-permute-start.13 = (f32[512,128]{1,0:T(8,128)S(1)}, f32[512,128]{1,0:T(8,128)S(1)}, u32[]{:S(2)}, u32[]{:S(2)}) collective-permute-start(f32[512,128]{1,0:T(8,128)S(1)} %add.27), channel_id=1, source_target_pairs={{4,0},{6,2},{8,4},{10,6},{12,8},{14,10},{16,12},{18,14},{20,16},{2... | collective-permute-start | bytes 786440 | tf_op jit(solution)/shard_map/ppermute | solution.py:300
  92.4 10.5 %collective-permute-start.17 = (f32[512,128]{1,0:T(8,128)S(1)}, f32[512,128]{1,0:T(8,128)S(1)}, u32[]{:S(2)}, u32[]{:S(2)}) collective-permute-start(f32[512,128]{1,0:T(8,128)S(1)} %add.30), channel_id=1, source_target_pairs={{4,0},{6,2},{8,4},{10,6},{12,8},{14,10},{16,12},{18,14},{20,16},{2... | collective-permute-start | bytes 786440 | tf_op jit(solution)/shard_map/ppermute | solution.py:300
  97.5 13.0 %collective-permute-start.14 = (f32[512,128]{1,0:T(8,128)S(1)}, f32[512,128]{1,0:T(8,128)S(1)}, u32[]{:S(2)}, u32[]{:S(2)}) collective-permute-start(f32[512,128]{1,0:T(8,128)S(1)} %add.28), channel_id=1, source_target_pairs={{4,0},{6,2},{8,4},{10,6},{12,8},{14,10},{16,12},{18,14},{20,16},{2... | collective-permute-start | bytes 786440 | tf_op jit(solution)/shard_map/ppermute | solution.py:300
  102.9 10.3 %collective-permute-start.18 = (f32[512,128]{1,0:T(8,128)S(1)}, f32[512,128]{1,0:T(8,128)S(1)}, u32[]{:S(2)}, u32[]{:S(2)}) collective-permute-start(f32[512,128]{1,0:T(8,128)S(1)} %add.31), channel_id=1, source_target_pairs={{4,0},{6,2},{8,4},{10,6},{12,8},{14,10},{16,12},{18,14},{20,16},{2... | collective-permute-start | bytes 786440 | tf_op jit(solution)/shard_map/ppermute | solution.py:300
  104.2 62.8 %collective-permute-start.10 = (f32[4,128,128]{2,1,0:T(8,128)S(1)}, f32[4,128,128]{2,1,0:T(8,128)S(1)}, u32[]{:S(2)}, u32[]{:S(2)}) collective-permute-start(f32[4,128,128]{2,1,0:T(8,128)S(1)} %get-tuple-element.57), channel_id=1, source_target_pairs={{0,2},{2,0},{4,6},{6,4},{8,10},{10,8},{12,14},{14,12},{16,18},{18,... | collective-permute-start | bytes 786440 | tf_op jit(solution)/shard_map/ppermute | solution.py:300
  113.3 66.1 %collective-permute-start.19 = (f32[512,128]{1,0:T(8,128)S(1)}, f32[512,128]{1,0:T(8,128)S(1)}, u32[]{:S(2)}, u32[]{:S(2)}) collective-permute-start(f32[512,128]{1,0:T(8,128)S(1)} %get-tuple-element.70), channel_id=1, source_target_pairs={{0,2},{2,0},{4,6},{6,4},{8,10},{10,8},{12,14},{14,12},{16,18},{18,... | collective-permute-start | bytes 786440 | tf_op jit(solution)/shard_map/ppermute | solution.py:300
  159.0 19.2 %all-to-all-start.1 = ((f32[16,1,128]{2,1,0:T(1,128)}), f32[16,1,128]{2,1,0:T(1,128)S(1)}, u32[]{:S(2)}, u32[]{:S(2)}) async-start(f32[16,1,128]{2,1,0:T(1,128)} %broadcast_in_dim.2), calls=%async_computation.1 | async-start | bytes 16384 | tf_op jit(solution)/shard_map/all_to_all | solution.py:394
  (6 other events, 4.9 us)

commit v3 on v2

v3 whole, which is shorter than its diff:
```python
import functools

import jax
import jax.numpy as jnp
from jax import lax
from jax.experimental import pallas as pl
from jax.experimental.pallas import tpu as pltpu
from jax.sharding import Mesh
from jax.sharding import PartitionSpec as P

HIDDEN = -1e30
TOK = 128
CHIP = 2 * TOK
REACH = 4
ROWS = 2 * CHIP
BODY = 2 * CHIP
F32, BF16 = jnp.float32, jnp.bfloat16
CTX = ("x", "yh", "z", "core")


def call(kernel, out_shape, in_specs, out_specs, grid=(1,), flops=0, moved=0, vmem=12, scratch=()):
    return pl.pallas_call(
        kernel,
        out_shape=out_shape,
        grid=grid,
        in_specs=in_specs,
        out_specs=out_specs,
        scratch_shapes=scratch,
        compiler_params=pltpu.CompilerParams(vmem_limit_bytes=vmem << 20),
        cost_estimate=pl.CostEstimate(flops=flops, bytes_accessed=moved, transcendentals=0),
    )


def whole(*shape):
    return pl.BlockSpec(shape, lambda *_: (0,) * len(shape))


SCALAR = pl.BlockSpec(memory_space=pltpu.SMEM)
FAR = pl.BlockSpec(memory_space=pltpu.HBM)


def sds(*shape):
    return jax.ShapeDtypeStruct(shape, F32)


def split(x):
    high = x.astype(BF16)
    return high, (x - high.astype(F32)).astype(BF16)


def left(x, axis):
    high, low = split(x)
    return jnp.concatenate([high, low, high], axis=axis)


def right(x):
    high, low = split(x)
    return jnp.concatenate([high, high, low], axis=0)


def mm(a, b):
    return jnp.dot(a, b, preferred_element_type=F32)


def spot(core, shape, axis):
    slot = lax.broadcasted_iota(jnp.int32, shape, axis)
    half = jnp.where(slot >= TOK, 1, 0)
    half = jnp.where(core == 0, half, 1 - half)
    return half * TOK + (slot & (TOK - 1))


def begins_row(block_ref):
    return jnp.concatenate([block_ref[BODY : BODY + 1, :], block_ref[BODY + 1 : BODY + 2, :]], axis=1)


def begun_after(row, core):
    later = spot(core, (CHIP, CHIP), 1) > spot(core, (CHIP, CHIP), 0)
    return jnp.sum(jnp.where(later, row, 0.0), axis=1, keepdims=True)


def fetch(sources, targets, sems):
    copies = [pltpu.make_async_copy(a, b, sems.at[i]) for i, (a, b) in enumerate(zip(sources, targets))]
    for copy in copies:
        copy.start()
    for copy in copies:
        copy.wait()


def prep_kv_kernel(core_ref, k_hbm, v_hbm, b_hbm, own_ref, sib_ref, k_ref, v_ref, b_ref, sems):
    fetch((k_hbm, v_hbm, b_hbm), (k_ref, v_ref, b_ref), sems)
    core = core_ref[0]
    for side in range(2):

        @pl.when(core == side)
        def _():
            for kind, source in enumerate((k_ref, v_ref)):
                for head in range(2):
                    rows = pl.ds((2 * head + kind) * TOK, TOK)
                    own_ref[rows, :] = source[pl.ds(2 * side + head, TOK, stride=4), :]
                    sib_ref[rows, :] = source[pl.ds(2 * (1 - side) + head, TOK, stride=4), :]

    row = lax.broadcasted_iota(jnp.int32, (8, TOK), 0)
    begins = jnp.where(row == 0, jnp.where(b_ref[...] > 0, 1.0, 0.0), 0.0)
    own_ref[4 * TOK :, :] = begins
    sib_ref[4 * TOK :, :] = begins


def prep_q_kernel(core_ref, q_hbm, d_hbm, own_ref, sib_ref, q_ref, d_ref, sems):
    fetch((q_hbm, d_hbm), (q_ref, d_ref), sems)
    core = core_ref[0]
    for side in range(2):

        @pl.when(core == side)
        def _():
            for kind, source in enumerate((q_ref, d_ref)):
                for head in range(4):
                    own_ref[kind, head] = source[pl.ds(4 * side + head, TOK, stride=8), :]
                    sib_ref[kind, head] = source[pl.ds(4 * (1 - side) + head, TOK, stride=8), :]


def pack_kernel(own_ref, far_ref, *outs):
    row = lax.broadcasted_iota(jnp.int32, (8, TOK), 0)
    first, second = (source[4 * TOK : 4 * TOK + 1, :] for source in (own_ref, far_ref))
    begins = jnp.where(row == 0, first, jnp.where(row == 1, second, 0.0))
    for head, out in enumerate(outs):
        for kind in range(2):
            for half, source in enumerate((own_ref, far_ref)):
                out[pl.ds(kind * CHIP + half * TOK, TOK), :] = source[pl.ds((2 * head + kind) * TOK, TOK), :]
        out[BODY:, :] = begins


def query_rows(own_ref, far_ref, kind, head):
    parts = []
    for mate in range(2):
        parts += [own_ref[kind, 2 * head + mate], far_ref[kind, 2 * head + mate]]
    return parts


def across(parts):
    return jnp.concatenate([part.T for part in parts], axis=1)


def near_kernel(head, width, chip_ref, core_ref, own_ref, far_ref, *refs):
    blocks, (p_ref, dp_ref, stat_ref) = refs[:REACH], refs[REACH:]
    chip, core = chip_ref[0], core_ref[0]
    scale = width ** (-0.5)
    queries = right(across(query_rows(own_ref, far_ref, 0, head)) * scale)
    cotangent = right(across(query_rows(own_ref, far_ref, 1, head)))
    place_row = spot(core, (CHIP, CHIP), 1)
    place_col = spot(core, (CHIP, CHIP), 0)
    row0 = begins_row(blocks[0])
    so_far = mm(
        jnp.broadcast_to(row0, (8, CHIP)).astype(BF16),
        jnp.where(place_col <= place_row, 1.0, 0.0).astype(BF16),
    )[0:1, :]
    so_far = jnp.concatenate([so_far, so_far], axis=1)
    causal = place_col <= place_row
    causal = jnp.concatenate([causal, causal], axis=1)
    between = so_far - jnp.sum(row0, axis=1, keepdims=True)
    peak = None
    for distance, block in enumerate(blocks):
        row = begins_row(block)
        after = begun_after(row, core)
        if distance:
            after = jnp.where(chip >= distance, after, 1e6)
        if distance == 1:
            between = so_far
        elif distance > 1:
            between = between + total
        total = jnp.sum(row, axis=1, keepdims=True)
        scores = mm(left(block[:CHIP, :], 1), queries)
        seen = after + between <= 1.5
        if distance == 0:
            seen = seen & causal
        scores = jnp.where(seen, scores, HIDDEN)
        rows = pl.ds(distance * CHIP, CHIP)
        p_ref[rows, :] = scores
        top = jnp.max(scores, axis=0, keepdims=True)
        peak = top if peak is None else jnp.maximum(peak, top)
        dp_ref[rows, :] = mm(left(block[CHIP:BODY, :], 1), cotangent)
    mass = jnp.zeros_like(peak)
    moment = jnp.zeros_like(peak)
    for distance in range(REACH):
        rows = pl.ds(distance * CHIP, CHIP)
        p = jnp.exp(p_ref[rows, :] - peak)
        p_ref[rows, :] = p
        mass = mass + jnp.sum(p, axis=0, keepdims=True)
        moment = moment + jnp.sum(p * dp_ref[rows, :], axis=0, keepdims=True)
    stat_ref[0:1, :] = peak
    stat_ref[1:2, :] = mass
    stat_ref[2:3, :] = moment
    stat_ref[3:4, :] = between + total


def gradients(p, ds, q_right, d_right, keys):
    k_high, k_low = split(keys.T)
    keys_left = jnp.concatenate([k_high, k_low, k_high], axis=1)
    ds_high, ds_low = split(ds)
    value_grad = mm(left(p, 1), d_right)
    key_grad = mm(jnp.concatenate([ds_high, ds_low, ds_high], axis=1), q_right)
    query_grad = mm(keys_left, jnp.concatenate([ds_high, ds_high, ds_low], axis=0))
    return key_grad, value_grad, query_grad


def last_kernel(head, width, chip_ref, core_ref, own_ref, far_ref, block, stat_ref, out_ref, dq_ref, stat2_ref):
    chip, core = chip_ref[0], core_ref[0]
    scale = width ** (-0.5)
    q_parts = query_rows(own_ref, far_ref, 0, head)
    d_parts = query_rows(own_ref, far_ref, 1, head)
    keys = block[:CHIP, :]
    scores = mm(left(keys, 1), right(across(q_parts) * scale))
    dp = mm(left(block[CHIP:BODY, :], 1), right(across(d_parts)))
    after = jnp.where(chip >= REACH, begun_after(begins_row(block), core), 1e6)
    inside = spot(core, (CHIP, CHIP), 0) > spot(core, (CHIP, CHIP), 1)
    inside = jnp.concatenate([inside, inside], axis=1)
    seen = (after + stat_ref[3:4, :] <= 1.5) & inside
    scores = jnp.where(seen, scores, HIDDEN)
    near_peak = stat_ref[0:1, :]
    peak = jnp.maximum(near_peak, jnp.max(scores, axis=0, keepdims=True))
    shrink = jnp.exp(near_peak - peak)
    p = jnp.exp(scores - peak)
    mass = stat_ref[1:2, :] * shrink + jnp.sum(p, axis=0, keepdims=True)
    moment = stat_ref[2:3, :] * shrink + jnp.sum(p * dp, axis=0, keepdims=True)
    share = 1.0 / mass
    delta = moment * share
    p = p * share
    ds = p * (dp - delta)
    q_right = right(jnp.concatenate(q_parts, axis=0) * scale)
    d_right = right(jnp.concatenate(d_parts, axis=0))
    key_grad, value_grad, query_grad = gradients(p, ds, q_right, d_right, keys)
    out_ref[:CHIP, :] = key_grad
    out_ref[CHIP:, :] = value_grad
    dq_ref[...] = query_grad
    stat2_ref[0:1, :] = shrink * share
    stat2_ref[1:2, :] = delta


def back_kernel(head, width, own_ref, far_ref, *refs):
    blocks, (p_ref, dp_ref, dq4_ref, stat2_ref) = refs[:REACH], refs[REACH : REACH + 4]
    grads, (dq_own, dq_sib, sum_ref) = refs[REACH + 4 : 2 * REACH + 4], refs[2 * REACH + 4 :]
    scale = width ** (-0.5)
    q_right = right(jnp.concatenate(query_rows(own_ref, far_ref, 0, head), axis=0) * scale)
    d_right = right(jnp.concatenate(query_rows(own_ref, far_ref, 1, head), axis=0))
    share, delta = stat2_ref[0:1, :], stat2_ref[1:2, :]
    total = dq4_ref[...]
    for distance in reversed(range(REACH)):
        rows = pl.ds(distance * CHIP, CHIP)
        p = p_ref[rows, :] * share
        ds = p * (dp_ref[rows, :] - delta)
        key_grad, value_grad, query_grad = gradients(
            p, ds, q_right, d_right, blocks[distance][:CHIP, :]
        )
        total = total + query_grad
        grads[distance][:CHIP, :] = key_grad
        grads[distance][CHIP:, :] = value_grad
    total = total * scale
    sum_ref[...] = jnp.broadcast_to(jnp.sum(total * total), (8, TOK))
    for mate in range(2):
        dq_own[mate] = total[:, (2 * mate) * TOK : (2 * mate + 1) * TOK].T
        dq_sib[mate] = total[:, (2 * mate + 1) * TOK : (2 * mate + 2) * TOK].T


def finish(got, own, keep_ref, give_ref, squares):
    total = jnp.zeros((8, TOK), F32)
    for kind in range(2):
        for half, out in ((0, keep_ref), (1, give_ref)):
            rows = pl.ds(kind * CHIP + half * TOK, TOK)
            grad = got[rows, :] + own[rows, :]
            out[pl.ds(kind * TOK, TOK), :] = grad
            total = total + jnp.sum((grad * grad).reshape(TOK // 8, 8, TOK), axis=0)
    return jnp.sum(total, axis=0, keepdims=True) + squares[0:1, :] * (1.0 / TOK)


def first_end_kernel(core_ref, got, own, squares, dq_own, dq_far, keep_ref, give_ref, row_ref, q_out):
    row_ref[...] = jnp.broadcast_to(finish(got, own, keep_ref, give_ref, squares), row_ref.shape)
    place_q(core_ref, dq_own, dq_far, q_out)


def second_end_kernel(got, own, squares, before, keep_ref, give_ref, row_ref):
    row = finish(got, own, keep_ref, give_ref, squares) + before[0:1, :]
    row_ref[...] = jnp.broadcast_to(row, row_ref.shape)


def place_q(core_ref, own_ref, far_ref, q_out):
    core = core_ref[0]
    for side in range(2):

        @pl.when(core == side)
        def _():
            for source, where in ((own_ref, side), (far_ref, 1 - side)):
                for head in range(4):
                    q_out[pl.ds(4 * where + head, TOK, stride=8), :] = source[head]


def place_kv_kernel(core_ref, own0, own1, far0, far1, k_out, v_out):
    core = core_ref[0]
    for side in range(2):

        @pl.when(core == side)
        def _():
            for sources, where in (((own0, own1), side), ((far0, far1), 1 - side)):
                for head, source in enumerate(sources):
                    for kind, out in enumerate((k_out, v_out)):
                        out[pl.ds(2 * where + head, TOK, stride=4), :] = source[pl.ds(kind * TOK, TOK), :]


def shards(sizes, queries, key_states, value_states, out_grad, step_begins):
    tokens, heads, width = queries.shape
    groups = key_states.shape[1]
    chips = sizes["x"] * sizes["yh"] * sizes["z"]
    plane = sizes["x"] * sizes["yh"] * sizes["core"] * sizes["yl"]
    chip = lax.axis_index(("x", "yh", "z")).astype(jnp.int32).reshape(1)
    core = lax.axis_index("core").astype(jnp.int32).reshape(1)

    def send(value, step, cross=0):
        pairs = [
            (c * 2 + k, (c + step) * 2 + (k ^ cross))
            for c in range(max(0, -step), min(chips, chips - step))
            for k in range(2)
        ]
        return lax.ppermute(value, CTX, pairs)

    half_rows = whole(4 * TOK + 8, width)
    qd = whole(2, 4, TOK, width)
    kv_own, kv_sib = call(
        prep_kv_kernel,
        (sds(4 * TOK + 8, width), sds(4 * TOK + 8, width)),
        [SCALAR, FAR, FAR, FAR],
        (half_rows, half_rows),
        moved=1 << 20,
        vmem=56,
        scratch=[pltpu.VMEM((tokens * groups, width), F32)] * 2
        + [pltpu.VMEM((1, tokens), jnp.int32), pltpu.SemaphoreType.DMA((3,))],
    )(
        core,
        key_states.reshape(tokens * groups, width),
        value_states.reshape(tokens * groups, width),
        step_begins.reshape(1, tokens),
    )
    qd_own, qd_sib = call(
        prep_q_kernel,
        (sds(2, 4, TOK, width), sds(2, 4, TOK, width)),
        [SCALAR, FAR, FAR],
        (qd, qd),
        moved=2 << 20,
        scratch=[pltpu.VMEM((tokens * heads, width), F32)] * 2 + [pltpu.SemaphoreType.DMA((2,))],
    )(core, queries.reshape(tokens * heads, width), out_grad.reshape(tokens * heads, width))
    block, body = whole(BODY + 8, width), whole(BODY, width)
    pack = call(pack_kernel, (sds(BODY + 8, width),) * 2, [half_rows] * 2, (block, block), moved=1 << 20)
    first = pack(send(kv_own, 1), send(kv_sib, 1, 1))
    first, qd_sib, kv_sib = lax.optimization_barrier((first, qd_sib, kv_sib))
    rings = [[None, first[0]], [None, first[1]]]
    for _ in range(REACH - 1):
        for ring in rings:
            ring.append(send(ring[-1], 1))
    rings[0][0], rings[1][0] = pack(kv_own, send(kv_sib, 0, 1))
    qd_far = send(qd_sib, 0, 1)
    one = 2 * ROWS * CHIP * width
    sheet, stats, turned = whole(REACH * CHIP, ROWS), whole(8, ROWS), whole(width, ROWS)
    pair = whole(2, TOK, width)
    got, grads, rest = [], [], []
    for head, ring in enumerate(rings):
        p, dp, stat = call(
            functools.partial(near_kernel, head, width),
            (sds(REACH * CHIP, ROWS), sds(REACH * CHIP, ROWS), sds(8, ROWS)),
            [SCALAR, SCALAR, qd, qd] + [block] * REACH,
            (sheet, sheet, stats),
            flops=2 * REACH * 3 * one,
            moved=6 << 20,
            vmem=16,
        )(chip, core, qd_own, qd_far, *ring[:REACH])
        grad, dq4, stat2 = call(
            functools.partial(last_kernel, head, width),
            (sds(BODY, width), sds(width, ROWS), sds(8, ROWS)),
            [SCALAR, SCALAR, qd, qd, block, stats],
            (body, turned, stats),
            flops=5 * 3 * one,
            moved=2 << 20,
        )(chip, core, qd_own, qd_far, ring[REACH], stat)
        got.append(send(grad, -1))
        out = call(
            functools.partial(back_kernel, head, width),
            (sds(BODY, width),) * REACH + (sds(2, TOK, width), sds(2, TOK, width), sds(8, TOK)),
            [qd, qd] + [block] * REACH + [sheet, sheet, turned, stats],
            (body,) * REACH + (pair, pair, whole(8, TOK)),
            flops=3 * REACH * 3 * one,
            moved=7 << 20,
            vmem=20,
        )(qd_own, qd_far, *ring[:REACH], p, dp, dq4, stat2)
        grads.append(out[:REACH])
        rest.append(out[REACH:])
    dq_own = jnp.concatenate([rest[0][0], rest[1][0]], axis=0)
    dq_far = send(jnp.concatenate([rest[0][1], rest[1][1]], axis=0), 0, 1)
    for distance in range(REACH - 1, 0, -1):
        got = [send(far + own[distance], -1) for far, own in zip(got, grads)]
    slot = whole(CHIP, width)
    keep0, give0, row, dq = call(
        first_end_kernel,
        (sds(CHIP, width), sds(CHIP, width), sds(8, width), sds(tokens * heads, width)),
        [SCALAR, body, body, whole(8, TOK)] + [whole(4, TOK, width)] * 2,
        (slot, slot, whole(8, width), whole(tokens * heads, width)),
        moved=2 << 20,
    )(core, got[0], grads[0][0], rest[0][2], dq_own, dq_far)
    far0 = send(give0, 0, 1)
    keep1, give1, row = call(
        second_end_kernel,
        (sds(CHIP, width), sds(CHIP, width), sds(plane, width)),
        [body, body, whole(8, TOK), whole(8, width)],
        (slot, slot, whole(plane, width)),
        moved=1 << 20,
    )(got[1], grads[1][0], rest[1][2], row)
    far1 = send(give1, 0, 1)
    parts = lax.all_to_all(row.reshape(plane, 1, width), ("x", "yh", "core", "yl"), 0, 0)
    parts = jnp.broadcast_to(jnp.sum(parts, axis=0, keepdims=True), (sizes["z"], 1, width))
    dk, dv = call(
        place_kv_kernel,
        (sds(tokens * groups, width), sds(tokens * groups, width)),
        [SCALAR] + [slot] * 4,
        (whole(tokens * groups, width), whole(tokens * groups, width)),
        moved=1 << 20,
    )(core, keep0, keep1, far0, far1)
    parts, dk, dv = lax.optimization_barrier((parts, dk, dv))
    parts = lax.all_to_all(parts, "z", 0, 0)
    entries = chips * sizes["core"] * sizes["yl"] * tokens * (heads + 2 * groups) * width
    grad_square = jnp.sum(parts) / entries
    return (
        dq.reshape(queries.shape),
        dk.reshape(key_states.shape),
        dv.reshape(value_states.shape),
        grad_square,
    )


def solution(mesh):
    sizes = {"z": 16, "core": 2, "yh": 2, "yl": mesh.shape["head"]}
    sizes["x"] = mesh.shape["ctx"] // (sizes["z"] * sizes["core"] * sizes["yh"])
    names = ("x", "yh", "z", "core", "yl")
    fine = Mesh(mesh.devices.reshape([sizes[name] for name in names]), names)
    rows = P(CTX, "yl", None)
    return jax.shard_map(
        functools.partial(shards, sizes),
        mesh=fine,
        in_specs=(rows, rows, rows, rows, P(CTX)),
        out_specs=(rows, rows, rows, P()),
        check_vma=False,
    )
```

time: 182 us -> 173 us (0.951)
  blocking collectives: 39.5 us -> 54.6 us
  starting transfers between devices: 69.8 us -> 58.9 us
  waiting for transfers between devices: 44 us -> 33.8 us
  local copies, waits for them, and re-layouts: 8.53 us -> 3.04 us
  Pallas kernels: 16.1 us -> 18.2 us
    all_to_all x0 -> x1, blocking collectives: none -> 17.5 us  [shards(): parts = lax.all_to_all(parts, 'z', 0, 0)]
    all_to_all x1 -> x0, waiting for transfers between devices: 10.3 us -> none  [shards(): parts = lax.all_to_all(parts, 'z', 0, 0)]
    all_to_all x1 -> x0, starting transfers between devices: 7.96 us -> none  [shards(): parts = lax.all_to_all(parts, 'z', 0, 0)]
    unnamed x18 -> x6, local copies, waits for them, and re-layouts: 7.92 us -> 3.03 us
    ppermute x20 -> x21, starting transfers between devices: 61.8 us -> 58.9 us  [send(): return lax.ppermute(value, CTX, pairs)]
    all_to_all x1, blocking collectives: 39.5 us -> 37.1 us  [shards(): lax.all_to_all(row.reshape(plane, 1, width), ('x', 'yh', 'core', 'yl'), 0...]
    pallas_call x7 -> x11, Pallas kernels: 15.2 us -> 17.3 us  [the longest x2 5.08 us: shards(): call(functools.partial(back_kernel, head, width), (sds(BODY, width),) * R...]
    ppermute x20 -> x21, waiting for transfers between devices: 33.7 us -> 33.8 us  [send(): return lax.ppermute(value, CTX, pairs)]
  transfers between devices with their start and end apart: 21 -> 21, of which waited for: 12 -> 11; matrix products, arithmetic and copies ran while one was open for 1% -> 0% of each run, Pallas kernels for 6% -> 9%
where the time goes in v3:
time: 173 us; the launch traced here: 172 us
  starting transfers between devices  58.9 us (34%)
  blocking collectives  54.6 us (32%)
  waiting for transfers between devices  33.8 us (20%)
  Pallas kernels  18.2 us (11%)
  local copies, waits for them, and re-layouts  3.04 us (2%)
  between operations  2.71 us (2%)
    ppermute x21, starting transfers between devices, send(): return lax.ppermute(value, CTX, pairs)  58.9 us
    all_to_all x1, blocking collectives, shards(): lax.all_to_all(row.reshape(plane, 1, width), ('x', 'yh', 'core', 'yl'), 0...  37.1 us
    ppermute x21, waiting for transfers between devices, send(): return lax.ppermute(value, CTX, pairs)  33.8 us
    all_to_all x1, blocking collectives, shards(): parts = lax.all_to_all(parts, 'z', 0, 0)  17.5 us
    pallas_call x2, Pallas kernels, shards(): call(functools.partial(back_kernel, head, width), (sds(BODY, width),) * R...  5.08 us
    pallas_call x2, Pallas kernels, shards(): call(functools.partial(last_kernel, head, width), (sds(BODY, width), sds(...  4.65 us
    pallas_call x2, Pallas kernels, shards(): call(functools.partial(near_kernel, head, width), (sds(REACH * CHIP, ROWS...  4.33 us
  transfers between devices with their start and end apart: 21, of which 11 were waited for; matrix products, arithmetic and copies ran while one was open for 0% of the time, Pallas kernels for 9%

profile of v3, /device:TPU:1, one launch (start us, length us, event | category | flops | bytes accessed | tf_op | source)
XLA Modules:
  0.0 172.1 jit_solution(6202237053006800351)
XLA Ops:
  2.5 4.4 %collective-permute-start = (f32[520,128]{1,0:T(8,128)}, f32[520,128]{1,0:T(8,128)S(1)}, u32[]{:S(2)}, u32[]{:S(2)}) collective-permute-start(f32[520,128]{1,0:T(8,128)} %get-tuple-element.55.own_ref), channel_id=1, source_target_pairs={{0,4},{2,6},{4,8},{6,10},{8,12},{10,14},{12,16},{14,18},{16,20},{1... | collective-permute-start | bytes 798728 | tf_op jit(solution)/shard_map/ppermute | solution.py:321
  6.9 4.4 %collective-permute-start.1 = (f32[520,128]{1,0:T(8,128)}, f32[520,128]{1,0:T(8,128)S(1)}, u32[]{:S(2)}, u32[]{:S(2)}) collective-permute-start(f32[520,128]{1,0:T(8,128)} %get-tuple-element.62), channel_id=1, source_target_pairs={{0,6},{2,4},{4,10},{6,8},{8,14},{10,12},{12,18},{14,16},{16,22},{1... | collective-permute-start | bytes 798728 | tf_op jit(solution)/shard_map/ppermute | solution.py:321
  13.7 4.0 %collective-permute-done.1.far_ref = f32[520,128]{1,0:T(8,128)S(1)} collective-permute-done((f32[520,128]{1,0:T(8,128)}, f32[520,128]{1,0:T(8,128)S(1)}, u32[]{:S(2)}, u32[]{:S(2)}) %collective-permute-start.1) | collective-permute-done | bytes 266272 | tf_op jit(solution)/shard_map/ppermute | solution.py:321
  17.8 6.2 %collective-permute-start.3 = (f32[520,128]{1,0:T(8,128)S(1)}, f32[520,128]{1,0:T(8,128)S(1)}, u32[]{:S(2)}, u32[]{:S(2)}) collective-permute-start(f32[520,128]{1,0:T(8,128)S(1)} %get-tuple-element.61.refs_1_), channel_id=1, source_target_pairs={{0,4},{2,6},{4,8},{6,10},{8,12},{10,14},{12,16},{14,18},{16,20},{1... | collective-permute-start | bytes 798728 | tf_op jit(solution)/shard_map/ppermute | solution.py:321
  24.0 2.4 %collective-permute-start.11 = (f32[520,128]{1,0:T(8,128)S(1)}, f32[520,128]{1,0:T(8,128)S(1)}, u32[]{:S(2)}, u32[]{:S(2)}) collective-permute-start(f32[520,128]{1,0:T(8,128)S(1)} %get-tuple-element.77.refs_1_), channel_id=1, source_target_pairs={{0,4},{2,6},{4,8},{6,10},{8,12},{10,14},{12,16},{14,18},{16,20},{1... | collective-permute-start | bytes 798728 | tf_op jit(solution)/shard_map/ppermute | solution.py:321
  26.4 2.7 %collective-permute-start.2 = (f32[2,4,128,128]{3,2,1,0:T(8,128)S(1)}, f32[2,4,128,128]{3,2,1,0:T(8,128)S(1)}, u32[]{:S(2)}, u32[]{:S(2)}) collective-permute-start(f32[2,4,128,128]{3,2,1,0:T(8,128)S(1)} %get-tuple-element.60), channel_id=1, source_target_pairs={{0,2},{2,0},{4,6},{6,4},{8,10},{10,8},{12,14},{14,12},{16,18},{18,... | collective-permute-start | bytes 1572872 | tf_op jit(solution)/shard_map/ppermute | solution.py:321
  30.1 4.1 %collective-permute-start.4 = (f32[520,128]{1,0:T(8,128)S(1)}, f32[520,128]{1,0:T(8,128)S(1)}, u32[]{:S(2)}, u32[]{:S(2)}) collective-permute-start(f32[520,128]{1,0:T(8,128)S(1)} %collective-permute-done.3.refs_2_), channel_id=1, source_target_pairs={{0,4},{2,6},{4,8},{6,10},{8,12},{10,14},{12,16},{14,18},{16,20},{1... | collective-permute-start | bytes 798728 | tf_op jit(solution)/shard_map/ppermute | solution.py:321
  35.8 4.1 %collective-permute-start.12 = (f32[520,128]{1,0:T(8,128)S(1)}, f32[520,128]{1,0:T(8,128)S(1)}, u32[]{:S(2)}, u32[]{:S(2)}) collective-permute-start(f32[520,128]{1,0:T(8,128)S(1)} %collective-permute-done.11.refs_2_), channel_id=1, source_target_pairs={{0,4},{2,6},{4,8},{6,10},{8,12},{10,14},{12,16},{14,18},{16,20},{1... | collective-permute-start | bytes 798728 | tf_op jit(solution)/shard_map/ppermute | solution.py:321
  41.9 4.5 %collective-permute-start.5 = (f32[520,128]{1,0:T(8,128)S(1)}, f32[520,128]{1,0:T(8,128)}, u32[]{:S(2)}, u32[]{:S(2)}) collective-permute-start(f32[520,128]{1,0:T(8,128)S(1)} %collective-permute-done.4.refs_3_), channel_id=1, source_target_pairs={{0,4},{2,6},{4,8},{6,10},{8,12},{10,14},{12,16},{14,18},{16,20},{1... | collective-permute-start | bytes 798728 | tf_op jit(solution)/shard_map/ppermute | solution.py:321
  47.2 4.9 %collective-permute-start.13 = (f32[520,128]{1,0:T(8,128)S(1)}, f32[520,128]{1,0:T(8,128)}, u32[]{:S(2)}, u32[]{:S(2)}) collective-permute-start(f32[520,128]{1,0:T(8,128)S(1)} %collective-permute-done.12.refs_3_), channel_id=1, source_target_pairs={{0,4},{2,6},{4,8},{6,10},{8,12},{10,14},{12,16},{14,18},{16,20},{1... | collective-permute-start | bytes 798728 | tf_op jit(solution)/shard_map/ppermute | solution.py:321
  57.5 2.3 %shard_map.89 = (f32[512,128]{1,0:T(8,128)S(1)}, f32[128,512]{1,0:T(8,128)S(1)}, f32[8,512]{1,0:T(8,128)S(1)}) custom-call(s32[1]{0:T(128)} %bitcast.1.chip_ref, s32[1]{0:T(128)} %bitcast.core_ref, f32[2,4,128,128]{3,2,1,0:T(8,128)S(1)} %get-tuple-element.54.own_ref, f32[2,4,128,128]{3,2,1,0:T(8,128)S(1)} %collective-permute-done.2.far_ref, ...), custom_call_target="tpu_custom_call" | custom-call | flops 503316480 | bytes 2097152 | tf_op jit(solution)/shard_map/pallas_call | solution.py:372
  61.2 2.3 %shard_map.92 = (f32[512,128]{1,0:T(8,128)S(1)}, f32[128,512]{1,0:T(8,128)S(1)}, f32[8,512]{1,0:T(8,128)S(1)}) custom-call(s32[1]{0:T(128)} %bitcast.1.chip_ref, s32[1]{0:T(128)} %bitcast.core_ref, f32[2,4,128,128]{3,2,1,0:T(8,128)S(1)} %get-tuple-element.54.own_ref, f32[2,4,128,128]{3,2,1,0:T(8,128)S(1)} %collective-permute-done.2.far_ref, ...), custom_call_target="tpu_custom_call" | custom-call | flops 503316480 | bytes 2097152 | tf_op jit(solution)/shard_map/pallas_call | solution.py:372
  65.0 2.5 %shard_map.93 = (f32[512,128]{1,0:T(8,128)S(1)}, f32[512,128]{1,0:T(8,128)S(1)}, f32[512,128]{1,0:T(8,128)S(1)}, f32[512,128]{1,0:T(8,128)S(1)}, f32[2,128,128]{...) custom-call(f32[2,4,128,128]{3,2,1,0:T(8,128)S(1)} %get-tuple-element.54.own_ref, ...), custom_call_target="tpu_custom_call" | custom-call | flops 1207959552 | bytes 7340032 | tf_op jit(solution)/shard_map/pallas_call | solution.py:381
  67.5 2.5 %shard_map.90 = (f32[512,128]{1,0:T(8,128)S(1)}, f32[512,128]{1,0:T(8,128)S(1)}, f32[512,128]{1,0:T(8,128)S(1)}, f32[512,128]{1,0:T(8,128)S(1)}, f32[2,128,128]{...) custom-call(f32[2,4,128,128]{3,2,1,0:T(8,128)S(1)} %get-tuple-element.54.own_ref, ...), custom_call_target="tpu_custom_call" | custom-call | flops 1207959552 | bytes 7340032 | tf_op jit(solution)/shard_map/pallas_call | solution.py:381
  71.4 3.8 %collective-permute-done.15 = f32[512,128]{1,0:T(8,128)S(1)} collective-permute-done((f32[512,128]{1,0:T(8,128)S(1)}, f32[512,128]{1,0:T(8,128)S(1)}, u32[]{:S(2)}, u32[]{:S(2)}) %collective-permute-start.15) | collective-permute-done | bytes 262176 | tf_op jit(solution)/shard_map/ppermute | solution.py:321
  76.5 4.6 %collective-permute-done.8 = f32[512,128]{1,0:T(8,128)S(1)} collective-permute-done((f32[512,128]{1,0:T(8,128)S(1)}, f32[512,128]{1,0:T(8,128)S(1)}, u32[]{:S(2)}, u32[]{:S(2)}) %collective-permute-start.8) | collective-permute-done | bytes 262176 | tf_op jit(solution)/shard_map/ppermute | solution.py:321
  82.4 4.3 %collective-permute-done.16 = f32[512,128]{1,0:T(8,128)S(1)} collective-permute-done((f32[512,128]{1,0:T(8,128)S(1)}, f32[512,128]{1,0:T(8,128)S(1)}, u32[]{:S(2)}, u32[]{:S(2)}) %collective-permute-start.16) | collective-permute-done | bytes 262176 | tf_op jit(solution)/shard_map/ppermute | solution.py:321
  88.1 3.7 %collective-permute-start.14 = (f32[4,128,128]{2,1,0:T(8,128)S(1)}, f32[4,128,128]{2,1,0:T(8,128)S(1)}, u32[]{:S(2)}, u32[]{:S(2)}) collective-permute-start(f32[4,128,128]{2,1,0:T(8,128)S(1)} %pad_maximum_fusion.1), channel_id=1, source_target_pairs={{0,2},{2,0},{4,6},{6,4},{8,10},{10,8},{12,14},{14,12},{16,18},{18,... | collective-permute-start | bytes 786440 | tf_op jit(solution)/shard_map/ppermute | solution.py:321
  93.6 4.3 %collective-permute-done.17 = f32[512,128]{1,0:T(8,128)S(1)} collective-permute-done((f32[512,128]{1,0:T(8,128)S(1)}, f32[512,128]{1,0:T(8,128)S(1)}, u32[]{:S(2)}, u32[]{:S(2)}) %collective-permute-start.17) | collective-permute-done | bytes 262176 | tf_op jit(solution)/shard_map/ppermute | solution.py:321
  99.2 4.2 %collective-permute-done.10.got = f32[512,128]{1,0:T(8,128)S(1)} collective-permute-done((f32[512,128]{1,0:T(8,128)S(1)}, f32[512,128]{1,0:T(8,128)S(1)}, u32[]{:S(2)}, u32[]{:S(2)}) %collective-permute-start.10) | collective-permute-done | bytes 262176 | tf_op jit(solution)/shard_map/ppermute | solution.py:321
  104.5 4.6 %collective-permute-done.18.got = f32[512,128]{1,0:T(8,128)S(1)} collective-permute-done((f32[512,128]{1,0:T(8,128)S(1)}, f32[512,128]{1,0:T(8,128)S(1)}, u32[]{:S(2)}, u32[]{:S(2)}) %collective-permute-start.18) | collective-permute-done | bytes 262176 | tf_op jit(solution)/shard_map/ppermute | solution.py:321
  109.2 3.1 %collective-permute-start.20 = (f32[256,128]{1,0:T(8,128)S(1)}, f32[256,128]{1,0:T(8,128)S(1)}, u32[]{:S(2)}, u32[]{:S(2)}) collective-permute-start(f32[256,128]{1,0:T(8,128)S(1)} %get-tuple-element.98), channel_id=1, source_target_pairs={{0,2},{2,0},{4,6},{6,4},{8,10},{10,8},{12,14},{14,12},{16,18},{18,... | collective-permute-start | bytes 393224 | tf_op jit(solution)/shard_map/ppermute | solution.py:321
  114.2 37.1 %all_to_all.10 = f32[32,1,128]{2,1,0:T(1,128)S(1)} all-to-all(f32[32,1,128]{2,1,0:T(1,128)S(1)} %bitcast.16), channel_id=1, replica_groups=mesh['x'=4,'yh'=2,'z'=16,'core'=2,'yl'=2] {'x','yh','core','yl'}, dimensions={0} | all-to-all | bytes 32768 | tf_op jit(solution)/shard_map/all_to_all | solution.py:413
  152.2 17.5 %all_to_all.11 = f32[16,1,128]{2,1,0:T(1,128)S(1)} all-to-all(f32[16,1,128]{2,1,0:T(1,128)S(1)} %broadcast_in_dim.2), channel_id=1, replica_groups=mesh['x'=4,'yh'=2,'z'=16,'core'=2,'yl'=2] {'z'}, dimensions={0} | all-to-all | bytes 16384 | tf_op jit(solution)/shard_map/all_to_all | solution.py:423
  (50 shorter events, 30.7 us)
Async XLA Ops:
  2.5 11.2 %collective-permute-start = (f32[520,128]{1,0:T(8,128)}, f32[520,128]{1,0:T(8,128)S(1)}, u32[]{:S(2)}, u32[]{:S(2)}) collective-permute-start(f32[520,128]{1,0:T(8,128)} %get-tuple-element.55.own_ref), channel_id=1, source_target_pairs={{0,4},{2,6},{4,8},{6,10},{8,12},{10,14},{12,16},{14,18},{16,20},{1... | collective-permute-start | bytes 798728 | tf_op jit(solution)/shard_map/ppermute | solution.py:321
  6.9 10.8 %collective-permute-start.1 = (f32[520,128]{1,0:T(8,128)}, f32[520,128]{1,0:T(8,128)S(1)}, u32[]{:S(2)}, u32[]{:S(2)}) collective-permute-start(f32[520,128]{1,0:T(8,128)} %get-tuple-element.62), channel_id=1, source_target_pairs={{0,6},{2,4},{4,10},{6,8},{8,14},{10,12},{12,18},{14,16},{16,22},{1... | collective-permute-start | bytes 798728 | tf_op jit(solution)/shard_map/ppermute | solution.py:321
  11.3 1.0 copy-start
  12.4 1.0 copy-start.1
  17.8 12.3 %collective-permute-start.3 = (f32[520,128]{1,0:T(8,128)S(1)}, f32[520,128]{1,0:T(8,128)S(1)}, u32[]{:S(2)}, u32[]{:S(2)}) collective-permute-start(f32[520,128]{1,0:T(8,128)S(1)} %get-tuple-element.61.refs_1_), channel_id=1, source_target_pairs={{0,4},{2,6},{4,8},{6,10},{8,12},{10,14},{12,16},{14,18},{16,20},{1... | collective-permute-start | bytes 798728 | tf_op jit(solution)/shard_map/ppermute | solution.py:321
  24.0 11.8 %collective-permute-start.11 = (f32[520,128]{1,0:T(8,128)S(1)}, f32[520,128]{1,0:T(8,128)S(1)}, u32[]{:S(2)}, u32[]{:S(2)}) collective-permute-start(f32[520,128]{1,0:T(8,128)S(1)} %get-tuple-element.77.refs_1_), channel_id=1, source_target_pairs={{0,4},{2,6},{4,8},{6,10},{8,12},{10,14},{12,16},{14,18},{16,20},{1... | collective-permute-start | bytes 798728 | tf_op jit(solution)/shard_map/ppermute | solution.py:321
  26.4 26.7 %collective-permute-start.2 = (f32[2,4,128,128]{3,2,1,0:T(8,128)S(1)}, f32[2,4,128,128]{3,2,1,0:T(8,128)S(1)}, u32[]{:S(2)}, u32[]{:S(2)}) collective-permute-start(f32[2,4,128,128]{3,2,1,0:T(8,128)S(1)} %get-tuple-element.60), channel_id=1, source_target_pairs={{0,2},{2,0},{4,6},{6,4},{8,10},{10,8},{12,14},{14,12},{16,18},{18,... | collective-permute-start | bytes 1572872 | tf_op jit(solution)/shard_map/ppermute | solution.py:321
  30.1 11.8 %collective-permute-start.4 = (f32[520,128]{1,0:T(8,128)S(1)}, f32[520,128]{1,0:T(8,128)S(1)}, u32[]{:S(2)}, u32[]{:S(2)}) collective-permute-start(f32[520,128]{1,0:T(8,128)S(1)} %collective-permute-done.3.refs_2_), channel_id=1, source_target_pairs={{0,4},{2,6},{4,8},{6,10},{8,12},{10,14},{12,16},{14,18},{16,20},{1... | collective-permute-start | bytes 798728 | tf_op jit(solution)/shard_map/ppermute | solution.py:321
  35.8 11.4 %collective-permute-start.12 = (f32[520,128]{1,0:T(8,128)S(1)}, f32[520,128]{1,0:T(8,128)S(1)}, u32[]{:S(2)}, u32[]{:S(2)}) collective-permute-start(f32[520,128]{1,0:T(8,128)S(1)} %collective-permute-done.11.refs_2_), channel_id=1, source_target_pairs={{0,4},{2,6},{4,8},{6,10},{8,12},{10,14},{12,16},{14,18},{16,20},{1... | collective-permute-start | bytes 798728 | tf_op jit(solution)/shard_map/ppermute | solution.py:321
  39.9 12.2 %collective-permute-start.6 = (f32[520,128]{1,0:T(8,128)}, f32[520,128]{1,0:T(8,128)S(1)}, u32[]{:S(2)}, u32[]{:S(2)}) collective-permute-start(f32[520,128]{1,0:T(8,128)} %get-tuple-element.62), channel_id=1, source_target_pairs={{0,2},{2,0},{4,6},{6,4},{8,10},{10,8},{12,14},{14,12},{16,18},{18,... | collective-permute-start | bytes 798728 | tf_op jit(solution)/shard_map/ppermute | solution.py:321
  41.9 15.6 %collective-permute-start.5 = (f32[520,128]{1,0:T(8,128)S(1)}, f32[520,128]{1,0:T(8,128)}, u32[]{:S(2)}, u32[]{:S(2)}) collective-permute-start(f32[520,128]{1,0:T(8,128)S(1)} %collective-permute-done.4.refs_3_), channel_id=1, source_target_pairs={{0,4},{2,6},{4,8},{6,10},{8,12},{10,14},{12,16},{14,18},{16,20},{1... | collective-permute-start | bytes 798728 | tf_op jit(solution)/shard_map/ppermute | solution.py:321
  47.2 13.9 %collective-permute-start.13 = (f32[520,128]{1,0:T(8,128)S(1)}, f32[520,128]{1,0:T(8,128)}, u32[]{:S(2)}, u32[]{:S(2)}) collective-permute-start(f32[520,128]{1,0:T(8,128)S(1)} %collective-permute-done.12.refs_3_), channel_id=1, source_target_pairs={{0,4},{2,6},{4,8},{6,10},{8,12},{10,14},{12,16},{14,18},{16,20},{1... | collective-permute-start | bytes 798728 | tf_op jit(solution)/shard_map/ppermute | solution.py:321
  52.2 1.0 copy-start.2
  59.8 10.2 %collective-permute-start.7 = (f32[512,128]{1,0:T(8,128)S(1)}, f32[512,128]{1,0:T(8,128)S(1)}, u32[]{:S(2)}, u32[]{:S(2)}) collective-permute-start(f32[512,128]{1,0:T(8,128)S(1)} %get-tuple-element.65), channel_id=1, source_target_pairs={{4,0},{6,2},{8,4},{10,6},{12,8},{14,10},{16,12},{18,14},{20,16},{2... | collective-permute-start | bytes 786440 | tf_op jit(solution)/shard_map/ppermute | solution.py:321
  63.5 11.7 %collective-permute-start.15 = (f32[512,128]{1,0:T(8,128)S(1)}, f32[512,128]{1,0:T(8,128)S(1)}, u32[]{:S(2)}, u32[]{:S(2)}) collective-permute-start(f32[512,128]{1,0:T(8,128)S(1)} %get-tuple-element.87), channel_id=1, source_target_pairs={{4,0},{6,2},{8,4},{10,6},{12,8},{14,10},{16,12},{18,14},{20,16},{2... | collective-permute-start | bytes 786440 | tf_op jit(solution)/shard_map/ppermute | solution.py:321
  70.1 11.0 %collective-permute-start.8 = (f32[512,128]{1,0:T(8,128)S(1)}, f32[512,128]{1,0:T(8,128)S(1)}, u32[]{:S(2)}, u32[]{:S(2)}) collective-permute-start(f32[512,128]{1,0:T(8,128)S(1)} %add.26), channel_id=1, source_target_pairs={{4,0},{6,2},{8,4},{10,6},{12,8},{14,10},{16,12},{18,14},{20,16},{2... | collective-permute-start | bytes 786440 | tf_op jit(solution)/shard_map/ppermute | solution.py:321
  75.2 11.5 %collective-permute-start.16 = (f32[512,128]{1,0:T(8,128)S(1)}, f32[512,128]{1,0:T(8,128)S(1)}, u32[]{:S(2)}, u32[]{:S(2)}) collective-permute-start(f32[512,128]{1,0:T(8,128)S(1)} %add.29), channel_id=1, source_target_pairs={{4,0},{6,2},{8,4},{10,6},{12,8},{14,10},{16,12},{18,14},{20,16},{2... | collective-permute-start | bytes 786440 | tf_op jit(solution)/shard_map/ppermute | solution.py:321
  81.1 11.1 %collective-permute-start.9 = (f32[512,128]{1,0:T(8,128)S(1)}, f32[512,128]{1,0:T(8,128)S(1)}, u32[]{:S(2)}, u32[]{:S(2)}) collective-permute-start(f32[512,128]{1,0:T(8,128)S(1)} %add.27), channel_id=1, source_target_pairs={{4,0},{6,2},{8,4},{10,6},{12,8},{14,10},{16,12},{18,14},{20,16},{2... | collective-permute-start | bytes 786440 | tf_op jit(solution)/shard_map/ppermute | solution.py:321
  86.7 11.1 %collective-permute-start.17 = (f32[512,128]{1,0:T(8,128)S(1)}, f32[512,128]{1,0:T(8,128)S(1)}, u32[]{:S(2)}, u32[]{:S(2)}) collective-permute-start(f32[512,128]{1,0:T(8,128)S(1)} %add.30), channel_id=1, source_target_pairs={{4,0},{6,2},{8,4},{10,6},{12,8},{14,10},{16,12},{18,14},{20,16},{2... | collective-permute-start | bytes 786440 | tf_op jit(solution)/shard_map/ppermute | solution.py:321
  88.1 11.2 %collective-permute-start.14 = (f32[4,128,128]{2,1,0:T(8,128)S(1)}, f32[4,128,128]{2,1,0:T(8,128)S(1)}, u32[]{:S(2)}, u32[]{:S(2)}) collective-permute-start(f32[4,128,128]{2,1,0:T(8,128)S(1)} %pad_maximum_fusion.1), channel_id=1, source_target_pairs={{0,2},{2,0},{4,6},{6,4},{8,10},{10,8},{12,14},{14,12},{16,18},{18,... | collective-permute-start | bytes 786440 | tf_op jit(solution)/shard_map/ppermute | solution.py:321
  92.3 11.2 %collective-permute-start.10 = (f32[512,128]{1,0:T(8,128)S(1)}, f32[512,128]{1,0:T(8,128)S(1)}, u32[]{:S(2)}, u32[]{:S(2)}) collective-permute-start(f32[512,128]{1,0:T(8,128)S(1)} %add.28), channel_id=1, source_target_pairs={{4,0},{6,2},{8,4},{10,6},{12,8},{14,10},{16,12},{18,14},{20,16},{2... | collective-permute-start | bytes 786440 | tf_op jit(solution)/shard_map/ppermute | solution.py:321
  97.9 11.2 %collective-permute-start.18 = (f32[512,128]{1,0:T(8,128)S(1)}, f32[512,128]{1,0:T(8,128)S(1)}, u32[]{:S(2)}, u32[]{:S(2)}) collective-permute-start(f32[512,128]{1,0:T(8,128)S(1)} %add.31), channel_id=1, source_target_pairs={{4,0},{6,2},{8,4},{10,6},{12,8},{14,10},{16,12},{18,14},{20,16},{2... | collective-permute-start | bytes 786440 | tf_op jit(solution)/shard_map/ppermute | solution.py:321
  109.2 42.2 %collective-permute-start.20 = (f32[256,128]{1,0:T(8,128)S(1)}, f32[256,128]{1,0:T(8,128)S(1)}, u32[]{:S(2)}, u32[]{:S(2)}) collective-permute-start(f32[256,128]{1,0:T(8,128)S(1)} %get-tuple-element.98), channel_id=1, source_target_pairs={{0,2},{2,0},{4,6},{6,4},{8,10},{10,8},{12,14},{14,12},{16,18},{18,... | collective-permute-start | bytes 393224 | tf_op jit(solution)/shard_map/ppermute | solution.py:321
  112.3 39.1 %collective-permute-start.19 = (f32[256,128]{1,0:T(8,128)S(1)}, f32[256,128]{1,0:T(8,128)S(1)}, u32[]{:S(2)}, u32[]{:S(2)}) collective-permute-start(f32[256,128]{1,0:T(8,128)S(1)} %get-tuple-element.97), channel_id=1, source_target_pairs={{0,2},{2,0},{4,6},{6,4},{8,10},{10,8},{12,14},{14,12},{16,18},{18,... | collective-permute-start | bytes 393224 | tf_op jit(solution)/shard_map/ppermute | solution.py:321

commit v4 on v3

--- a/solution.py
+++ b/solution.py
@@ -86,7 +86,7 @@
         copy.wait()
 
 
-def prep_kv_kernel(core_ref, k_hbm, v_hbm, b_hbm, own_ref, sib_ref, k_ref, v_ref, b_ref, sems):
+def prep_kv_kernel(core_ref, k_hbm, v_hbm, b_hbm, own0, own1, sib0, sib1, all_sib, k_ref, v_ref, b_ref, sems):
     fetch((k_hbm, v_hbm, b_hbm), (k_ref, v_ref, b_ref), sems)
     core = core_ref[0]
     for side in range(2):
@@ -94,15 +94,18 @@
         @pl.when(core == side)
         def _():
             for kind, source in enumerate((k_ref, v_ref)):
-                for head in range(2):
-                    rows = pl.ds((2 * head + kind) * TOK, TOK)
+                for head, (own_ref, sib_ref) in enumerate(((own0, sib0), (own1, sib1))):
+                    rows = pl.ds(kind * TOK, TOK)
                     own_ref[rows, :] = source[pl.ds(2 * side + head, TOK, stride=4), :]
-                    sib_ref[rows, :] = source[pl.ds(2 * (1 - side) + head, TOK, stride=4), :]
+                    other = source[pl.ds(2 * (1 - side) + head, TOK, stride=4), :]
+                    sib_ref[rows, :] = other
+                    all_sib[pl.ds((2 * head + kind) * TOK, TOK), :] = other
 
     row = lax.broadcasted_iota(jnp.int32, (8, TOK), 0)
     begins = jnp.where(row == 0, jnp.where(b_ref[...] > 0, 1.0, 0.0), 0.0)
-    own_ref[4 * TOK :, :] = begins
-    sib_ref[4 * TOK :, :] = begins
+    for out in (own0, own1, sib0, sib1):
+        out[CHIP:, :] = begins
+    all_sib[BODY:, :] = begins
 
 
 def prep_q_kernel(core_ref, q_hbm, d_hbm, own_ref, sib_ref, q_ref, d_ref, sems):
@@ -118,15 +121,25 @@
                     sib_ref[kind, head] = source[pl.ds(4 * (1 - side) + head, TOK, stride=8), :]
 
 
-def pack_kernel(own_ref, far_ref, *outs):
+def pack_kernel(own_ref, far_ref, out):
     row = lax.broadcasted_iota(jnp.int32, (8, TOK), 0)
-    first, second = (source[4 * TOK : 4 * TOK + 1, :] for source in (own_ref, far_ref))
-    begins = jnp.where(row == 0, first, jnp.where(row == 1, second, 0.0))
-    for head, out in enumerate(outs):
+    first, second = (source[CHIP : CHIP + 1, :] for source in (own_ref, far_ref))
+    out[BODY:, :] = jnp.where(row == 0, first, jnp.where(row == 1, second, 0.0))
+    for kind in range(2):
+        for half, source in enumerate((own_ref, far_ref)):
+            out[pl.ds(kind * CHIP + half * TOK, TOK), :] = source[pl.ds(kind * TOK, TOK), :]
+
+
+def pack_own_kernel(own0, own1, far_ref, *outs):
+    row = lax.broadcasted_iota(jnp.int32, (8, TOK), 0)
+    begins = jnp.where(
+        row == 0, own0[CHIP : CHIP + 1, :], jnp.where(row == 1, far_ref[BODY : BODY + 1, :], 0.0)
+    )
+    for head, (own_ref, out) in enumerate(zip((own0, own1), outs)):
+        out[BODY:, :] = begins
         for kind in range(2):
-            for half, source in enumerate((own_ref, far_ref)):
-                out[pl.ds(kind * CHIP + half * TOK, TOK), :] = source[pl.ds((2 * head + kind) * TOK, TOK), :]
-        out[BODY:, :] = begins
+            out[pl.ds(kind * CHIP, TOK), :] = own_ref[pl.ds(kind * TOK, TOK), :]
+            out[pl.ds(kind * CHIP + TOK, TOK), :] = far_ref[pl.ds((2 * head + kind) * TOK, TOK), :]
 
 
 def query_rows(own_ref, far_ref, kind, head):
@@ -320,13 +333,13 @@
         ]
         return lax.ppermute(value, CTX, pairs)
 
-    half_rows = whole(4 * TOK + 8, width)
+    half_rows = whole(CHIP + 8, width)
     qd = whole(2, 4, TOK, width)
-    kv_own, kv_sib = call(
+    *kv_own, kv_sib0, kv_sib1, sib_all = call(
         prep_kv_kernel,
-        (sds(4 * TOK + 8, width), sds(4 * TOK + 8, width)),
+        (sds(CHIP + 8, width),) * 4 + (sds(BODY + 8, width),),
         [SCALAR, FAR, FAR, FAR],
-        (half_rows, half_rows),
+        (half_rows,) * 4 + (whole(BODY + 8, width),),
         moved=1 << 20,
         vmem=56,
         scratch=[pltpu.VMEM((tokens * groups, width), F32)] * 2
@@ -346,29 +359,43 @@
         scratch=[pltpu.VMEM((tokens * heads, width), F32)] * 2 + [pltpu.SemaphoreType.DMA((2,))],
     )(core, queries.reshape(tokens * heads, width), out_grad.reshape(tokens * heads, width))
     block, body = whole(BODY + 8, width), whole(BODY, width)
-    pack = call(pack_kernel, (sds(BODY + 8, width),) * 2, [half_rows] * 2, (block, block), moved=1 << 20)
-    first = pack(send(kv_own, 1), send(kv_sib, 1, 1))
-    first, qd_sib, kv_sib = lax.optimization_barrier((first, qd_sib, kv_sib))
-    rings = [[None, first[0]], [None, first[1]]]
-    for _ in range(REACH - 1):
+    pack = call(pack_kernel, sds(BODY + 8, width), [half_rows] * 2, block, moved=1 << 19)
+    kv_sib = [kv_sib0, kv_sib1]
+    rings = [[None, pack(send(own, 1), send(sib, 1, 1))] for own, sib in zip(kv_own, kv_sib)]
+    rings[1][1], qd_sib, sib_all = lax.optimization_barrier((rings[1][1], qd_sib, sib_all))
+    for _ in range(REACH - 2):
         for ring in rings:
             ring.append(send(ring[-1], 1))
-    rings[0][0], rings[1][0] = pack(kv_own, send(kv_sib, 0, 1))
     qd_far = send(qd_sib, 0, 1)
+    rings[0][0], rings[1][0] = call(
+        pack_own_kernel,
+        (sds(BODY + 8, width),) * 2,
+        [half_rows, half_rows, block],
+        (block, block),
+        moved=1 << 20,
+    )(*kv_own, send(sib_all, 0, 1))
     one = 2 * ROWS * CHIP * width
     sheet, stats, turned = whole(REACH * CHIP, ROWS), whole(8, ROWS), whole(width, ROWS)
     pair = whole(2, TOK, width)
     got, grads, rest = [], [], []
+    near = []
     for head, ring in enumerate(rings):
-        p, dp, stat = call(
-            functools.partial(near_kernel, head, width),
-            (sds(REACH * CHIP, ROWS), sds(REACH * CHIP, ROWS), sds(8, ROWS)),
-            [SCALAR, SCALAR, qd, qd] + [block] * REACH,
-            (sheet, sheet, stats),
-            flops=2 * REACH * 3 * one,
-            moved=6 << 20,
-            vmem=16,
-        )(chip, core, qd_own, qd_far, *ring[:REACH])
+        if head:
+            ring[-1], near[0] = lax.optimization_barrier((ring[-1], near[0]))
+        ring.append(send(ring[-1], 1))
+        near.append(
+            call(
+                functools.partial(near_kernel, head, width),
+                (sds(REACH * CHIP, ROWS), sds(REACH * CHIP, ROWS), sds(8, ROWS)),
+                [SCALAR, SCALAR, qd, qd] + [block] * REACH,
+                (sheet, sheet, stats),
+                flops=2 * REACH * 3 * one,
+                moved=6 << 20,
+                vmem=16,
+            )(chip, core, qd_own, qd_far, *ring[:REACH])
+        )
+    for head, ring in enumerate(rings):
+        p, dp, stat = near[head]
         grad, dq4, stat2 = call(
             functools.partial(last_kernel, head, width),
             (sds(BODY, width), sds(width, ROWS), sds(8, ROWS)),
@@ -402,6 +429,7 @@
         moved=2 << 20,
     )(core, got[0], grads[0][0], rest[0][2], dq_own, dq_far)
     far0 = send(give0, 0, 1)
+    got[1], far0 = lax.optimization_barrier((got[1], far0))
     keep1, give1, row = call(
         second_end_kernel,
         (sds(CHIP, width), sds(CHIP, width), sds(plane, width)),

time: 173 us -> 164 us (0.948)
  waiting for transfers between devices: 33.8 us -> 20.4 us
  starting transfers between devices: 58.9 us -> 70 us
  blocking collectives: 54.6 us -> 49.4 us
    ppermute x21 -> x23, waiting for transfers between devices: 33.8 us -> 20.4 us  [send(): return lax.ppermute(value, CTX, pairs)]
    ppermute x21 -> x23, starting transfers between devices: 58.9 us -> 70 us  [send(): return lax.ppermute(value, CTX, pairs)]
    all_to_all x1, blocking collectives: 37.1 us -> 30.3 us  [shards(): lax.all_to_all(row.reshape(plane, 1, width), ('x', 'yh', 'core', 'yl'), 0...]
    pallas_call x2, Pallas kernels: 4.65 us -> 2.73 us  [shards(): call(functools.partial(last_kernel, head, width), (sds(BODY, width), sds(...]
  transfers between devices with their start and end apart: 21 -> 23, of which waited for: 11 -> 9; matrix products, arithmetic and copies ran while one was open for 0% -> 0% of each run, Pallas kernels for 9% -> 9%
where the time goes in v4:
time: 164 us; the launch traced here: 163 us
  starting transfers between devices  70 us (43%)
  blocking collectives  49.4 us (30%)
  waiting for transfers between devices  20.4 us (12%)
  Pallas kernels  17.2 us (10%)
  between operations  2.84 us (2%)
  local copies, waits for them, and re-layouts  2.1 us (1%)
    ppermute x23, starting transfers between devices, send(): return lax.ppermute(value, CTX, pairs)  70 us
    all_to_all x1, blocking collectives, shards(): lax.all_to_all(row.reshape(plane, 1, width), ('x', 'yh', 'core', 'yl'), 0...  30.3 us
    ppermute x23, waiting for transfers between devices, send(): return lax.ppermute(value, CTX, pairs)  20.4 us
    all_to_all x1, blocking collectives, shards(): parts = lax.all_to_all(parts, 'z', 0, 0)  19.1 us
    pallas_call x2, Pallas kernels, shards(): call(functools.partial(back_kernel, head, width), (sds(BODY, width),) * R...  5.07 us
    pallas_call x2, Pallas kernels, shards(): call(functools.partial(near_kernel, head, width), (sds(REACH * CHIP, ROWS...  4.33 us
  transfers between devices with their start and end apart: 23, of which 9 were waited for; matrix products, arithmetic and copies ran while one was open for 0% of the time, Pallas kernels for 9%

profile of v4, /device:TPU:1, one launch (start us, length us, event | category | flops | bytes accessed | tf_op | source)
XLA Modules:
  0.0 162.7 jit_solution(11629466031960125196)
XLA Ops:
  2.6 5.1 %collective-permute-start.4 = (f32[264,128]{1,0:T(8,128)}, f32[264,128]{1,0:T(8,128)S(1)}, u32[]{:S(2)}, u32[]{:S(2)}) collective-permute-start(f32[264,128]{1,0:T(8,128)} %get-tuple-element.67), channel_id=1, source_target_pairs={{0,6},{2,4},{4,10},{6,8},{8,14},{10,12},{12,18},{14,16},{16,22},{1... | collective-permute-start | bytes 405512 | tf_op jit(solution)/shard_map/ppermute | solution.py:334
  7.7 3.5 %collective-permute-start.3 = (f32[264,128]{1,0:T(8,128)}, f32[264,128]{1,0:T(8,128)S(1)}, u32[]{:S(2)}, u32[]{:S(2)}) collective-permute-start(f32[264,128]{1,0:T(8,128)} %get-tuple-element.66.own0), channel_id=1, source_target_pairs={{0,4},{2,6},{4,8},{6,10},{8,12},{10,14},{12,16},{14,18},{16,20},{1... | collective-permute-start | bytes 405512 | tf_op jit(solution)/shard_map/ppermute | solution.py:334
  11.3 3.5 %collective-permute-start.1 = (f32[264,128]{1,0:T(8,128)}, f32[264,128]{1,0:T(8,128)S(1)}, u32[]{:S(2)}, u32[]{:S(2)}) collective-permute-start(f32[264,128]{1,0:T(8,128)} %get-tuple-element.62), channel_id=1, source_target_pairs={{0,6},{2,4},{4,10},{6,8},{8,14},{10,12},{12,18},{14,16},{16,22},{1... | collective-permute-start | bytes 405512 | tf_op jit(solution)/shard_map/ppermute | solution.py:334
  14.8 4.8 %collective-permute-start = (f32[264,128]{1,0:T(8,128)}, f32[264,128]{1,0:T(8,128)S(1)}, u32[]{:S(2)}, u32[]{:S(2)}) collective-permute-start(f32[264,128]{1,0:T(8,128)} %get-tuple-element.61.own1), channel_id=1, source_target_pairs={{0,4},{2,6},{4,8},{6,10},{8,12},{10,14},{12,16},{14,18},{16,20},{1... | collective-permute-start | bytes 405512 | tf_op jit(solution)/shard_map/ppermute | solution.py:334
  19.6 3.6 %collective-permute-start.5 = (f32[520,128]{1,0:T(8,128)S(1)}, f32[520,128]{1,0:T(8,128)S(1)}, u32[]{:S(2)}, u32[]{:S(2)}) collective-permute-start(f32[520,128]{1,0:T(8,128)S(1)} %shard_map.87.refs_1_), channel_id=1, source_target_pairs={{0,4},{2,6},{4,8},{6,10},{8,12},{10,14},{12,16},{14,18},{16,20},{1... | collective-permute-start | bytes 798728 | tf_op jit(solution)/shard_map/ppermute | solution.py:334
  26.4 2.9 %collective-permute-start.2 = (f32[2,4,128,128]{3,2,1,0:T(8,128)}, f32[2,4,128,128]{3,2,1,0:T(8,128)S(1)}, u32[]{:S(2)}, u32[]{:S(2)}) collective-permute-start(f32[2,4,128,128]{3,2,1,0:T(8,128)} %get-tuple-element.65), channel_id=1, source_target_pairs={{0,2},{2,0},{4,6},{6,4},{8,10},{10,8},{12,14},{14,12},{16,18},{18,... | collective-permute-start | bytes 1572872 | tf_op jit(solution)/shard_map/ppermute | solution.py:334
  29.3 3.5 %collective-permute-start.8 = (f32[520,128]{1,0:T(8,128)S(1)}, f32[520,128]{1,0:T(8,128)S(1)}, u32[]{:S(2)}, u32[]{:S(2)}) collective-permute-start(f32[520,128]{1,0:T(8,128)S(1)} %shard_map.86.refs_1_), channel_id=1, source_target_pairs={{0,4},{2,6},{4,8},{6,10},{8,12},{10,14},{12,16},{14,18},{16,20},{1... | collective-permute-start | bytes 798728 | tf_op jit(solution)/shard_map/ppermute | solution.py:334
  32.9 3.5 %collective-permute-start.6 = (f32[520,128]{1,0:T(8,128)S(1)}, f32[520,128]{1,0:T(8,128)S(1)}, u32[]{:S(2)}, u32[]{:S(2)}) collective-permute-start(f32[520,128]{1,0:T(8,128)S(1)} %collective-permute-done.5.refs_2_), channel_id=1, source_target_pairs={{0,4},{2,6},{4,8},{6,10},{8,12},{10,14},{12,16},{14,18},{16,20},{1... | collective-permute-start | bytes 798728 | tf_op jit(solution)/shard_map/ppermute | solution.py:334
  36.4 2.5 %collective-permute-start.10 = (f32[520,128]{1,0:T(8,128)}, f32[520,128]{1,0:T(8,128)S(1)}, u32[]{:S(2)}, u32[]{:S(2)}) collective-permute-start(f32[520,128]{1,0:T(8,128)} %get-tuple-element.69), channel_id=1, source_target_pairs={{0,2},{2,0},{4,6},{6,4},{8,10},{10,8},{12,14},{14,12},{16,18},{18,... | collective-permute-start | bytes 798728 | tf_op jit(solution)/shard_map/ppermute | solution.py:334
  38.9 4.8 %collective-permute-start.9 = (f32[520,128]{1,0:T(8,128)S(1)}, f32[520,128]{1,0:T(8,128)S(1)}, u32[]{:S(2)}, u32[]{:S(2)}) collective-permute-start(f32[520,128]{1,0:T(8,128)S(1)} %collective-permute-done.8.refs_2_), channel_id=1, source_target_pairs={{0,4},{2,6},{4,8},{6,10},{8,12},{10,14},{12,16},{14,18},{16,20},{1... | collective-permute-start | bytes 798728 | tf_op jit(solution)/shard_map/ppermute | solution.py:334
  44.4 4.1 %collective-permute-start.7 = (f32[520,128]{1,0:T(8,128)S(1)}, f32[520,128]{1,0:T(8,128)S(1)}, u32[]{:S(2)}, u32[]{:S(2)}) collective-permute-start(f32[520,128]{1,0:T(8,128)S(1)} %collective-permute-done.6.refs_3_), channel_id=1, source_target_pairs={{0,4},{2,6},{4,8},{6,10},{8,12},{10,14},{12,16},{14,18},{16,20},{1... | collective-permute-start | bytes 798728 | tf_op jit(solution)/shard_map/ppermute | solution.py:334
  48.6 2.2 %shard_map.89 = (f32[1024,512]{1,0:T(8,128)S(1)}, f32[1024,512]{1,0:T(8,128)S(1)}, f32[8,512]{1,0:T(8,128)S(1)}) custom-call(s32[1]{0:T(128)} %bitcast.1.chip_ref, s32[1]{0:T(128)} %bitcast.core_ref, f32[2,4,128,128]{3,2,1,0:T(8,128)S(1)} %get-tuple-element.60.own_ref, f32[2,4,128,128]{3,2,1,0:T(8,128)S(1)} %collective-permute-done.2.far_ref, ...), custom_call_target="tpu_custom_call" | custom-call | flops 805306368 | bytes 6291456 | tf_op jit(solution)/shard_map/pallas_call | solution.py:387
  50.8 4.2 %collective-permute-start.15 = (f32[520,128]{1,0:T(8,128)S(1)}, f32[520,128]{1,0:T(8,128)S(1)}, u32[]{:S(2)}, u32[]{:S(2)}) collective-permute-start(f32[520,128]{1,0:T(8,128)S(1)} %collective-permute-done.9.refs_3_), channel_id=1, source_target_pairs={{0,4},{2,6},{4,8},{6,10},{8,12},{10,14},{12,16},{14,18},{16,20},{1... | collective-permute-start | bytes 798728 | tf_op jit(solution)/shard_map/ppermute | solution.py:334
  63.3 2.5 %shard_map.91 = (f32[512,128]{1,0:T(8,128)S(1)}, f32[512,128]{1,0:T(8,128)S(1)}, f32[512,128]{1,0:T(8,128)S(1)}, f32[512,128]{1,0:T(8,128)S(1)}, f32[2,128,128]{...) custom-call(f32[2,4,128,128]{3,2,1,0:T(8,128)S(1)} %get-tuple-element.60.own_ref, ...), custom_call_target="tpu_custom_call" | custom-call | flops 1207959552 | bytes 7340032 | tf_op jit(solution)/shard_map/pallas_call | solution.py:408
  68.2 2.5 %shard_map.94 = (f32[512,128]{1,0:T(8,128)S(1)}, f32[512,128]{1,0:T(8,128)S(1)}, f32[512,128]{1,0:T(8,128)S(1)}, f32[512,128]{1,0:T(8,128)S(1)}, f32[2,128,128]{...) custom-call(f32[2,4,128,128]{3,2,1,0:T(8,128)S(1)} %get-tuple-element.60.own_ref, ...), custom_call_target="tpu_custom_call" | custom-call | flops 1207959552 | bytes 7340032 | tf_op jit(solution)/shard_map/pallas_call | solution.py:408
  73.8 4.4 %collective-permute-done.12 = f32[512,128]{1,0:T(8,128)S(1)} collective-permute-done((f32[512,128]{1,0:T(8,128)S(1)}, f32[512,128]{1,0:T(8,128)S(1)}, u32[]{:S(2)}, u32[]{:S(2)}) %collective-permute-start.12) | collective-permute-done | bytes 262176 | tf_op jit(solution)/shard_map/ppermute | solution.py:334
  79.5 3.8 %collective-permute-done.18 = f32[512,128]{1,0:T(8,128)S(1)} collective-permute-done((f32[512,128]{1,0:T(8,128)S(1)}, f32[512,128]{1,0:T(8,128)S(1)}, u32[]{:S(2)}, u32[]{:S(2)}) %collective-permute-start.18) | collective-permute-done | bytes 262176 | tf_op jit(solution)/shard_map/ppermute | solution.py:334
  84.7 5.2 %collective-permute-start.16 = (f32[4,128,128]{2,1,0:T(8,128)S(1)}, f32[4,128,128]{2,1,0:T(8,128)S(1)}, u32[]{:S(2)}, u32[]{:S(2)}) collective-permute-start(f32[4,128,128]{2,1,0:T(8,128)S(1)} %pad_maximum_fusion.1), channel_id=1, source_target_pairs={{0,2},{2,0},{4,6},{6,4},{8,10},{10,8},{12,14},{14,12},{16,18},{18,... | collective-permute-start | bytes 786440 | tf_op jit(solution)/shard_map/ppermute | solution.py:334
  91.2 3.1 %collective-permute-done.19 = f32[512,128]{1,0:T(8,128)S(1)} collective-permute-done((f32[512,128]{1,0:T(8,128)S(1)}, f32[512,128]{1,0:T(8,128)S(1)}, u32[]{:S(2)}, u32[]{:S(2)}) %collective-permute-start.19) | collective-permute-done | bytes 262176 | tf_op jit(solution)/shard_map/ppermute | solution.py:334
  95.7 4.0 %collective-permute-done.14.got = f32[512,128]{1,0:T(8,128)S(1)} collective-permute-done((f32[512,128]{1,0:T(8,128)S(1)}, f32[512,128]{1,0:T(8,128)S(1)}, u32[]{:S(2)}, u32[]{:S(2)}) %collective-permute-start.14) | collective-permute-done | bytes 262176 | tf_op jit(solution)/shard_map/ppermute | solution.py:334
  100.7 6.0 %collective-permute-start.21 = (f32[256,128]{1,0:T(8,128)S(1)}, f32[256,128]{1,0:T(8,128)S(1)}, u32[]{:S(2)}, u32[]{:S(2)}) collective-permute-start(f32[256,128]{1,0:T(8,128)S(1)} %get-tuple-element.101), channel_id=1, source_target_pairs={{0,2},{2,0},{4,6},{6,4},{8,10},{10,8},{12,14},{14,12},{16,18},{18,... | collective-permute-start | bytes 393224 | tf_op jit(solution)/shard_map/ppermute | solution.py:334
  107.8 2.3 %collective-permute-start.22 = (f32[256,128]{1,0:T(8,128)S(1)}, f32[256,128]{1,0:T(8,128)S(1)}, u32[]{:S(2)}, u32[]{:S(2)}) collective-permute-start(f32[256,128]{1,0:T(8,128)S(1)} %get-tuple-element.110), channel_id=1, source_target_pairs={{0,2},{2,0},{4,6},{6,4},{8,10},{10,8},{12,14},{14,12},{16,18},{18,... | collective-permute-start | bytes 393224 | tf_op jit(solution)/shard_map/ppermute | solution.py:334
  110.1 30.3 %all_to_all.10 = f32[32,1,128]{2,1,0:T(1,128)S(1)} all-to-all(f32[32,1,128]{2,1,0:T(1,128)S(1)} %bitcast.16), channel_id=1, replica_groups=mesh['x'=4,'yh'=2,'z'=16,'core'=2,'yl'=2] {'x','yh','core','yl'}, dimensions={0} | all-to-all | bytes 32768 | tf_op jit(solution)/shard_map/all_to_all | solution.py:441
  141.3 19.1 %all_to_all.11 = f32[16,1,128]{2,1,0:T(1,128)S(1)} all-to-all(f32[16,1,128]{2,1,0:T(1,128)S(1)} %broadcast_in_dim.2), channel_id=1, replica_groups=mesh['x'=4,'yh'=2,'z'=16,'core'=2,'yl'=2] {'z'}, dimensions={0} | all-to-all | bytes 16384 | tf_op jit(solution)/shard_map/all_to_all | solution.py:451
  (57 shorter events, 28.5 us)
Async XLA Ops:
  2.6 45.9 %copy-start.2 = (f32[264,128]{1,0:T(8,128)S(1)}, f32[264,128]{1,0:T(8,128)}, u32[]{:S(2)}) copy-start(f32[264,128]{1,0:T(8,128)} %get-tuple-element.66.own0) | copy-start | bytes 405508
  2.6 17.0 %collective-permute-start.4 = (f32[264,128]{1,0:T(8,128)}, f32[264,128]{1,0:T(8,128)S(1)}, u32[]{:S(2)}, u32[]{:S(2)}) collective-permute-start(f32[264,128]{1,0:T(8,128)} %get-tuple-element.67), channel_id=1, source_target_pairs={{0,6},{2,4},{4,10},{6,8},{8,14},{10,12},{12,18},{14,16},{16,22},{1... | collective-permute-start | bytes 405512 | tf_op jit(solution)/shard_map/ppermute | solution.py:334
  7.7 11.9 %collective-permute-start.3 = (f32[264,128]{1,0:T(8,128)}, f32[264,128]{1,0:T(8,128)S(1)}, u32[]{:S(2)}, u32[]{:S(2)}) collective-permute-start(f32[264,128]{1,0:T(8,128)} %get-tuple-element.66.own0), channel_id=1, source_target_pairs={{0,4},{2,6},{4,8},{6,10},{8,12},{10,14},{12,16},{14,18},{16,20},{1... | collective-permute-start | bytes 405512 | tf_op jit(solution)/shard_map/ppermute | solution.py:334
  11.3 15.1 %collective-permute-start.1 = (f32[264,128]{1,0:T(8,128)}, f32[264,128]{1,0:T(8,128)S(1)}, u32[]{:S(2)}, u32[]{:S(2)}) collective-permute-start(f32[264,128]{1,0:T(8,128)} %get-tuple-element.62), channel_id=1, source_target_pairs={{0,6},{2,4},{4,10},{6,8},{8,14},{10,12},{12,18},{14,16},{16,22},{1... | collective-permute-start | bytes 405512 | tf_op jit(solution)/shard_map/ppermute | solution.py:334
  14.8 11.6 %collective-permute-start = (f32[264,128]{1,0:T(8,128)}, f32[264,128]{1,0:T(8,128)S(1)}, u32[]{:S(2)}, u32[]{:S(2)}) collective-permute-start(f32[264,128]{1,0:T(8,128)} %get-tuple-element.61.own1), channel_id=1, source_target_pairs={{0,4},{2,6},{4,8},{6,10},{8,12},{10,14},{12,16},{14,18},{16,20},{1... | collective-permute-start | bytes 405512 | tf_op jit(solution)/shard_map/ppermute | solution.py:334
  19.6 13.2 %collective-permute-start.5 = (f32[520,128]{1,0:T(8,128)S(1)}, f32[520,128]{1,0:T(8,128)S(1)}, u32[]{:S(2)}, u32[]{:S(2)}) collective-permute-start(f32[520,128]{1,0:T(8,128)S(1)} %shard_map.87.refs_1_), channel_id=1, source_target_pairs={{0,4},{2,6},{4,8},{6,10},{8,12},{10,14},{12,16},{14,18},{16,20},{1... | collective-permute-start | bytes 798728 | tf_op jit(solution)/shard_map/ppermute | solution.py:334
  26.4 22.1 %collective-permute-start.2 = (f32[2,4,128,128]{3,2,1,0:T(8,128)}, f32[2,4,128,128]{3,2,1,0:T(8,128)S(1)}, u32[]{:S(2)}, u32[]{:S(2)}) collective-permute-start(f32[2,4,128,128]{3,2,1,0:T(8,128)} %get-tuple-element.65), channel_id=1, source_target_pairs={{0,2},{2,0},{4,6},{6,4},{8,10},{10,8},{12,14},{14,12},{16,18},{18,... | collective-permute-start | bytes 1572872 | tf_op jit(solution)/shard_map/ppermute | solution.py:334
  29.3 9.6 %collective-permute-start.8 = (f32[520,128]{1,0:T(8,128)S(1)}, f32[520,128]{1,0:T(8,128)S(1)}, u32[]{:S(2)}, u32[]{:S(2)}) collective-permute-start(f32[520,128]{1,0:T(8,128)S(1)} %shard_map.86.refs_1_), channel_id=1, source_target_pairs={{0,4},{2,6},{4,8},{6,10},{8,12},{10,14},{12,16},{14,18},{16,20},{1... | collective-permute-start | bytes 798728 | tf_op jit(solution)/shard_map/ppermute | solution.py:334
  32.9 11.5 %collective-permute-start.6 = (f32[520,128]{1,0:T(8,128)S(1)}, f32[520,128]{1,0:T(8,128)S(1)}, u32[]{:S(2)}, u32[]{:S(2)}) collective-permute-start(f32[520,128]{1,0:T(8,128)S(1)} %collective-permute-done.5.refs_2_), channel_id=1, source_target_pairs={{0,4},{2,6},{4,8},{6,10},{8,12},{10,14},{12,16},{14,18},{16,20},{1... | collective-permute-start | bytes 798728 | tf_op jit(solution)/shard_map/ppermute | solution.py:334
  36.4 12.0 %collective-permute-start.10 = (f32[520,128]{1,0:T(8,128)}, f32[520,128]{1,0:T(8,128)S(1)}, u32[]{:S(2)}, u32[]{:S(2)}) collective-permute-start(f32[520,128]{1,0:T(8,128)} %get-tuple-element.69), channel_id=1, source_target_pairs={{0,2},{2,0},{4,6},{6,4},{8,10},{10,8},{12,14},{14,12},{16,18},{18,... | collective-permute-start | bytes 798728 | tf_op jit(solution)/shard_map/ppermute | solution.py:334
  38.9 11.8 %collective-permute-start.9 = (f32[520,128]{1,0:T(8,128)S(1)}, f32[520,128]{1,0:T(8,128)S(1)}, u32[]{:S(2)}, u32[]{:S(2)}) collective-permute-start(f32[520,128]{1,0:T(8,128)S(1)} %collective-permute-done.8.refs_2_), channel_id=1, source_target_pairs={{0,4},{2,6},{4,8},{6,10},{8,12},{10,14},{12,16},{14,18},{16,20},{1... | collective-permute-start | bytes 798728 | tf_op jit(solution)/shard_map/ppermute | solution.py:334
  44.4 11.4 %collective-permute-start.7 = (f32[520,128]{1,0:T(8,128)S(1)}, f32[520,128]{1,0:T(8,128)S(1)}, u32[]{:S(2)}, u32[]{:S(2)}) collective-permute-start(f32[520,128]{1,0:T(8,128)S(1)} %collective-permute-done.6.refs_3_), channel_id=1, source_target_pairs={{0,4},{2,6},{4,8},{6,10},{8,12},{10,14},{12,16},{14,18},{16,20},{1... | collective-permute-start | bytes 798728 | tf_op jit(solution)/shard_map/ppermute | solution.py:334
  50.8 9.9 %collective-permute-start.15 = (f32[520,128]{1,0:T(8,128)S(1)}, f32[520,128]{1,0:T(8,128)S(1)}, u32[]{:S(2)}, u32[]{:S(2)}) collective-permute-start(f32[520,128]{1,0:T(8,128)S(1)} %collective-permute-done.9.refs_3_), channel_id=1, source_target_pairs={{0,4},{2,6},{4,8},{6,10},{8,12},{10,14},{12,16},{14,18},{16,20},{1... | collective-permute-start | bytes 798728 | tf_op jit(solution)/shard_map/ppermute | solution.py:334
  57.1 9.5 %collective-permute-start.11 = (f32[512,128]{1,0:T(8,128)S(1)}, f32[512,128]{1,0:T(8,128)S(1)}, u32[]{:S(2)}, u32[]{:S(2)}) collective-permute-start(f32[512,128]{1,0:T(8,128)S(1)} %get-tuple-element.75), channel_id=1, source_target_pairs={{4,0},{6,2},{8,4},{10,6},{12,8},{14,10},{16,12},{18,14},{20,16},{2... | collective-permute-start | bytes 786440 | tf_op jit(solution)/shard_map/ppermute | solution.py:334
  62.0 10.5 %collective-permute-start.17 = (f32[512,128]{1,0:T(8,128)S(1)}, f32[512,128]{1,0:T(8,128)S(1)}, u32[]{:S(2)}, u32[]{:S(2)}) collective-permute-start(f32[512,128]{1,0:T(8,128)S(1)} %get-tuple-element.97), channel_id=1, source_target_pairs={{4,0},{6,2},{8,4},{10,6},{12,8},{14,10},{16,12},{18,14},{20,16},{2... | collective-permute-start | bytes 786440 | tf_op jit(solution)/shard_map/ppermute | solution.py:334
  66.7 11.5 %collective-permute-start.12 = (f32[512,128]{1,0:T(8,128)S(1)}, f32[512,128]{1,0:T(8,128)S(1)}, u32[]{:S(2)}, u32[]{:S(2)}) collective-permute-start(f32[512,128]{1,0:T(8,128)S(1)} %add.26), channel_id=1, source_target_pairs={{4,0},{6,2},{8,4},{10,6},{12,8},{14,10},{16,12},{18,14},{20,16},{2... | collective-permute-start | bytes 786440 | tf_op jit(solution)/shard_map/ppermute | solution.py:334
  72.5 10.8 %collective-permute-start.18 = (f32[512,128]{1,0:T(8,128)S(1)}, f32[512,128]{1,0:T(8,128)S(1)}, u32[]{:S(2)}, u32[]{:S(2)}) collective-permute-start(f32[512,128]{1,0:T(8,128)S(1)} %add.29), channel_id=1, source_target_pairs={{4,0},{6,2},{8,4},{10,6},{12,8},{14,10},{16,12},{18,14},{20,16},{2... | collective-permute-start | bytes 786440 | tf_op jit(solution)/shard_map/ppermute | solution.py:334
  78.2 11.7 %collective-permute-start.13 = (f32[512,128]{1,0:T(8,128)S(1)}, f32[512,128]{1,0:T(8,128)S(1)}, u32[]{:S(2)}, u32[]{:S(2)}) collective-permute-start(f32[512,128]{1,0:T(8,128)S(1)} %add.27), channel_id=1, source_target_pairs={{4,0},{6,2},{8,4},{10,6},{12,8},{14,10},{16,12},{18,14},{20,16},{2... | collective-permute-start | bytes 786440 | tf_op jit(solution)/shard_map/ppermute | solution.py:334
  83.3 11.0 %collective-permute-start.19 = (f32[512,128]{1,0:T(8,128)S(1)}, f32[512,128]{1,0:T(8,128)S(1)}, u32[]{:S(2)}, u32[]{:S(2)}) collective-permute-start(f32[512,128]{1,0:T(8,128)S(1)} %add.30), channel_id=1, source_target_pairs={{4,0},{6,2},{8,4},{10,6},{12,8},{14,10},{16,12},{18,14},{20,16},{2... | collective-permute-start | bytes 786440 | tf_op jit(solution)/shard_map/ppermute | solution.py:334
  84.7 11.1 %collective-permute-start.16 = (f32[4,128,128]{2,1,0:T(8,128)S(1)}, f32[4,128,128]{2,1,0:T(8,128)S(1)}, u32[]{:S(2)}, u32[]{:S(2)}) collective-permute-start(f32[4,128,128]{2,1,0:T(8,128)S(1)} %pad_maximum_fusion.1), channel_id=1, source_target_pairs={{0,2},{2,0},{4,6},{6,4},{8,10},{10,8},{12,14},{14,12},{16,18},{18,... | collective-permute-start | bytes 786440 | tf_op jit(solution)/shard_map/ppermute | solution.py:334
  89.9 9.8 %collective-permute-start.14 = (f32[512,128]{1,0:T(8,128)S(1)}, f32[512,128]{1,0:T(8,128)S(1)}, u32[]{:S(2)}, u32[]{:S(2)}) collective-permute-start(f32[512,128]{1,0:T(8,128)S(1)} %add.28), channel_id=1, source_target_pairs={{4,0},{6,2},{8,4},{10,6},{12,8},{14,10},{16,12},{18,14},{20,16},{2... | collective-permute-start | bytes 786440 | tf_op jit(solution)/shard_map/ppermute | solution.py:334
  94.4 12.4 %collective-permute-start.20 = (f32[512,128]{1,0:T(8,128)S(1)}, f32[512,128]{1,0:T(8,128)S(1)}, u32[]{:S(2)}, u32[]{:S(2)}) collective-permute-start(f32[512,128]{1,0:T(8,128)S(1)} %add.31), channel_id=1, source_target_pairs={{4,0},{6,2},{8,4},{10,6},{12,8},{14,10},{16,12},{18,14},{20,16},{2... | collective-permute-start | bytes 786440 | tf_op jit(solution)/shard_map/ppermute | solution.py:334
  100.7 7.0 %collective-permute-start.21 = (f32[256,128]{1,0:T(8,128)S(1)}, f32[256,128]{1,0:T(8,128)S(1)}, u32[]{:S(2)}, u32[]{:S(2)}) collective-permute-start(f32[256,128]{1,0:T(8,128)S(1)} %get-tuple-element.101), channel_id=1, source_target_pairs={{0,2},{2,0},{4,6},{6,4},{8,10},{10,8},{12,14},{14,12},{16,18},{18,... | collective-permute-start | bytes 393224 | tf_op jit(solution)/shard_map/ppermute | solution.py:334
  107.8 32.6 %collective-permute-start.22 = (f32[256,128]{1,0:T(8,128)S(1)}, f32[256,128]{1,0:T(8,128)S(1)}, u32[]{:S(2)}, u32[]{:S(2)}) collective-permute-start(f32[256,128]{1,0:T(8,128)S(1)} %get-tuple-element.110), channel_id=1, source_target_pairs={{0,2},{2,0},{4,6},{6,4},{8,10},{10,8},{12,14},{14,12},{16,18},{18,... | collective-permute-start | bytes 393224 | tf_op jit(solution)/shard_map/ppermute | solution.py:334
  (3 other events, 48.0 us)

commit v5 on v4

--- a/solution.py
+++ b/solution.py
@@ -273,24 +273,16 @@
         dq_sib[mate] = total[:, (2 * mate + 1) * TOK : (2 * mate + 2) * TOK].T
 
 
-def finish(got, own, keep_ref, give_ref, squares):
+def end_kernel(got0, got1, own0, own1, squares0, squares1, keep_ref, give_ref, row_ref):
     total = jnp.zeros((8, TOK), F32)
-    for kind in range(2):
-        for half, out in ((0, keep_ref), (1, give_ref)):
-            rows = pl.ds(kind * CHIP + half * TOK, TOK)
-            grad = got[rows, :] + own[rows, :]
-            out[pl.ds(kind * TOK, TOK), :] = grad
-            total = total + jnp.sum((grad * grad).reshape(TOK // 8, 8, TOK), axis=0)
-    return jnp.sum(total, axis=0, keepdims=True) + squares[0:1, :] * (1.0 / TOK)
-
-
-def first_end_kernel(core_ref, got, own, squares, dq_own, dq_far, keep_ref, give_ref, row_ref, q_out):
-    row_ref[...] = jnp.broadcast_to(finish(got, own, keep_ref, give_ref, squares), row_ref.shape)
-    place_q(core_ref, dq_own, dq_far, q_out)
-
-
-def second_end_kernel(got, own, squares, before, keep_ref, give_ref, row_ref):
-    row = finish(got, own, keep_ref, give_ref, squares) + before[0:1, :]
+    for head, (got, own) in enumerate(((got0, own0), (got1, own1))):
+        for kind in range(2):
+            for half, out in enumerate((keep_ref, give_ref)):
+                rows = pl.ds(kind * CHIP + half * TOK, TOK)
+                grad = got[rows, :] + own[rows, :]
+                out[pl.ds((2 * head + kind) * TOK, TOK), :] = grad
+                total = total + jnp.sum((grad * grad).reshape(TOK // 8, 8, TOK), axis=0)
+    row = jnp.sum(total, axis=0, keepdims=True) + (squares0[0:1, :] + squares1[0:1, :]) * (1.0 / TOK)
     row_ref[...] = jnp.broadcast_to(row, row_ref.shape)
 
 
@@ -305,16 +297,17 @@
                     q_out[pl.ds(4 * where + head, TOK, stride=8), :] = source[head]
 
 
-def place_kv_kernel(core_ref, own0, own1, far0, far1, k_out, v_out):
+def place_kv_kernel(core_ref, own_ref, far_ref, k_out, v_out):
     core = core_ref[0]
     for side in range(2):
 
         @pl.when(core == side)
         def _():
-            for sources, where in (((own0, own1), side), ((far0, far1), 1 - side)):
-                for head, source in enumerate(sources):
+            for source, where in ((own_ref, side), (far_ref, 1 - side)):
+                for head in range(2):
                     for kind, out in enumerate((k_out, v_out)):
-                        out[pl.ds(2 * where + head, TOK, stride=4), :] = source[pl.ds(kind * TOK, TOK), :]
+                        rows = pl.ds((2 * head + kind) * TOK, TOK)
+                        out[pl.ds(2 * where + head, TOK, stride=4), :] = source[rows, :]
 
 
 def shards(sizes, queries, key_states, value_states, out_grad, step_begins):
@@ -405,6 +398,8 @@
             moved=2 << 20,
         )(chip, core, qd_own, qd_far, ring[REACH], stat)
         got.append(send(grad, -1))
+        if head:
+            got[0], p = lax.optimization_barrier((got[0] + grads[0][REACH - 1], p))
         out = call(
             functools.partial(back_kernel, head, width),
             (sds(BODY, width),) * REACH + (sds(2, TOK, width), sds(2, TOK, width), sds(8, TOK)),
@@ -416,37 +411,40 @@
         )(qd_own, qd_far, *ring[:REACH], p, dp, dq4, stat2)
         grads.append(out[:REACH])
         rest.append(out[REACH:])
+    got[1] = got[1] + grads[1][REACH - 1]
     dq_own = jnp.concatenate([rest[0][0], rest[1][0]], axis=0)
     dq_far = send(jnp.concatenate([rest[0][1], rest[1][1]], axis=0), 0, 1)
-    for distance in range(REACH - 1, 0, -1):
-        got = [send(far + own[distance], -1) for far, own in zip(got, grads)]
-    slot = whole(CHIP, width)
-    keep0, give0, row, dq = call(
-        first_end_kernel,
-        (sds(CHIP, width), sds(CHIP, width), sds(8, width), sds(tokens * heads, width)),
-        [SCALAR, body, body, whole(8, TOK)] + [whole(4, TOK, width)] * 2,
-        (slot, slot, whole(8, width), whole(tokens * heads, width)),
+    dq = call(
+        place_q,
+        sds(tokens * heads, width),
+        [SCALAR] + [whole(4, TOK, width)] * 2,
+        whole(tokens * heads, width),
+        moved=1 << 20,
+    )(core, dq_own, dq_far)
+    for distance in range(REACH - 2, -1, -1):
+        got = [send(far, -1) for far in got]
+        if distance == 0:
+            break
+        got = [far + own[distance] for far, own in zip(got, grads)]
+        if distance == 1:
+            got[0], dq = lax.optimization_barrier((got[0], dq))
+    keep, give, row = call(
+        end_kernel,
+        (sds(BODY, width), sds(BODY, width), sds(plane, width)),
+        [body] * 4 + [whole(8, TOK)] * 2,
+        (body, body, whole(plane, width)),
         moved=2 << 20,
-    )(core, got[0], grads[0][0], rest[0][2], dq_own, dq_far)
-    far0 = send(give0, 0, 1)
-    got[1], far0 = lax.optimization_barrier((got[1], far0))
-    keep1, give1, row = call(
-        second_end_kernel,
-        (sds(CHIP, width), sds(CHIP, width), sds(plane, width)),
-        [body, body, whole(8, TOK), whole(8, width)],
-        (slot, slot, whole(plane, width)),
-        moved=1 << 20,
-    )(got[1], grads[1][0], rest[1][2], row)
-    far1 = send(give1, 0, 1)
+    )(got[0], got[1], grads[0][0], grads[1][0], rest[0][2], rest[1][2])
+    far = send(give, 0, 1)
     parts = lax.all_to_all(row.reshape(plane, 1, width), ("x", "yh", "core", "yl"), 0, 0)
     parts = jnp.broadcast_to(jnp.sum(parts, axis=0, keepdims=True), (sizes["z"], 1, width))
     dk, dv = call(
         place_kv_kernel,
         (sds(tokens * groups, width), sds(tokens * groups, width)),
-        [SCALAR] + [slot] * 4,
+        [SCALAR] + [body] * 2,
         (whole(tokens * groups, width), whole(tokens * groups, width)),
         moved=1 << 20,
-    )(core, keep0, keep1, far0, far1)
+    )(core, keep, far)
     parts, dk, dv = lax.optimization_barrier((parts, dk, dv))
     parts = lax.all_to_all(parts, "z", 0, 0)
     entries = chips * sizes["core"] * sizes["yl"] * tokens * (heads + 2 * groups) * width

time: 164 us -> 162 us (0.988)
  starting transfers between devices: 70 us -> 65.7 us
  waiting for transfers between devices: 20.4 us -> 24.5 us
    ppermute x23 -> x22, starting transfers between devices: 70 us -> 65.7 us  [send(): return lax.ppermute(value, CTX, pairs)]
    ppermute x23 -> x22, waiting for transfers between devices: 20.4 us -> 24.5 us  [send(): return lax.ppermute(value, CTX, pairs)]
  transfers between devices with their start and end apart: 23 -> 22, of which waited for: 9 -> 9; matrix products, arithmetic and copies ran while one was open for 0% -> 0% of each run, Pallas kernels for 9% -> 9%
where the time goes in v5:
time: 162 us
  starting transfers between devices  65.7 us (41%)
  blocking collectives  48.4 us (30%)
  waiting for transfers between devices  24.5 us (15%)
  Pallas kernels  17.2 us (11%)
  between operations  2.82 us (2%)
  local copies, waits for them, and re-layouts  2.1 us (1%)
    ppermute x22, starting transfers between devices, send(): return lax.ppermute(value, CTX, pairs)  65.7 us
    all_to_all x1, blocking collectives, shards(): lax.all_to_all(row.reshape(plane, 1, width), ('x', 'yh', 'core', 'yl'), 0...  29.4 us
    ppermute x22, waiting for transfers between devices, send(): return lax.ppermute(value, CTX, pairs)  24.5 us
    all_to_all x1, blocking collectives, shards(): parts = lax.all_to_all(parts, 'z', 0, 0)  19.1 us
    pallas_call x2, Pallas kernels, shards(): call(functools.partial(back_kernel, head, width), (sds(BODY, width),) * R...  5.08 us
    pallas_call x2, Pallas kernels, shards(): call(functools.partial(near_kernel, head, width), (sds(REACH * CHIP, ROWS...  4.33 us
  transfers between devices with their start and end apart: 22, of which 9 were waited for; matrix products, arithmetic and copies ran while one was open for 0% of the time, Pallas kernels for 9%

profile of v5, /device:TPU:1, one launch (start us, length us, event | category | flops | bytes accessed | tf_op | source)
XLA Modules:
  0.0 161.6 jit_solution(11029210636485874808)
XLA Ops:
  2.7 5.1 %collective-permute-start.4 = (f32[264,128]{1,0:T(8,128)}, f32[264,128]{1,0:T(8,128)S(1)}, u32[]{:S(2)}, u32[]{:S(2)}) collective-permute-start(f32[264,128]{1,0:T(8,128)} %get-tuple-element.65), channel_id=1, source_target_pairs={{0,6},{2,4},{4,10},{6,8},{8,14},{10,12},{12,18},{14,16},{16,22},{1... | collective-permute-start | bytes 405512 | tf_op jit(solution)/shard_map/ppermute | solution.py:327
  7.7 3.5 %collective-permute-start.3 = (f32[264,128]{1,0:T(8,128)}, f32[264,128]{1,0:T(8,128)S(1)}, u32[]{:S(2)}, u32[]{:S(2)}) collective-permute-start(f32[264,128]{1,0:T(8,128)} %get-tuple-element.64.own0), channel_id=1, source_target_pairs={{0,4},{2,6},{4,8},{6,10},{8,12},{10,14},{12,16},{14,18},{16,20},{1... | collective-permute-start | bytes 405512 | tf_op jit(solution)/shard_map/ppermute | solution.py:327
  11.3 3.5 %collective-permute-start.1 = (f32[264,128]{1,0:T(8,128)}, f32[264,128]{1,0:T(8,128)S(1)}, u32[]{:S(2)}, u32[]{:S(2)}) collective-permute-start(f32[264,128]{1,0:T(8,128)} %get-tuple-element.60), channel_id=1, source_target_pairs={{0,6},{2,4},{4,10},{6,8},{8,14},{10,12},{12,18},{14,16},{16,22},{1... | collective-permute-start | bytes 405512 | tf_op jit(solution)/shard_map/ppermute | solution.py:327
  14.8 4.8 %collective-permute-start = (f32[264,128]{1,0:T(8,128)}, f32[264,128]{1,0:T(8,128)S(1)}, u32[]{:S(2)}, u32[]{:S(2)}) collective-permute-start(f32[264,128]{1,0:T(8,128)} %get-tuple-element.59.own1), channel_id=1, source_target_pairs={{0,4},{2,6},{4,8},{6,10},{8,12},{10,14},{12,16},{14,18},{16,20},{1... | collective-permute-start | bytes 405512 | tf_op jit(solution)/shard_map/ppermute | solution.py:327
  19.7 3.6 %collective-permute-start.5 = (f32[520,128]{1,0:T(8,128)S(1)}, f32[520,128]{1,0:T(8,128)S(1)}, u32[]{:S(2)}, u32[]{:S(2)}) collective-permute-start(f32[520,128]{1,0:T(8,128)S(1)} %shard_map.87.refs_1_), channel_id=1, source_target_pairs={{0,4},{2,6},{4,8},{6,10},{8,12},{10,14},{12,16},{14,18},{16,20},{1... | collective-permute-start | bytes 798728 | tf_op jit(solution)/shard_map/ppermute | solution.py:327
  26.4 2.9 %collective-permute-start.2 = (f32[2,4,128,128]{3,2,1,0:T(8,128)}, f32[2,4,128,128]{3,2,1,0:T(8,128)S(1)}, u32[]{:S(2)}, u32[]{:S(2)}) collective-permute-start(f32[2,4,128,128]{3,2,1,0:T(8,128)} %get-tuple-element.63), channel_id=1, source_target_pairs={{0,2},{2,0},{4,6},{6,4},{8,10},{10,8},{12,14},{14,12},{16,18},{18,... | collective-permute-start | bytes 1572872 | tf_op jit(solution)/shard_map/ppermute | solution.py:327
  29.3 3.5 %collective-permute-start.8 = (f32[520,128]{1,0:T(8,128)S(1)}, f32[520,128]{1,0:T(8,128)S(1)}, u32[]{:S(2)}, u32[]{:S(2)}) collective-permute-start(f32[520,128]{1,0:T(8,128)S(1)} %shard_map.86.refs_1_), channel_id=1, source_target_pairs={{0,4},{2,6},{4,8},{6,10},{8,12},{10,14},{12,16},{14,18},{16,20},{1... | collective-permute-start | bytes 798728 | tf_op jit(solution)/shard_map/ppermute | solution.py:327
  32.9 3.5 %collective-permute-start.6 = (f32[520,128]{1,0:T(8,128)S(1)}, f32[520,128]{1,0:T(8,128)S(1)}, u32[]{:S(2)}, u32[]{:S(2)}) collective-permute-start(f32[520,128]{1,0:T(8,128)S(1)} %collective-permute-done.5.refs_2_), channel_id=1, source_target_pairs={{0,4},{2,6},{4,8},{6,10},{8,12},{10,14},{12,16},{14,18},{16,20},{1... | collective-permute-start | bytes 798728 | tf_op jit(solution)/shard_map/ppermute | solution.py:327
  36.5 2.5 %collective-permute-start.10 = (f32[520,128]{1,0:T(8,128)}, f32[520,128]{1,0:T(8,128)S(1)}, u32[]{:S(2)}, u32[]{:S(2)}) collective-permute-start(f32[520,128]{1,0:T(8,128)} %get-tuple-element.67), channel_id=1, source_target_pairs={{0,2},{2,0},{4,6},{6,4},{8,10},{10,8},{12,14},{14,12},{16,18},{18,... | collective-permute-start | bytes 798728 | tf_op jit(solution)/shard_map/ppermute | solution.py:327
  39.0 4.8 %collective-permute-start.9 = (f32[520,128]{1,0:T(8,128)S(1)}, f32[520,128]{1,0:T(8,128)S(1)}, u32[]{:S(2)}, u32[]{:S(2)}) collective-permute-start(f32[520,128]{1,0:T(8,128)S(1)} %collective-permute-done.8.refs_2_), channel_id=1, source_target_pairs={{0,4},{2,6},{4,8},{6,10},{8,12},{10,14},{12,16},{14,18},{16,20},{1... | collective-permute-start | bytes 798728 | tf_op jit(solution)/shard_map/ppermute | solution.py:327
  44.4 4.1 %collective-permute-start.7 = (f32[520,128]{1,0:T(8,128)S(1)}, f32[520,128]{1,0:T(8,128)S(1)}, u32[]{:S(2)}, u32[]{:S(2)}) collective-permute-start(f32[520,128]{1,0:T(8,128)S(1)} %collective-permute-done.6.refs_3_), channel_id=1, source_target_pairs={{0,4},{2,6},{4,8},{6,10},{8,12},{10,14},{12,16},{14,18},{16,20},{1... | collective-permute-start | bytes 798728 | tf_op jit(solution)/shard_map/ppermute | solution.py:327
  48.6 2.2 %shard_map.89 = (f32[1024,512]{1,0:T(8,128)S(1)}, f32[1024,512]{1,0:T(8,128)S(1)}, f32[8,512]{1,0:T(8,128)S(1)}) custom-call(s32[1]{0:T(128)} %bitcast.chip_ref, s32[1]{0:T(128)} %bitcast.1.core_ref, f32[2,4,128,128]{3,2,1,0:T(8,128)S(1)} %get-tuple-element.58.own_ref, f32[2,4,128,128]{3,2,1,0:T(8,128)S(1)} %collective-permute-done.2.far_ref, ...), custom_call_target="tpu_custom_call" | custom-call | flops 805306368 | bytes 6291456 | tf_op jit(solution)/shard_map/pallas_call | solution.py:380
  50.8 4.2 %collective-permute-start.14 = (f32[520,128]{1,0:T(8,128)S(1)}, f32[520,128]{1,0:T(8,128)S(1)}, u32[]{:S(2)}, u32[]{:S(2)}) collective-permute-start(f32[520,128]{1,0:T(8,128)S(1)} %collective-permute-done.9.refs_3_), channel_id=1, source_target_pairs={{0,4},{2,6},{4,8},{6,10},{8,12},{10,14},{12,16},{14,18},{16,20},{1... | collective-permute-start | bytes 798728 | tf_op jit(solution)/shard_map/ppermute | solution.py:327
  63.3 2.5 %shard_map.91 = (f32[512,128]{1,0:T(8,128)S(1)}, f32[512,128]{1,0:T(8,128)S(1)}, f32[512,128]{1,0:T(8,128)S(1)}, f32[512,128]{1,0:T(8,128)S(1)}, f32[2,128,128]{...) custom-call(f32[2,4,128,128]{3,2,1,0:T(8,128)S(1)} %get-tuple-element.58.own_ref, ...), custom_call_target="tpu_custom_call" | custom-call | flops 1207959552 | bytes 7340032 | tf_op jit(solution)/shard_map/pallas_call | solution.py:403
  68.2 2.5 %shard_map.94 = (f32[512,128]{1,0:T(8,128)S(1)}, f32[512,128]{1,0:T(8,128)S(1)}, f32[512,128]{1,0:T(8,128)S(1)}, f32[512,128]{1,0:T(8,128)S(1)}, f32[2,128,128]{...) custom-call(f32[2,4,128,128]{3,2,1,0:T(8,128)S(1)} %get-tuple-element.58.own_ref, ...), custom_call_target="tpu_custom_call" | custom-call | flops 1207959552 | bytes 7340032 | tf_op jit(solution)/shard_map/pallas_call | solution.py:403
  73.8 4.8 %collective-permute-start.15 = (f32[4,128,128]{2,1,0:T(8,128)S(1)}, f32[4,128,128]{2,1,0:T(8,128)S(1)}, u32[]{:S(2)}, u32[]{:S(2)}) collective-permute-start(f32[4,128,128]{2,1,0:T(8,128)S(1)} %pad_maximum_fusion.1), channel_id=1, source_target_pairs={{0,2},{2,0},{4,6},{6,4},{8,10},{10,8},{12,14},{14,12},{16,18},{18,... | collective-permute-start | bytes 786440 | tf_op jit(solution)/shard_map/ppermute | solution.py:327
  79.9 3.4 %collective-permute-done.18 = f32[512,128]{1,0:T(8,128)S(1)} collective-permute-done((f32[512,128]{1,0:T(8,128)S(1)}, f32[512,128]{1,0:T(8,128)S(1)}, u32[]{:S(2)}, u32[]{:S(2)}) %collective-permute-start.18) | collective-permute-done | bytes 262176 | tf_op jit(solution)/shard_map/ppermute | solution.py:327
  85.6 3.3 %collective-permute-done.13 = f32[512,128]{1,0:T(8,128)S(1)} collective-permute-done((f32[512,128]{1,0:T(8,128)S(1)}, f32[512,128]{1,0:T(8,128)S(1)}, u32[]{:S(2)}, u32[]{:S(2)}) %collective-permute-start.13) | collective-permute-done | bytes 262176 | tf_op jit(solution)/shard_map/ppermute | solution.py:327
  90.2 4.3 %collective-permute-done.19 = f32[512,128]{1,0:T(8,128)S(1)} collective-permute-done((f32[512,128]{1,0:T(8,128)S(1)}, f32[512,128]{1,0:T(8,128)S(1)}, u32[]{:S(2)}, u32[]{:S(2)}) %collective-permute-start.19) | collective-permute-done | bytes 262176 | tf_op jit(solution)/shard_map/ppermute | solution.py:327
  95.9 3.9 %collective-permute-done.16.got0 = f32[512,128]{1,0:T(8,128)S(1)} collective-permute-done((f32[512,128]{1,0:T(8,128)S(1)}, f32[512,128]{1,0:T(8,128)S(1)}, u32[]{:S(2)}, u32[]{:S(2)}) %collective-permute-start.16) | collective-permute-done | bytes 262176 | tf_op jit(solution)/shard_map/ppermute | solution.py:327
  99.7 5.6 %collective-permute-done.20.got1 = f32[512,128]{1,0:T(8,128)S(1)} collective-permute-done((f32[512,128]{1,0:T(8,128)S(1)}, f32[512,128]{1,0:T(8,128)S(1)}, u32[]{:S(2)}, u32[]{:S(2)}) %collective-permute-start.20) | collective-permute-done | bytes 262176 | tf_op jit(solution)/shard_map/ppermute | solution.py:327
  105.4 4.4 %collective-permute-start.21 = (f32[512,128]{1,0:T(8,128)S(1)}, f32[512,128]{1,0:T(8,128)S(1)}, u32[]{:S(2)}, u32[]{:S(2)}) collective-permute-start(f32[512,128]{1,0:T(8,128)S(1)} %get-tuple-element.106), channel_id=1, source_target_pairs={{0,2},{2,0},{4,6},{6,4},{8,10},{10,8},{12,14},{14,12},{16,18},{18,... | collective-permute-start | bytes 786440 | tf_op jit(solution)/shard_map/ppermute | solution.py:327
  109.8 29.4 %all_to_all.10 = f32[32,1,128]{2,1,0:T(1,128)S(1)} all-to-all(f32[32,1,128]{2,1,0:T(1,128)S(1)} %bitcast.16), channel_id=1, replica_groups=mesh['x'=4,'yh'=2,'z'=16,'core'=2,'yl'=2] {'x','yh','core','yl'}, dimensions={0} | all-to-all | bytes 32768 | tf_op jit(solution)/shard_map/all_to_all | solution.py:439
  140.1 19.1 %all_to_all.11 = f32[16,1,128]{2,1,0:T(1,128)S(1)} all-to-all(f32[16,1,128]{2,1,0:T(1,128)S(1)} %broadcast_in_dim.2), channel_id=1, replica_groups=mesh['x'=4,'yh'=2,'z'=16,'core'=2,'yl'=2] {'z'}, dimensions={0} | all-to-all | bytes 16384 | tf_op jit(solution)/shard_map/all_to_all | solution.py:449
  (55 shorter events, 27.5 us)
Async XLA Ops:
  2.6 45.9 %copy-start.2 = (f32[264,128]{1,0:T(8,128)S(1)}, f32[264,128]{1,0:T(8,128)}, u32[]{:S(2)}) copy-start(f32[264,128]{1,0:T(8,128)} %get-tuple-element.64.own0) | copy-start | bytes 405508
  2.6 45.9 %copy-start.3 = (f32[264,128]{1,0:T(8,128)S(1)}, f32[264,128]{1,0:T(8,128)}, u32[]{:S(2)}) copy-start(f32[264,128]{1,0:T(8,128)} %get-tuple-element.59.own1) | copy-start | bytes 405508
  2.7 17.0 %collective-permute-start.4 = (f32[264,128]{1,0:T(8,128)}, f32[264,128]{1,0:T(8,128)S(1)}, u32[]{:S(2)}, u32[]{:S(2)}) collective-permute-start(f32[264,128]{1,0:T(8,128)} %get-tuple-element.65), channel_id=1, source_target_pairs={{0,6},{2,4},{4,10},{6,8},{8,14},{10,12},{12,18},{14,16},{16,22},{1... | collective-permute-start | bytes 405512 | tf_op jit(solution)/shard_map/ppermute | solution.py:327
  7.7 11.9 %collective-permute-start.3 = (f32[264,128]{1,0:T(8,128)}, f32[264,128]{1,0:T(8,128)S(1)}, u32[]{:S(2)}, u32[]{:S(2)}) collective-permute-start(f32[264,128]{1,0:T(8,128)} %get-tuple-element.64.own0), channel_id=1, source_target_pairs={{0,4},{2,6},{4,8},{6,10},{8,12},{10,14},{12,16},{14,18},{16,20},{1... | collective-permute-start | bytes 405512 | tf_op jit(solution)/shard_map/ppermute | solution.py:327
  11.3 15.1 %collective-permute-start.1 = (f32[264,128]{1,0:T(8,128)}, f32[264,128]{1,0:T(8,128)S(1)}, u32[]{:S(2)}, u32[]{:S(2)}) collective-permute-start(f32[264,128]{1,0:T(8,128)} %get-tuple-element.60), channel_id=1, source_target_pairs={{0,6},{2,4},{4,10},{6,8},{8,14},{10,12},{12,18},{14,16},{16,22},{1... | collective-permute-start | bytes 405512 | tf_op jit(solution)/shard_map/ppermute | solution.py:327
  14.8 11.6 %collective-permute-start = (f32[264,128]{1,0:T(8,128)}, f32[264,128]{1,0:T(8,128)S(1)}, u32[]{:S(2)}, u32[]{:S(2)}) collective-permute-start(f32[264,128]{1,0:T(8,128)} %get-tuple-element.59.own1), channel_id=1, source_target_pairs={{0,4},{2,6},{4,8},{6,10},{8,12},{10,14},{12,16},{14,18},{16,20},{1... | collective-permute-start | bytes 405512 | tf_op jit(solution)/shard_map/ppermute | solution.py:327
  19.7 13.2 %collective-permute-start.5 = (f32[520,128]{1,0:T(8,128)S(1)}, f32[520,128]{1,0:T(8,128)S(1)}, u32[]{:S(2)}, u32[]{:S(2)}) collective-permute-start(f32[520,128]{1,0:T(8,128)S(1)} %shard_map.87.refs_1_), channel_id=1, source_target_pairs={{0,4},{2,6},{4,8},{6,10},{8,12},{10,14},{12,16},{14,18},{16,20},{1... | collective-permute-start | bytes 798728 | tf_op jit(solution)/shard_map/ppermute | solution.py:327
  26.4 22.1 %collective-permute-start.2 = (f32[2,4,128,128]{3,2,1,0:T(8,128)}, f32[2,4,128,128]{3,2,1,0:T(8,128)S(1)}, u32[]{:S(2)}, u32[]{:S(2)}) collective-permute-start(f32[2,4,128,128]{3,2,1,0:T(8,128)} %get-tuple-element.63), channel_id=1, source_target_pairs={{0,2},{2,0},{4,6},{6,4},{8,10},{10,8},{12,14},{14,12},{16,18},{18,... | collective-permute-start | bytes 1572872 | tf_op jit(solution)/shard_map/ppermute | solution.py:327
  29.3 9.6 %collective-permute-start.8 = (f32[520,128]{1,0:T(8,128)S(1)}, f32[520,128]{1,0:T(8,128)S(1)}, u32[]{:S(2)}, u32[]{:S(2)}) collective-permute-start(f32[520,128]{1,0:T(8,128)S(1)} %shard_map.86.refs_1_), channel_id=1, source_target_pairs={{0,4},{2,6},{4,8},{6,10},{8,12},{10,14},{12,16},{14,18},{16,20},{1... | collective-permute-start | bytes 798728 | tf_op jit(solution)/shard_map/ppermute | solution.py:327
  32.9 11.5 %collective-permute-start.6 = (f32[520,128]{1,0:T(8,128)S(1)}, f32[520,128]{1,0:T(8,128)S(1)}, u32[]{:S(2)}, u32[]{:S(2)}) collective-permute-start(f32[520,128]{1,0:T(8,128)S(1)} %collective-permute-done.5.refs_2_), channel_id=1, source_target_pairs={{0,4},{2,6},{4,8},{6,10},{8,12},{10,14},{12,16},{14,18},{16,20},{1... | collective-permute-start | bytes 798728 | tf_op jit(solution)/shard_map/ppermute | solution.py:327
  36.5 12.0 %collective-permute-start.10 = (f32[520,128]{1,0:T(8,128)}, f32[520,128]{1,0:T(8,128)S(1)}, u32[]{:S(2)}, u32[]{:S(2)}) collective-permute-start(f32[520,128]{1,0:T(8,128)} %get-tuple-element.67), channel_id=1, source_target_pairs={{0,2},{2,0},{4,6},{6,4},{8,10},{10,8},{12,14},{14,12},{16,18},{18,... | collective-permute-start | bytes 798728 | tf_op jit(solution)/shard_map/ppermute | solution.py:327
  39.0 11.8 %collective-permute-start.9 = (f32[520,128]{1,0:T(8,128)S(1)}, f32[520,128]{1,0:T(8,128)S(1)}, u32[]{:S(2)}, u32[]{:S(2)}) collective-permute-start(f32[520,128]{1,0:T(8,128)S(1)} %collective-permute-done.8.refs_2_), channel_id=1, source_target_pairs={{0,4},{2,6},{4,8},{6,10},{8,12},{10,14},{12,16},{14,18},{16,20},{1... | collective-permute-start | bytes 798728 | tf_op jit(solution)/shard_map/ppermute | solution.py:327
  44.4 11.4 %collective-permute-start.7 = (f32[520,128]{1,0:T(8,128)S(1)}, f32[520,128]{1,0:T(8,128)S(1)}, u32[]{:S(2)}, u32[]{:S(2)}) collective-permute-start(f32[520,128]{1,0:T(8,128)S(1)} %collective-permute-done.6.refs_3_), channel_id=1, source_target_pairs={{0,4},{2,6},{4,8},{6,10},{8,12},{10,14},{12,16},{14,18},{16,20},{1... | collective-permute-start | bytes 798728 | tf_op jit(solution)/shard_map/ppermute | solution.py:327
  50.8 9.9 %collective-permute-start.14 = (f32[520,128]{1,0:T(8,128)S(1)}, f32[520,128]{1,0:T(8,128)S(1)}, u32[]{:S(2)}, u32[]{:S(2)}) collective-permute-start(f32[520,128]{1,0:T(8,128)S(1)} %collective-permute-done.9.refs_3_), channel_id=1, source_target_pairs={{0,4},{2,6},{4,8},{6,10},{8,12},{10,14},{12,16},{14,18},{16,20},{1... | collective-permute-start | bytes 798728 | tf_op jit(solution)/shard_map/ppermute | solution.py:327
  57.2 9.5 %collective-permute-start.11 = (f32[512,128]{1,0:T(8,128)S(1)}, f32[512,128]{1,0:T(8,128)S(1)}, u32[]{:S(2)}, u32[]{:S(2)}) collective-permute-start(f32[512,128]{1,0:T(8,128)S(1)} %get-tuple-element.73), channel_id=1, source_target_pairs={{4,0},{6,2},{8,4},{10,6},{12,8},{14,10},{16,12},{18,14},{20,16},{2... | collective-permute-start | bytes 786440 | tf_op jit(solution)/shard_map/ppermute | solution.py:327
  62.0 10.4 %collective-permute-start.17 = (f32[512,128]{1,0:T(8,128)S(1)}, f32[512,128]{1,0:T(8,128)S(1)}, u32[]{:S(2)}, u32[]{:S(2)}) collective-permute-start(f32[512,128]{1,0:T(8,128)S(1)} %get-tuple-element.96), channel_id=1, source_target_pairs={{4,0},{6,2},{8,4},{10,6},{12,8},{14,10},{16,12},{18,14},{20,16},{2... | collective-permute-start | bytes 786440 | tf_op jit(solution)/shard_map/ppermute | solution.py:327
  66.7 11.9 %collective-permute-start.12 = (f32[512,128]{1,0:T(8,128)S(1)}, f32[512,128]{1,0:T(8,128)S(1)}, u32[]{:S(2)}, u32[]{:S(2)}) collective-permute-start(f32[512,128]{1,0:T(8,128)S(1)} %add.26), channel_id=1, source_target_pairs={{4,0},{6,2},{8,4},{10,6},{12,8},{14,10},{16,12},{18,14},{20,16},{2... | collective-permute-start | bytes 786440 | tf_op jit(solution)/shard_map/ppermute | solution.py:327
  72.5 10.8 %collective-permute-start.18 = (f32[512,128]{1,0:T(8,128)S(1)}, f32[512,128]{1,0:T(8,128)S(1)}, u32[]{:S(2)}, u32[]{:S(2)}) collective-permute-start(f32[512,128]{1,0:T(8,128)S(1)} %add.29), channel_id=1, source_target_pairs={{4,0},{6,2},{8,4},{10,6},{12,8},{14,10},{16,12},{18,14},{20,16},{2... | collective-permute-start | bytes 786440 | tf_op jit(solution)/shard_map/ppermute | solution.py:327
  73.8 10.9 %collective-permute-start.15 = (f32[4,128,128]{2,1,0:T(8,128)S(1)}, f32[4,128,128]{2,1,0:T(8,128)S(1)}, u32[]{:S(2)}, u32[]{:S(2)}) collective-permute-start(f32[4,128,128]{2,1,0:T(8,128)S(1)} %pad_maximum_fusion.1), channel_id=1, source_target_pairs={{0,2},{2,0},{4,6},{6,4},{8,10},{10,8},{12,14},{14,12},{16,18},{18,... | collective-permute-start | bytes 786440 | tf_op jit(solution)/shard_map/ppermute | solution.py:327
  78.6 10.3 %collective-permute-start.13 = (f32[512,128]{1,0:T(8,128)S(1)}, f32[512,128]{1,0:T(8,128)S(1)}, u32[]{:S(2)}, u32[]{:S(2)}) collective-permute-start(f32[512,128]{1,0:T(8,128)S(1)} %add.27), channel_id=1, source_target_pairs={{4,0},{6,2},{8,4},{10,6},{12,8},{14,10},{16,12},{18,14},{20,16},{2... | collective-permute-start | bytes 786440 | tf_op jit(solution)/shard_map/ppermute | solution.py:327
  83.3 11.2 %collective-permute-start.19 = (f32[512,128]{1,0:T(8,128)S(1)}, f32[512,128]{1,0:T(8,128)S(1)}, u32[]{:S(2)}, u32[]{:S(2)}) collective-permute-start(f32[512,128]{1,0:T(8,128)S(1)} %add.30), channel_id=1, source_target_pairs={{4,0},{6,2},{8,4},{10,6},{12,8},{14,10},{16,12},{18,14},{20,16},{2... | collective-permute-start | bytes 786440 | tf_op jit(solution)/shard_map/ppermute | solution.py:327
  88.9 10.8 %collective-permute-start.16 = (f32[512,128]{1,0:T(8,128)S(1)}, f32[512,128]{1,0:T(8,128)S(1)}, u32[]{:S(2)}, u32[]{:S(2)}) collective-permute-start(f32[512,128]{1,0:T(8,128)S(1)} %add.28), channel_id=1, source_target_pairs={{4,0},{6,2},{8,4},{10,6},{12,8},{14,10},{16,12},{18,14},{20,16},{2... | collective-permute-start | bytes 786440 | tf_op jit(solution)/shard_map/ppermute | solution.py:327
  94.6 10.8 %collective-permute-start.20 = (f32[512,128]{1,0:T(8,128)S(1)}, f32[512,128]{1,0:T(8,128)S(1)}, u32[]{:S(2)}, u32[]{:S(2)}) collective-permute-start(f32[512,128]{1,0:T(8,128)S(1)} %add.31), channel_id=1, source_target_pairs={{4,0},{6,2},{8,4},{10,6},{12,8},{14,10},{16,12},{18,14},{20,16},{2... | collective-permute-start | bytes 786440 | tf_op jit(solution)/shard_map/ppermute | solution.py:327
  105.4 33.8 %collective-permute-start.21 = (f32[512,128]{1,0:T(8,128)S(1)}, f32[512,128]{1,0:T(8,128)S(1)}, u32[]{:S(2)}, u32[]{:S(2)}) collective-permute-start(f32[512,128]{1,0:T(8,128)S(1)} %get-tuple-element.106), channel_id=1, source_target_pairs={{0,2},{2,0},{4,6},{6,4},{8,10},{10,8},{12,14},{14,12},{16,18},{18,... | collective-permute-start | bytes 786440 | tf_op jit(solution)/shard_map/ppermute | solution.py:327
  (2 other events, 2.1 us)

commit v6 on v5

--- a/solution.py
+++ b/solution.py
@@ -355,6 +355,7 @@
     pack = call(pack_kernel, sds(BODY + 8, width), [half_rows] * 2, block, moved=1 << 19)
     kv_sib = [kv_sib0, kv_sib1]
     rings = [[None, pack(send(own, 1), send(sib, 1, 1))] for own, sib in zip(kv_own, kv_sib)]
+    rings[0][1], qd_own = lax.optimization_barrier((rings[0][1], qd_own))
     rings[1][1], qd_sib, sib_all = lax.optimization_barrier((rings[1][1], qd_sib, sib_all))
     for _ in range(REACH - 2):
         for ring in rings:

time: 162 us -> 163 us (level)
  transfers between devices with their start and end apart: 22 -> 22, of which waited for: 9 -> 10; matrix products, arithmetic and copies ran while one was open for 0% -> 0% of each run, Pallas kernels for 9% -> 9%
where the time goes in v6:
time: 163 us; the launch traced here: 162 us
  starting transfers between devices  65.2 us (40%)
  blocking collectives  49.3 us (30%)
  waiting for transfers between devices  24.8 us (15%)
  Pallas kernels  17.2 us (11%)
  between operations  2.8 us (2%)
  local copies, waits for them, and re-layouts  2.09 us (1%)
    ppermute x22, starting transfers between devices, send(): return lax.ppermute(value, CTX, pairs)  65.2 us
    all_to_all x1, blocking collectives, shards(): lax.all_to_all(row.reshape(plane, 1, width), ('x', 'yh', 'core', 'yl'), 0...  30.2 us
    ppermute x22, waiting for transfers between devices, send(): return lax.ppermute(value, CTX, pairs)  24.8 us
    all_to_all x1, blocking collectives, shards(): parts = lax.all_to_all(parts, 'z', 0, 0)  19.1 us
    pallas_call x2, Pallas kernels, shards(): call(functools.partial(back_kernel, head, width), (sds(BODY, width),) * R...  5.07 us
    pallas_call x2, Pallas kernels, shards(): call(functools.partial(near_kernel, head, width), (sds(REACH * CHIP, ROWS...  4.33 us
  transfers between devices with their start and end apart: 22, of which 10 were waited for; matrix products, arithmetic and copies ran while one was open for 0% of the time, Pallas kernels for 9%

profile of v6, /device:TPU:1, one launch (start us, length us, event | category | flops | bytes accessed | tf_op | source)
XLA Modules:
  0.0 162.3 jit_solution(2640415630439916076)
XLA Ops:
  2.6 4.9 %collective-permute-start.1 = (f32[264,128]{1,0:T(8,128)}, f32[264,128]{1,0:T(8,128)S(1)}, u32[]{:S(2)}, u32[]{:S(2)}) collective-permute-start(f32[264,128]{1,0:T(8,128)} %get-tuple-element.61), channel_id=1, source_target_pairs={{0,6},{2,4},{4,10},{6,8},{8,14},{10,12},{12,18},{14,16},{16,22},{1... | collective-permute-start | bytes 405512 | tf_op jit(solution)/shard_map/ppermute | solution.py:327
  7.6 3.5 %collective-permute-start = (f32[264,128]{1,0:T(8,128)}, f32[264,128]{1,0:T(8,128)S(1)}, u32[]{:S(2)}, u32[]{:S(2)}) collective-permute-start(f32[264,128]{1,0:T(8,128)} %get-tuple-element.60.own0), channel_id=1, source_target_pairs={{0,4},{2,6},{4,8},{6,10},{8,12},{10,14},{12,16},{14,18},{16,20},{1... | collective-permute-start | bytes 405512 | tf_op jit(solution)/shard_map/ppermute | solution.py:327
  11.1 3.5 %collective-permute-start.3 = (f32[264,128]{1,0:T(8,128)}, f32[264,128]{1,0:T(8,128)S(1)}, u32[]{:S(2)}, u32[]{:S(2)}) collective-permute-start(f32[264,128]{1,0:T(8,128)} %get-tuple-element.65), channel_id=1, source_target_pairs={{0,6},{2,4},{4,10},{6,8},{8,14},{10,12},{12,18},{14,16},{16,22},{1... | collective-permute-start | bytes 405512 | tf_op jit(solution)/shard_map/ppermute | solution.py:327
  14.7 4.8 %collective-permute-start.2 = (f32[264,128]{1,0:T(8,128)}, f32[264,128]{1,0:T(8,128)S(1)}, u32[]{:S(2)}, u32[]{:S(2)}) collective-permute-start(f32[264,128]{1,0:T(8,128)} %get-tuple-element.64.own1), channel_id=1, source_target_pairs={{0,4},{2,6},{4,8},{6,10},{8,12},{10,14},{12,16},{14,18},{16,20},{1... | collective-permute-start | bytes 405512 | tf_op jit(solution)/shard_map/ppermute | solution.py:327
  22.7 3.6 %collective-permute-start.5 = (f32[520,128]{1,0:T(8,128)S(1)}, f32[520,128]{1,0:T(8,128)S(1)}, u32[]{:S(2)}, u32[]{:S(2)}) collective-permute-start(f32[520,128]{1,0:T(8,128)S(1)} %shard_map.85.refs_1_), channel_id=1, source_target_pairs={{0,4},{2,6},{4,8},{6,10},{8,12},{10,14},{12,16},{14,18},{16,20},{1... | collective-permute-start | bytes 798728 | tf_op jit(solution)/shard_map/ppermute | solution.py:327
  26.3 2.9 %collective-permute-start.4 = (f32[2,4,128,128]{3,2,1,0:T(8,128)}, f32[2,4,128,128]{3,2,1,0:T(8,128)S(1)}, u32[]{:S(2)}, u32[]{:S(2)}) collective-permute-start(f32[2,4,128,128]{3,2,1,0:T(8,128)} %get-tuple-element.68), channel_id=1, source_target_pairs={{0,2},{2,0},{4,6},{6,4},{8,10},{10,8},{12,14},{14,12},{16,18},{18,... | collective-permute-start | bytes 1572872 | tf_op jit(solution)/shard_map/ppermute | solution.py:327
  29.2 3.5 %collective-permute-start.8 = (f32[520,128]{1,0:T(8,128)S(1)}, f32[520,128]{1,0:T(8,128)S(1)}, u32[]{:S(2)}, u32[]{:S(2)}) collective-permute-start(f32[520,128]{1,0:T(8,128)S(1)} %shard_map.87.refs_1_), channel_id=1, source_target_pairs={{0,4},{2,6},{4,8},{6,10},{8,12},{10,14},{12,16},{14,18},{16,20},{1... | collective-permute-start | bytes 798728 | tf_op jit(solution)/shard_map/ppermute | solution.py:327
  32.8 3.5 %collective-permute-start.6 = (f32[520,128]{1,0:T(8,128)S(1)}, f32[520,128]{1,0:T(8,128)S(1)}, u32[]{:S(2)}, u32[]{:S(2)}) collective-permute-start(f32[520,128]{1,0:T(8,128)S(1)} %collective-permute-done.5.refs_2_), channel_id=1, source_target_pairs={{0,4},{2,6},{4,8},{6,10},{8,12},{10,14},{12,16},{14,18},{16,20},{1... | collective-permute-start | bytes 798728 | tf_op jit(solution)/shard_map/ppermute | solution.py:327
  36.3 2.8 %collective-permute-start.10 = (f32[520,128]{1,0:T(8,128)}, f32[520,128]{1,0:T(8,128)S(1)}, u32[]{:S(2)}, u32[]{:S(2)}) collective-permute-start(f32[520,128]{1,0:T(8,128)} %get-tuple-element.71), channel_id=1, source_target_pairs={{0,2},{2,0},{4,6},{6,4},{8,10},{10,8},{12,14},{14,12},{16,18},{18,... | collective-permute-start | bytes 798728 | tf_op jit(solution)/shard_map/ppermute | solution.py:327
  39.1 4.4 %collective-permute-start.9 = (f32[520,128]{1,0:T(8,128)S(1)}, f32[520,128]{1,0:T(8,128)S(1)}, u32[]{:S(2)}, u32[]{:S(2)}) collective-permute-start(f32[520,128]{1,0:T(8,128)S(1)} %collective-permute-done.8.refs_2_), channel_id=1, source_target_pairs={{0,4},{2,6},{4,8},{6,10},{8,12},{10,14},{12,16},{14,18},{16,20},{1... | collective-permute-start | bytes 798728 | tf_op jit(solution)/shard_map/ppermute | solution.py:327
  44.2 4.1 %collective-permute-start.7 = (f32[520,128]{1,0:T(8,128)S(1)}, f32[520,128]{1,0:T(8,128)S(1)}, u32[]{:S(2)}, u32[]{:S(2)}) collective-permute-start(f32[520,128]{1,0:T(8,128)S(1)} %collective-permute-done.6.refs_3_), channel_id=1, source_target_pairs={{0,4},{2,6},{4,8},{6,10},{8,12},{10,14},{12,16},{14,18},{16,20},{1... | collective-permute-start | bytes 798728 | tf_op jit(solution)/shard_map/ppermute | solution.py:327
  48.4 2.2 %shard_map.89 = (f32[1024,512]{1,0:T(8,128)S(1)}, f32[1024,512]{1,0:T(8,128)S(1)}, f32[8,512]{1,0:T(8,128)S(1)}) custom-call(s32[1]{0:T(128)} %bitcast.chip_ref, s32[1]{0:T(128)} %bitcast.1.core_ref, f32[2,4,128,128]{3,2,1,0:T(8,128)S(1)} %get-tuple-element.63.own_ref, f32[2,4,128,128]{3,2,1,0:T(8,128)S(1)} %collective-permute-done.4.far_ref, ...), custom_call_target="tpu_custom_call" | custom-call | flops 805306368 | bytes 6291456 | tf_op jit(solution)/shard_map/pallas_call | solution.py:381
  50.6 4.2 %collective-permute-start.14 = (f32[520,128]{1,0:T(8,128)S(1)}, f32[520,128]{1,0:T(8,128)S(1)}, u32[]{:S(2)}, u32[]{:S(2)}) collective-permute-start(f32[520,128]{1,0:T(8,128)S(1)} %collective-permute-done.9.refs_3_), channel_id=1, source_target_pairs={{0,4},{2,6},{4,8},{6,10},{8,12},{10,14},{12,16},{14,18},{16,20},{1... | collective-permute-start | bytes 798728 | tf_op jit(solution)/shard_map/ppermute | solution.py:327
  63.4 2.5 %shard_map.91 = (f32[512,128]{1,0:T(8,128)S(1)}, f32[512,128]{1,0:T(8,128)S(1)}, f32[512,128]{1,0:T(8,128)S(1)}, f32[512,128]{1,0:T(8,128)S(1)}, f32[2,128,128]{...) custom-call(f32[2,4,128,128]{3,2,1,0:T(8,128)S(1)} %get-tuple-element.63.own_ref, ...), custom_call_target="tpu_custom_call" | custom-call | flops 1207959552 | bytes 7340032 | tf_op jit(solution)/shard_map/pallas_call | solution.py:404
  68.1 2.5 %shard_map.94 = (f32[512,128]{1,0:T(8,128)S(1)}, f32[512,128]{1,0:T(8,128)S(1)}, f32[512,128]{1,0:T(8,128)S(1)}, f32[512,128]{1,0:T(8,128)S(1)}, f32[2,128,128]{...) custom-call(f32[2,4,128,128]{3,2,1,0:T(8,128)S(1)} %get-tuple-element.63.own_ref, ...), custom_call_target="tpu_custom_call" | custom-call | flops 1207959552 | bytes 7340032 | tf_op jit(solution)/shard_map/pallas_call | solution.py:404
  73.7 4.6 %collective-permute-start.15 = (f32[4,128,128]{2,1,0:T(8,128)S(1)}, f32[4,128,128]{2,1,0:T(8,128)S(1)}, u32[]{:S(2)}, u32[]{:S(2)}) collective-permute-start(f32[4,128,128]{2,1,0:T(8,128)S(1)} %pad_maximum_fusion.1), channel_id=1, source_target_pairs={{0,2},{2,0},{4,6},{6,4},{8,10},{10,8},{12,14},{14,12},{16,18},{18,... | collective-permute-start | bytes 786440 | tf_op jit(solution)/shard_map/ppermute | solution.py:327
  79.6 3.6 %collective-permute-done.18 = f32[512,128]{1,0:T(8,128)S(1)} collective-permute-done((f32[512,128]{1,0:T(8,128)S(1)}, f32[512,128]{1,0:T(8,128)S(1)}, u32[]{:S(2)}, u32[]{:S(2)}) %collective-permute-start.18) | collective-permute-done | bytes 262176 | tf_op jit(solution)/shard_map/ppermute | solution.py:327
  85.6 3.3 %collective-permute-done.13 = f32[512,128]{1,0:T(8,128)S(1)} collective-permute-done((f32[512,128]{1,0:T(8,128)S(1)}, f32[512,128]{1,0:T(8,128)S(1)}, u32[]{:S(2)}, u32[]{:S(2)}) %collective-permute-start.13) | collective-permute-done | bytes 262176 | tf_op jit(solution)/shard_map/ppermute | solution.py:327
  90.2 4.6 %collective-permute-done.19 = f32[512,128]{1,0:T(8,128)S(1)} collective-permute-done((f32[512,128]{1,0:T(8,128)S(1)}, f32[512,128]{1,0:T(8,128)S(1)}, u32[]{:S(2)}, u32[]{:S(2)}) %collective-permute-start.19) | collective-permute-done | bytes 262176 | tf_op jit(solution)/shard_map/ppermute | solution.py:327
  96.1 3.6 %collective-permute-done.16.got0 = f32[512,128]{1,0:T(8,128)S(1)} collective-permute-done((f32[512,128]{1,0:T(8,128)S(1)}, f32[512,128]{1,0:T(8,128)S(1)}, u32[]{:S(2)}, u32[]{:S(2)}) %collective-permute-start.16) | collective-permute-done | bytes 262176 | tf_op jit(solution)/shard_map/ppermute | solution.py:327
  99.7 5.6 %collective-permute-done.20.got1 = f32[512,128]{1,0:T(8,128)S(1)} collective-permute-done((f32[512,128]{1,0:T(8,128)S(1)}, f32[512,128]{1,0:T(8,128)S(1)}, u32[]{:S(2)}, u32[]{:S(2)}) %collective-permute-start.20) | collective-permute-done | bytes 262176 | tf_op jit(solution)/shard_map/ppermute | solution.py:327
  105.4 4.3 %collective-permute-start.21 = (f32[512,128]{1,0:T(8,128)S(1)}, f32[512,128]{1,0:T(8,128)S(1)}, u32[]{:S(2)}, u32[]{:S(2)}) collective-permute-start(f32[512,128]{1,0:T(8,128)S(1)} %get-tuple-element.110), channel_id=1, source_target_pairs={{0,2},{2,0},{4,6},{6,4},{8,10},{10,8},{12,14},{14,12},{16,18},{18,... | collective-permute-start | bytes 786440 | tf_op jit(solution)/shard_map/ppermute | solution.py:327
  109.7 30.2 %all_to_all.10 = f32[32,1,128]{2,1,0:T(1,128)S(1)} all-to-all(f32[32,1,128]{2,1,0:T(1,128)S(1)} %bitcast.16), channel_id=1, replica_groups=mesh['x'=4,'yh'=2,'z'=16,'core'=2,'yl'=2] {'x','yh','core','yl'}, dimensions={0} | all-to-all | bytes 32768 | tf_op jit(solution)/shard_map/all_to_all | solution.py:440
  140.8 19.1 %all_to_all.11 = f32[16,1,128]{2,1,0:T(1,128)S(1)} all-to-all(f32[16,1,128]{2,1,0:T(1,128)S(1)} %broadcast_in_dim.2), channel_id=1, replica_groups=mesh['x'=4,'yh'=2,'z'=16,'core'=2,'yl'=2] {'z'}, dimensions={0} | all-to-all | bytes 16384 | tf_op jit(solution)/shard_map/all_to_all | solution.py:450
  (55 shorter events, 27.5 us)
Async XLA Ops:
  2.6 20.0 %collective-permute-start.1 = (f32[264,128]{1,0:T(8,128)}, f32[264,128]{1,0:T(8,128)S(1)}, u32[]{:S(2)}, u32[]{:S(2)}) collective-permute-start(f32[264,128]{1,0:T(8,128)} %get-tuple-element.61), channel_id=1, source_target_pairs={{0,6},{2,4},{4,10},{6,8},{8,14},{10,12},{12,18},{14,16},{16,22},{1... | collective-permute-start | bytes 405512 | tf_op jit(solution)/shard_map/ppermute | solution.py:327
  7.6 15.1 %collective-permute-start = (f32[264,128]{1,0:T(8,128)}, f32[264,128]{1,0:T(8,128)S(1)}, u32[]{:S(2)}, u32[]{:S(2)}) collective-permute-start(f32[264,128]{1,0:T(8,128)} %get-tuple-element.60.own0), channel_id=1, source_target_pairs={{0,4},{2,6},{4,8},{6,10},{8,12},{10,14},{12,16},{14,18},{16,20},{1... | collective-permute-start | bytes 405512 | tf_op jit(solution)/shard_map/ppermute | solution.py:327
  11.1 15.1 %collective-permute-start.3 = (f32[264,128]{1,0:T(8,128)}, f32[264,128]{1,0:T(8,128)S(1)}, u32[]{:S(2)}, u32[]{:S(2)}) collective-permute-start(f32[264,128]{1,0:T(8,128)} %get-tuple-element.65), channel_id=1, source_target_pairs={{0,6},{2,4},{4,10},{6,8},{8,14},{10,12},{12,18},{14,16},{16,22},{1... | collective-permute-start | bytes 405512 | tf_op jit(solution)/shard_map/ppermute | solution.py:327
  14.7 11.6 %collective-permute-start.2 = (f32[264,128]{1,0:T(8,128)}, f32[264,128]{1,0:T(8,128)S(1)}, u32[]{:S(2)}, u32[]{:S(2)}) collective-permute-start(f32[264,128]{1,0:T(8,128)} %get-tuple-element.64.own1), channel_id=1, source_target_pairs={{0,4},{2,6},{4,8},{6,10},{8,12},{10,14},{12,16},{14,18},{16,20},{1... | collective-permute-start | bytes 405512 | tf_op jit(solution)/shard_map/ppermute | solution.py:327
  21.5 26.8 %copy-start.2 = (f32[264,128]{1,0:T(8,128)S(1)}, f32[264,128]{1,0:T(8,128)}, u32[]{:S(2)}) copy-start(f32[264,128]{1,0:T(8,128)} %get-tuple-element.60.own0) | copy-start | bytes 405508
  21.5 26.8 %copy-start.3 = (f32[264,128]{1,0:T(8,128)S(1)}, f32[264,128]{1,0:T(8,128)}, u32[]{:S(2)}) copy-start(f32[264,128]{1,0:T(8,128)} %get-tuple-element.64.own1) | copy-start | bytes 405508
  22.7 10.1 %collective-permute-start.5 = (f32[520,128]{1,0:T(8,128)S(1)}, f32[520,128]{1,0:T(8,128)S(1)}, u32[]{:S(2)}, u32[]{:S(2)}) collective-permute-start(f32[520,128]{1,0:T(8,128)S(1)} %shard_map.85.refs_1_), channel_id=1, source_target_pairs={{0,4},{2,6},{4,8},{6,10},{8,12},{10,14},{12,16},{14,18},{16,20},{1... | collective-permute-start | bytes 798728 | tf_op jit(solution)/shard_map/ppermute | solution.py:327
  26.3 22.1 %collective-permute-start.4 = (f32[2,4,128,128]{3,2,1,0:T(8,128)}, f32[2,4,128,128]{3,2,1,0:T(8,128)S(1)}, u32[]{:S(2)}, u32[]{:S(2)}) collective-permute-start(f32[2,4,128,128]{3,2,1,0:T(8,128)} %get-tuple-element.68), channel_id=1, source_target_pairs={{0,2},{2,0},{4,6},{6,4},{8,10},{10,8},{12,14},{14,12},{16,18},{18,... | collective-permute-start | bytes 1572872 | tf_op jit(solution)/shard_map/ppermute | solution.py:327
  29.2 9.9 %collective-permute-start.8 = (f32[520,128]{1,0:T(8,128)S(1)}, f32[520,128]{1,0:T(8,128)S(1)}, u32[]{:S(2)}, u32[]{:S(2)}) collective-permute-start(f32[520,128]{1,0:T(8,128)S(1)} %shard_map.87.refs_1_), channel_id=1, source_target_pairs={{0,4},{2,6},{4,8},{6,10},{8,12},{10,14},{12,16},{14,18},{16,20},{1... | collective-permute-start | bytes 798728 | tf_op jit(solution)/shard_map/ppermute | solution.py:327
  32.8 11.5 %collective-permute-start.6 = (f32[520,128]{1,0:T(8,128)S(1)}, f32[520,128]{1,0:T(8,128)S(1)}, u32[]{:S(2)}, u32[]{:S(2)}) collective-permute-start(f32[520,128]{1,0:T(8,128)S(1)} %collective-permute-done.5.refs_2_), channel_id=1, source_target_pairs={{0,4},{2,6},{4,8},{6,10},{8,12},{10,14},{12,16},{14,18},{16,20},{1... | collective-permute-start | bytes 798728 | tf_op jit(solution)/shard_map/ppermute | solution.py:327
  36.3 12.0 %collective-permute-start.10 = (f32[520,128]{1,0:T(8,128)}, f32[520,128]{1,0:T(8,128)S(1)}, u32[]{:S(2)}, u32[]{:S(2)}) collective-permute-start(f32[520,128]{1,0:T(8,128)} %get-tuple-element.71), channel_id=1, source_target_pairs={{0,2},{2,0},{4,6},{6,4},{8,10},{10,8},{12,14},{14,12},{16,18},{18,... | collective-permute-start | bytes 798728 | tf_op jit(solution)/shard_map/ppermute | solution.py:327
  39.1 11.5 %collective-permute-start.9 = (f32[520,128]{1,0:T(8,128)S(1)}, f32[520,128]{1,0:T(8,128)S(1)}, u32[]{:S(2)}, u32[]{:S(2)}) collective-permute-start(f32[520,128]{1,0:T(8,128)S(1)} %collective-permute-done.8.refs_2_), channel_id=1, source_target_pairs={{0,4},{2,6},{4,8},{6,10},{8,12},{10,14},{12,16},{14,18},{16,20},{1... | collective-permute-start | bytes 798728 | tf_op jit(solution)/shard_map/ppermute | solution.py:327
  44.2 11.4 %collective-permute-start.7 = (f32[520,128]{1,0:T(8,128)S(1)}, f32[520,128]{1,0:T(8,128)S(1)}, u32[]{:S(2)}, u32[]{:S(2)}) collective-permute-start(f32[520,128]{1,0:T(8,128)S(1)} %collective-permute-done.6.refs_3_), channel_id=1, source_target_pairs={{0,4},{2,6},{4,8},{6,10},{8,12},{10,14},{12,16},{14,18},{16,20},{1... | collective-permute-start | bytes 798728 | tf_op jit(solution)/shard_map/ppermute | solution.py:327
  50.6 10.1 %collective-permute-start.14 = (f32[520,128]{1,0:T(8,128)S(1)}, f32[520,128]{1,0:T(8,128)S(1)}, u32[]{:S(2)}, u32[]{:S(2)}) collective-permute-start(f32[520,128]{1,0:T(8,128)S(1)} %collective-permute-done.9.refs_3_), channel_id=1, source_target_pairs={{0,4},{2,6},{4,8},{6,10},{8,12},{10,14},{12,16},{14,18},{16,20},{1... | collective-permute-start | bytes 798728 | tf_op jit(solution)/shard_map/ppermute | solution.py:327
  57.0 9.5 %collective-permute-start.11 = (f32[512,128]{1,0:T(8,128)S(1)}, f32[512,128]{1,0:T(8,128)S(1)}, u32[]{:S(2)}, u32[]{:S(2)}) collective-permute-start(f32[512,128]{1,0:T(8,128)S(1)} %get-tuple-element.77), channel_id=1, source_target_pairs={{4,0},{6,2},{8,4},{10,6},{12,8},{14,10},{16,12},{18,14},{20,16},{2... | collective-permute-start | bytes 786440 | tf_op jit(solution)/shard_map/ppermute | solution.py:327
  62.1 10.2 %collective-permute-start.17 = (f32[512,128]{1,0:T(8,128)S(1)}, f32[512,128]{1,0:T(8,128)S(1)}, u32[]{:S(2)}, u32[]{:S(2)}) collective-permute-start(f32[512,128]{1,0:T(8,128)S(1)} %get-tuple-element.100), channel_id=1, source_target_pairs={{4,0},{6,2},{8,4},{10,6},{12,8},{14,10},{16,12},{18,14},{20,16},{2... | collective-permute-start | bytes 786440 | tf_op jit(solution)/shard_map/ppermute | solution.py:327
  66.6 11.7 %collective-permute-start.12 = (f32[512,128]{1,0:T(8,128)S(1)}, f32[512,128]{1,0:T(8,128)S(1)}, u32[]{:S(2)}, u32[]{:S(2)}) collective-permute-start(f32[512,128]{1,0:T(8,128)S(1)} %add.26), channel_id=1, source_target_pairs={{4,0},{6,2},{8,4},{10,6},{12,8},{14,10},{16,12},{18,14},{20,16},{2... | collective-permute-start | bytes 786440 | tf_op jit(solution)/shard_map/ppermute | solution.py:327
  72.4 10.9 %collective-permute-start.18 = (f32[512,128]{1,0:T(8,128)S(1)}, f32[512,128]{1,0:T(8,128)S(1)}, u32[]{:S(2)}, u32[]{:S(2)}) collective-permute-start(f32[512,128]{1,0:T(8,128)S(1)} %add.29), channel_id=1, source_target_pairs={{4,0},{6,2},{8,4},{10,6},{12,8},{14,10},{16,12},{18,14},{20,16},{2... | collective-permute-start | bytes 786440 | tf_op jit(solution)/shard_map/ppermute | solution.py:327
  73.7 10.9 %collective-permute-start.15 = (f32[4,128,128]{2,1,0:T(8,128)S(1)}, f32[4,128,128]{2,1,0:T(8,128)S(1)}, u32[]{:S(2)}, u32[]{:S(2)}) collective-permute-start(f32[4,128,128]{2,1,0:T(8,128)S(1)} %pad_maximum_fusion.1), channel_id=1, source_target_pairs={{0,2},{2,0},{4,6},{6,4},{8,10},{10,8},{12,14},{14,12},{16,18},{18,... | collective-permute-start | bytes 786440 | tf_op jit(solution)/shard_map/ppermute | solution.py:327
  78.3 10.6 %collective-permute-start.13 = (f32[512,128]{1,0:T(8,128)S(1)}, f32[512,128]{1,0:T(8,128)S(1)}, u32[]{:S(2)}, u32[]{:S(2)}) collective-permute-start(f32[512,128]{1,0:T(8,128)S(1)} %add.27), channel_id=1, source_target_pairs={{4,0},{6,2},{8,4},{10,6},{12,8},{14,10},{16,12},{18,14},{20,16},{2... | collective-permute-start | bytes 786440 | tf_op jit(solution)/shard_map/ppermute | solution.py:327
  83.3 11.5 %collective-permute-start.19 = (f32[512,128]{1,0:T(8,128)S(1)}, f32[512,128]{1,0:T(8,128)S(1)}, u32[]{:S(2)}, u32[]{:S(2)}) collective-permute-start(f32[512,128]{1,0:T(8,128)S(1)} %add.30), channel_id=1, source_target_pairs={{4,0},{6,2},{8,4},{10,6},{12,8},{14,10},{16,12},{18,14},{20,16},{2... | collective-permute-start | bytes 786440 | tf_op jit(solution)/shard_map/ppermute | solution.py:327
  88.9 10.8 %collective-permute-start.16 = (f32[512,128]{1,0:T(8,128)S(1)}, f32[512,128]{1,0:T(8,128)S(1)}, u32[]{:S(2)}, u32[]{:S(2)}) collective-permute-start(f32[512,128]{1,0:T(8,128)S(1)} %add.28), channel_id=1, source_target_pairs={{4,0},{6,2},{8,4},{10,6},{12,8},{14,10},{16,12},{18,14},{20,16},{2... | collective-permute-start | bytes 786440 | tf_op jit(solution)/shard_map/ppermute | solution.py:327
  94.8 10.5 %collective-permute-start.20 = (f32[512,128]{1,0:T(8,128)S(1)}, f32[512,128]{1,0:T(8,128)S(1)}, u32[]{:S(2)}, u32[]{:S(2)}) collective-permute-start(f32[512,128]{1,0:T(8,128)S(1)} %add.31), channel_id=1, source_target_pairs={{4,0},{6,2},{8,4},{10,6},{12,8},{14,10},{16,12},{18,14},{20,16},{2... | collective-permute-start | bytes 786440 | tf_op jit(solution)/shard_map/ppermute | solution.py:327
  105.4 34.6 %collective-permute-start.21 = (f32[512,128]{1,0:T(8,128)S(1)}, f32[512,128]{1,0:T(8,128)S(1)}, u32[]{:S(2)}, u32[]{:S(2)}) collective-permute-start(f32[512,128]{1,0:T(8,128)S(1)} %get-tuple-element.110), channel_id=1, source_target_pairs={{0,2},{2,0},{4,6},{6,4},{8,10},{10,8},{12,14},{14,12},{16,18},{18,... | collective-permute-start | bytes 786440 | tf_op jit(solution)/shard_map/ppermute | solution.py:327
  (2 other events, 2.1 us)
